TPU v7x, 32 devices: a whole 2x2x4 slice. The times are simulated.
32 devices in a mesh: groups: 2 (over y), seq: 4 (over z), head: 4 (over x, core).
Axes of the slice: x: 2, y: 2, z: 4, core: 2. Of those that a mesh axis runs over, the one named last changes fastest.
Arguments:
- q_feat: bfloat16 [8192, 256], P(('groups', 'seq'), 'head'), parts along dimension 0, may hold values from -4 to 4
- k_feat: bfloat16 [8192, 256], P(('groups', 'seq'), 'head'), parts along dimension 0, may hold values from -4 to 4
- swa_query: bfloat16 [8192, 2048], P(('groups', 'seq'), 'head'), parts along dimension 0, may hold values from -4.25 to 4.25
- swa_key: bfloat16 [8192, 2048], P(('groups', 'seq'), 'head'), parts along dimension 0, may hold values from -4.25 to 4.25
- values: bfloat16 [8192, 2048], P(('groups', 'seq'), 'head'), parts along dimension 0, may hold values from -6 to 6
- gain: float32 [2048], P('head'), may hold values from 0.5 to 1.5
Outputs:
- mixed_out: bfloat16 [8192, 2048], P(('groups', 'seq'), 'head'), parts along dimension 0
There are 2 independent parts, one for each index of `groups`. A program takes and returns all parts, laid end to end along the dimension named above; an argument that names none is the same for every part. Nothing has to cross between parts.
All inputs are finite; a program needn't handle non-finite values.
Results may differ from a plain program's by a relative error of at most 0.0044.
Values may be sent and summed in bfloat16 or wider, within the bound.
No kernel may reach another device: no remote copies, remote signals or barrier semaphores. Data moves between devices by JAX's collectives and lax.ppermute only.
A program may use at most 128 MiB of HBM per device.

v0:
```python
import jax
import jax.numpy as jnp
from jax import lax
from jax.sharding import PartitionSpec as P

HEAD_DIM = 128
WINDOW = 512


def shifted_2(value, axis, steps):
    count = lax.axis_size(axis)
    initial, last = (max(0, -steps), min(count, count - steps))
    return lax.ppermute(value, axis, [(source, source + steps) for source in range(initial, last)])


def shortened(x):
    return jax.tree.map(lambda a: a.astype(jnp.bfloat16) if a.dtype == jnp.float32 else a, x)


def features(vector):
    width = vector.shape[-1]
    outer_part = (vector[..., :, None] * vector[..., None, :]).reshape(
        vector.shape[:-1] + (width * width,)
    )
    constant = jnp.ones(vector.shape[:-1] + (1,), jnp.float32)
    return jnp.concatenate(
        [constant, vector * width ** (-0.25), outer_part * (0.5**0.5 * width ** (-0.5))], -1
    )


def add_pair(earlier, later):
    return (earlier[0] + later[0], earlier[1] + later[1])


def body(q_feat, k_feat, swa_query, swa_key, values, gain):
    highest = lax.Precision.HIGHEST
    tok_rows = swa_query.shape[0]
    head_count = swa_query.shape[1] // HEAD_DIM
    block_count = tok_rows // WINDOW
    feat_width = q_feat.shape[1] // head_count
    halo_key, halo_value = shifted_2(
        (swa_key[tok_rows - WINDOW :], values[tok_rows - WINDOW :]), "seq", 1
    )
    phi_key = features(
        k_feat.astype(jnp.float32).reshape(block_count, WINDOW, head_count, feat_width)
    ).astype(jnp.bfloat16)
    value_blocks = values.reshape(block_count, WINDOW, head_count, HEAD_DIM)
    block_states = jnp.einsum(
        "bjhn,bjhe->bhne", phi_key, value_blocks, preferred_element_type=jnp.float32
    )
    block_norms = jnp.sum(phi_key.astype(jnp.float32), 1)
    own_state = jnp.sum(block_states, 0)
    own_norm = jnp.sum(block_norms, 0)
    running = (own_state, own_norm)
    distance = 1
    while distance < lax.axis_size("seq"):
        shifted = shifted_2((shortened(running[0]), shortened(running[1])), "seq", distance)
        running = add_pair(running, shifted)
        distance = distance * 2
    prior_state = running[0] - own_state
    prior_norm = running[1] - own_norm
    start_pos = lax.axis_index("seq") * tok_rows
    wide_keys = jnp.concatenate([halo_key, swa_key], 0)
    wide_values = jnp.concatenate([halo_value, values], 0)
    row_idx = jnp.arange(WINDOW)[:, None]
    col_wide = jnp.arange(2 * WINDOW)[None, :]
    col_near = jnp.arange(WINDOW)[None, :]

    def one_block(block_idx):
        first_pos = start_pos + block_idx * WINDOW
        query3 = lax.dynamic_slice_in_dim(swa_query, block_idx * WINDOW, WINDOW, 0).reshape(
            WINDOW, head_count, HEAD_DIM
        )
        key_rows = lax.dynamic_slice_in_dim(wide_keys, block_idx * WINDOW, 2 * WINDOW, 0).reshape(
            2 * WINDOW, head_count, HEAD_DIM
        )
        val_rows = lax.dynamic_slice_in_dim(wide_values, block_idx * WINDOW, 2 * WINDOW, 0).reshape(
            2 * WINDOW, head_count, HEAD_DIM
        )
        scores = jnp.einsum(
            "ihe,jhe->hij", query3, key_rows, preferred_element_type=jnp.float32
        ) * HEAD_DIM ** (-0.5)
        offset = WINDOW + row_idx - col_wide
        allowed = (offset >= 0) & (offset < WINDOW) & (first_pos - WINDOW + col_wide >= 0)
        scores = jnp.where(allowed[None], scores, -1e30)
        top = jnp.max(scores, -1, keepdims=True)
        expo = jnp.exp(scores - top)
        weights = (expo / jnp.sum(expo, -1, keepdims=True)).astype(jnp.bfloat16)
        window_out = jnp.einsum(
            "hij,jhe->ihe", weights, val_rows, preferred_element_type=jnp.float32
        )
        qblock = lax.dynamic_slice_in_dim(q_feat, block_idx * WINDOW, WINDOW, 0).reshape(
            WINDOW, head_count, feat_width
        )
        kblock = lax.dynamic_slice_in_dim(k_feat, block_idx * WINDOW, WINDOW, 0).reshape(
            WINDOW, head_count, feat_width
        )
        vblock = lax.dynamic_slice_in_dim(values, block_idx * WINDOW, WINDOW, 0).reshape(
            WINDOW, head_count, HEAD_DIM
        )
        sim = jnp.einsum(
            "ihf,jhf->hij", qblock, kblock, preferred_element_type=jnp.float32
        ) * feat_width ** (-0.5)
        taylor = jnp.where((col_near <= row_idx)[None], 1.0 + sim + 0.5 * sim * sim, 0.0).astype(
            jnp.bfloat16
        )
        numer = jnp.einsum("hij,jhe->ihe", taylor, vblock, preferred_element_type=jnp.float32)
        denom = jnp.sum(taylor.astype(jnp.float32), -1).T
        return (numer, denom, window_out)

    numer, denom, window_out = lax.map(one_block, jnp.arange(block_count, dtype=jnp.int32))
    carried_state = prior_state[None] + (jnp.cumsum(block_states, 0) - block_states)
    carried_norm = prior_norm[None] + (jnp.cumsum(block_norms, 0) - block_norms)
    phi_query = (
        features(q_feat.astype(jnp.float32).reshape(block_count, WINDOW, head_count, feat_width))
        .astype(jnp.bfloat16)
        .astype(jnp.float32)
    )
    numer = numer + jnp.einsum("bihn,bhne->bihe", phi_query, carried_state, precision=highest)
    denom = denom + jnp.einsum("bihn,bhn->bih", phi_query, carried_norm, precision=highest)
    mixed = numer / denom[..., None] + window_out
    scale = lax.rsqrt(jnp.mean(mixed * mixed, -1, keepdims=True) + 1e-05)
    gain_rows = gain.reshape(head_count, HEAD_DIM)
    result = mixed * scale * gain_rows[None, None]
    return result.reshape(tok_rows, head_count * HEAD_DIM).astype(jnp.bfloat16)


def solution(mesh):
    placed = (
        P(("groups", "seq"), "head"),
        P(("groups", "seq"), "head"),
        P(("groups", "seq"), "head"),
        P(("groups", "seq"), "head"),
        P(("groups", "seq"), "head"),
        P("head"),
    )
    return jax.shard_map(
        body, mesh=mesh, in_specs=placed, out_specs=P(("groups", "seq"), "head"), check_vma=False
    )
```

profile of v0, /device:TPU:0, one launch (start us, length us, event | category | flops | bytes accessed | tf_op | source)
XLA Modules:
  0.0 111.5 jit_solution(14512180246416493788)
XLA Ops:
  0.0 1.5 %copy.19 = bf16[1024,512]{0,1:T(8,128)(2,1)S(1)} copy(bf16[1024,512]{1,0:T(8,128)(2,1)} %param.12) | data formatting | bytes 2097152
  2.4 5.7 %collective-permute-start = (bf16[512,512]{0,1:T(8,128)(2,1)}, bf16[512,512]{0,1:T(8,128)(2,1)}, u32[]{:S(2)}, u32[]{:S(2)}) collective-permute-start(bf16[512,512]{0,1:T(8,128)(2,1)} %slice.8), channel_id=1, source_target_pairs={{0,4},{4,8},{8,12},{1,5},{5,9},{9,13},{2,6},{6,10},{10,14},{3,7},{... | collective-permute-start | bytes 1572872 | tf_op jit(solution)/shard_map/ppermute | solution.py:13
  8.1 1.5 %copy.17 = bf16[1024,512]{0,1:T(8,128)(2,1)S(1)} copy(bf16[1024,512]{1,0:T(8,128)(2,1)} %param.11) | data formatting | bytes 2097152 | tf_op args[3]
  10.5 3.5 %collective-permute-start.1 = (bf16[512,512]{0,1:T(8,128)(2,1)}, bf16[512,512]{0,1:T(8,128)(2,1)}, u32[]{:S(2)}, u32[]{:S(2)}) collective-permute-start(bf16[512,512]{0,1:T(8,128)(2,1)} %slice.9), channel_id=1, source_target_pairs={{0,4},{4,8},{8,12},{1,5},{5,9},{9,13},{2,6},{6,10},{10,14},{3,7},{... | collective-permute-start | bytes 1572872 | tf_op jit(solution)/shard_map/ppermute | solution.py:13
  16.4 1.4 %convert_reduce_fusion.1 = (f32[2,4,273]{2,1,0:T(4,128)S(1)}, f32[4,273]{1,0:T(4,128)S(1)}) fusion(bf16[2,512,4,256]{1,3,2,0:T(8,128)(2,1)S(1)} %bitcast.98, bf16[2,512,4,16]{1,3,2,0:T(8,128)(2,1)S(1)} %get-tuple-element.327, bf16[273]{0:T(512)(128)(2,1)S(1)} %pad.3.clone), kind=kLoop, calls=%fused_computation.37 | loop fusion | flops 8942388 | bytes 2241874 | tf_op jit(solution)/shard_map/reduce_sum | solution.py:51
  17.8 2.7 %collective-permute-start.4 = (bf16[4,273]{1,0:T(4,128)(2,1)S(1)}, bf16[4,273]{1,0:T(4,128)(2,1)S(1)}, u32[]{:S(2)}, u32[]{:S(2)}) collective-permute-start(bf16[4,273]{1,0:T(4,128)(2,1)S(1)} %convert_element_type.61), channel_id=1, source_target_pairs={{0,4},{4,8},{8,12},{1,5},{5,9},{9,13},{2,6},{6,10},{10,14},{3,7},{... | collective-permute-start | bytes 6560 | tf_op jit(solution)/shard_map/ppermute | solution.py:13
  20.4 2.2 %reshape.193 = bf16[2,512,4,128]{3,2,1,0:T(4,128)(2,1)} reshape(bf16[1024,512]{1,0:T(8,128)(2,1)} %param.12) | data formatting | bytes 2097152 | tf_op jit(solution)/shard_map/reshape | solution.py:47
  22.6 3.9 %fusion.41 = (f32[4,273,128]{2,1,0:T(8,128)S(1)}, f32[2,4,273,128]{3,2,1,0:T(8,128)}) fusion(bf16[2,512,4,128]{3,2,1,0:T(4,128)(2,1)} %reshape.193, bf16[2,512,4,256]{1,3,2,0:T(8,128)(2,1)} %bitcast.99, bf16[2,512,4,16]{1,3,2,0:T(8,128)(2,1)S(1)} %get-tuple-element.327, bf16[273]{0:T(512)(128)(2,1)S(1)} %pad.3.clone), kind=kOutput, calls=%fused_computation.76 | convolution fusion | flops 293110272 | bytes 4954658 | tf_op jit(solution)/shard_map/bjhn,bjhe->bhne/dot_general | solution.py:48
  26.6 1.9 %collective-permute-start.2 = (bf16[4,273,128]{2,1,0:T(8,128)(2,1)S(1)}, bf16[4,273,128]{2,1,0:T(8,128)(2,1)S(1)}, u32[]{:S(2)}, u32[]{:S(2)}) collective-permute-start(bf16[4,273,128]{2,1,0:T(8,128)(2,1)S(1)} %convert_element_type.56), channel_id=1, source_target_pairs={{0,4},{4,8},{8,12},{1,5},{5,9},{9,13},{2,6},{6,10},{10,14},{3,7},{... | collective-permute-start | bytes 838664 | tf_op jit(solution)/shard_map/ppermute | solution.py:13
  28.9 2.0 %multiply_convert_fusion = bf16[2,512,4,16,16]{1,4,3,2,0:T(8,128)(2,1)} fusion(f32[2,512,4,16]{1,3,2,0:T(8,128)S(1)} %get-tuple-element.330), kind=kLoop, calls=%fused_computation.39 | loop fusion | flops 3145728 | bytes 2359296 | tf_op jit(solution)/shard_map/convert.5
  31.1 5.4 %collective-permute-start.5 = (bf16[4,273]{1,0:T(4,128)(2,1)S(1)}, bf16[4,273]{1,0:T(4,128)(2,1)S(1)}, u32[]{:S(2)}, u32[]{:S(2)}) collective-permute-start(bf16[4,273]{1,0:T(4,128)(2,1)S(1)} %fusion.36), channel_id=1, source_target_pairs={{0,8},{4,12},{1,9},{5,13},{2,10},{6,14},{3,11},{7,15},{16,24},{20,... | collective-permute-start | bytes 6560 | tf_op jit(solution)/shard_map/ppermute | solution.py:13
  37.9 3.7 %fusion.26 = f32[2,4,1,512]{3,2,1,0:T(1,128)} fusion(bf16[2,512,4,256]{1,3,2,0:T(8,128)(2,1)} %bitcast.100, bf16[2,512,4,16]{1,3,2,0:T(8,128)(2,1)S(1)} %get-tuple-element.329, bf16[273]{0:T(512)(128)(2,1)S(1)} %pad.3.clone, f32[2,4,273,1]{2,1,0,3:T(4,128)S(1)} %add_bitcast_fusion), kind=kOutput, calls=%fused_computation.51 | convolution fusion | flops 20127744 | bytes 2253890 | tf_op jit(solution)/shard_map/bihn,bhn->bih/dot_general | solution.py:120
  42.3 5.8 %collective-permute-start.3 = (bf16[4,273,128]{2,1,0:T(8,128)(2,1)}, bf16[4,273,128]{2,1,0:T(8,128)(2,1)}, u32[]{:S(2)}, u32[]{:S(2)}) collective-permute-start(bf16[4,273,128]{2,1,0:T(8,128)(2,1)} %fusion.34), channel_id=1, source_target_pairs={{0,8},{4,12},{1,9},{5,13},{2,10},{6,14},{3,11},{7,15},{16,24},{20,... | collective-permute-start | bytes 838664 | tf_op jit(solution)/shard_map/ppermute | solution.py:13
  50.5 51.6 %while.18 = (s32[]{:T(128)}, f32[2,512,4,128]{1,3,2,0:T(8,128)}, f32[2,512,4]{1,2,0:T(4,128)}, f32[2,512,4,128]{1,3,2,0:T(8,128)}, s32[2]{0:T(128)S(1)}, /*index...) while((s32[]{:T(128)}, f32[2,512,4,128]{1,3,2,0:T(8,128)}, ...), condition=%wide.region_4.5_spmd.clone.clone, body=%wide.region_0.4_spmd.clone.clone.sunk | while | flops 1400636928 | bytes 69253632 | solution.py:111
  53.1 1.5 %convert_reduce_fusion.4 = (f32[4,512]{1,0:T(4,128)S(1)}, bf16[4,512,512]{1,2,0:T(8,128)(2,1)S(1)}) fusion(bf16[512,4,16]{0,2,1:T(8,128)(2,1)S(1)} %bitcast.104, bf16[512,4,16]{0,2,1:T(8,128)(2,1)S(1)} %bitcast.103, pred[512,512]{0,1:T(8,128)(4,1)S(1)} %iota_compare_fusion.2), kind=kOutput, calls=%fused_computation.10.clone.1 | convolution fusion | flops 42989568 | bytes 2498560 | tf_op jit(solution)/shard_map/while/body/eval_jaxpr/ihf,jhf->hij/dot_general | solution.py:101
  57.1 1.7 %constant_dynamic-slice_fusion.12 = (bf16[1024,512]{0,1:T(8,128)(2,1)}, bf16[1024,512]{0,1:T(8,128)(2,1)}) fusion(bf16[1536,512]{0,1:T(8,128)(2,1)S(1)} %get-tuple-element.469, s32[]{:T(128)S(6)} %select_n.54, bf16[1536,512]{0,1:T(8,128)(2,1)S(1)} %get-tuple-element.466), kind=kLoop, calls=%fused_computation.28.clone.1 | loop fusion | bytes 4194308 | tf_op jit(solution)/shard_map/while/body/eval_jaxpr/dynamic_slice | solution.py:74
  58.8 1.4 %fusion.74 = pred[512,1024]{1,0:T(8,128)(4,1)} fusion(s32[512]{0:T(512)S(1)} %iota_add_fusion.3, pred[1024]{0:T(1024)(128)(4,1)S(1)} %fusion.73), kind=kLoop, calls=%fused_computation.18.clone.1 | loop fusion | flops 2621440 | bytes 527360 | tf_op jit(solution)/shard_map/while/body/eval_jaxpr/and | solution.py:84
  62.3 7.5 %fusion.75 = (f32[4,512]{1,0:T(4,128)S(1)}, f32[4,512,1024]{2,1,0:T(8,128)}) fusion(pred[512,1024]{1,0:T(8,128)(4,1)} %fusion.74, bf16[512,4,128]{0,2,1:T(8,128)(2,1)} %bitcast.97, bf16[1024,4,128]{0,2,1:T(8,128)(2,1)S(1)} %bitcast.96), kind=kOutput, calls=%fused_computation.75.clone.1 | convolution fusion | flops 545260544 | bytes 10493952 | tf_op jit(solution)/shard_map/while/body/eval_jaxpr/sub | solution.py:87
  69.9 6.5 %fusion.76 = f32[2,512,4,128]{1,3,2,0:T(8,128)} fusion(f32[2,512,4,128]{1,3,2,0:T(8,128)} %get-tuple-element.443, s32[]{:T(128)S(6)} %copy.58, bf16[1024,4,128]{0,2,1:T(8,128)(2,1)} %bitcast.95, f32[4,512,1024]{2,1,0:T(8,128)} %get-tuple-element.420, f32[4,512]{1,0:T(4,128)S(1)} %get-tuple-element.421), kind=kOutput, calls=%fused_computation.22.clone.1 | convolution fusion | flops 541065216 | bytes 10493956 | tf_op jit(solution)/shard_map/while/body/eval_jaxpr/hij,jhe->ihe/dot_general | solution.py:89
  79.0 1.5 %convert_reduce_fusion.4 = (f32[4,512]{1,0:T(4,128)S(1)}, bf16[4,512,512]{1,2,0:T(8,128)(2,1)S(1)}) fusion(bf16[512,4,16]{0,2,1:T(8,128)(2,1)S(1)} %bitcast.104, bf16[512,4,16]{0,2,1:T(8,128)(2,1)S(1)} %bitcast.103, pred[512,512]{0,1:T(8,128)(4,1)S(1)} %iota_compare_fusion.2), kind=kOutput, calls=%fused_computation.10.clone.1 | convolution fusion | flops 42989568 | bytes 2498560 | tf_op jit(solution)/shard_map/while/body/eval_jaxpr/ihf,jhf->hij/dot_general | solution.py:101
  83.0 1.7 %constant_dynamic-slice_fusion.12 = (bf16[1024,512]{0,1:T(8,128)(2,1)}, bf16[1024,512]{0,1:T(8,128)(2,1)}) fusion(bf16[1536,512]{0,1:T(8,128)(2,1)S(1)} %get-tuple-element.469, s32[]{:T(128)S(6)} %select_n.54, bf16[1536,512]{0,1:T(8,128)(2,1)S(1)} %get-tuple-element.466), kind=kLoop, calls=%fused_computation.28.clone.1 | loop fusion | bytes 4194308 | tf_op jit(solution)/shard_map/while/body/eval_jaxpr/dynamic_slice | solution.py:74
  88.2 7.6 %fusion.75 = (f32[4,512]{1,0:T(4,128)S(1)}, f32[4,512,1024]{2,1,0:T(8,128)}) fusion(pred[512,1024]{1,0:T(8,128)(4,1)} %fusion.74, bf16[512,4,128]{0,2,1:T(8,128)(2,1)} %bitcast.97, bf16[1024,4,128]{0,2,1:T(8,128)(2,1)S(1)} %bitcast.96), kind=kOutput, calls=%fused_computation.75.clone.1 | convolution fusion | flops 545260544 | bytes 10493952 | tf_op jit(solution)/shard_map/while/body/eval_jaxpr/sub | solution.py:87
  95.7 6.4 %fusion.76 = f32[2,512,4,128]{1,3,2,0:T(8,128)} fusion(f32[2,512,4,128]{1,3,2,0:T(8,128)} %get-tuple-element.443, s32[]{:T(128)S(6)} %copy.58, bf16[1024,4,128]{0,2,1:T(8,128)(2,1)} %bitcast.95, f32[4,512,1024]{2,1,0:T(8,128)} %get-tuple-element.420, f32[4,512]{1,0:T(4,128)S(1)} %get-tuple-element.421), kind=kOutput, calls=%fused_computation.22.clone.1 | convolution fusion | flops 541065216 | bytes 10493956 | tf_op jit(solution)/shard_map/while/body/eval_jaxpr/hij,jhe->ihe/dot_general | solution.py:89
  104.3 4.1 %fusion.27 = f32[2,4,128,512]{3,2,1,0:T(8,128)S(1)} fusion(bf16[2,512,4,256]{1,3,2,0:T(8,128)(2,1)} %bitcast.101, bf16[2,512,4,16]{1,3,2,0:T(8,128)(2,1)S(1)} %get-tuple-element.329, bf16[273]{0:T(512)(128)(2,1)S(1)} %pad.3.clone, f32[2,4,273,128]{3,2,1,0:T(8,128)S(1)} %copy-done.8, f32[4,273,128]{2,1,0:T(8,128)S(1)} %add_subtract_fusion), kind=kOutput, calls=%fused_computation.52 | convolution fusion | flops 1724556288 | bytes 6003234 | tf_op jit(solution)/shard_map/bihn,bhne->bihe/dot_general | solution.py:119
  (109 shorter events, 28.5 us)
Async XLA Ops:
  1.5 46.6 %copy-start.3 = (bf16[1024,512]{0,1:T(8,128)(2,1)}, bf16[1024,512]{0,1:T(8,128)(2,1)S(1)}, u32[]{:S(2)}) copy-start(bf16[1024,512]{0,1:T(8,128)(2,1)S(1)} %copy.19) | copy-start | bytes 3145732
  1.5 12.5 %copy-start.15 = (bf16[1024,64]{0,1:T(8,128)(2,1)S(1)}, bf16[1024,64]{0,1:T(8,128)(2,1)}, u32[]{:S(2)}) copy-start(bf16[1024,64]{0,1:T(8,128)(2,1)} %param.9) | copy-start | bytes 393220
  2.4 45.8 %collective-permute-start = (bf16[512,512]{0,1:T(8,128)(2,1)}, bf16[512,512]{0,1:T(8,128)(2,1)}, u32[]{:S(2)}, u32[]{:S(2)}) collective-permute-start(bf16[512,512]{0,1:T(8,128)(2,1)} %slice.8), channel_id=1, source_target_pairs={{0,4},{4,8},{8,12},{1,5},{5,9},{9,13},{2,6},{6,10},{10,14},{3,7},{... | collective-permute-start | bytes 1572872 | tf_op jit(solution)/shard_map/ppermute | solution.py:13
  9.6 5.4 %copy-start.5 = (bf16[1024,512]{0,1:T(8,128)(2,1)}, bf16[1024,512]{0,1:T(8,128)(2,1)S(1)}, u32[]{:S(2)}) copy-start(bf16[1024,512]{0,1:T(8,128)(2,1)S(1)} %copy.17) | copy-start | bytes 3145732
  10.5 38.8 %collective-permute-start.1 = (bf16[512,512]{0,1:T(8,128)(2,1)}, bf16[512,512]{0,1:T(8,128)(2,1)}, u32[]{:S(2)}, u32[]{:S(2)}) collective-permute-start(bf16[512,512]{0,1:T(8,128)(2,1)} %slice.9), channel_id=1, source_target_pairs={{0,4},{4,8},{8,12},{1,5},{5,9},{9,13},{2,6},{6,10},{10,14},{3,7},{... | collective-permute-start | bytes 1572872 | tf_op jit(solution)/shard_map/ppermute | solution.py:13
  17.8 13.4 %collective-permute-start.4 = (bf16[4,273]{1,0:T(4,128)(2,1)S(1)}, bf16[4,273]{1,0:T(4,128)(2,1)S(1)}, u32[]{:S(2)}, u32[]{:S(2)}) collective-permute-start(bf16[4,273]{1,0:T(4,128)(2,1)S(1)} %convert_element_type.61), channel_id=1, source_target_pairs={{0,4},{4,8},{8,12},{1,5},{5,9},{9,13},{2,6},{6,10},{10,14},{3,7},{... | collective-permute-start | bytes 6560 | tf_op jit(solution)/shard_map/ppermute | solution.py:13
  22.6 5.9 %copy-start.14 = (bf16[1024,64]{0,1:T(8,128)(2,1)S(1)}, bf16[1024,64]{0,1:T(8,128)(2,1)}, u32[]{:S(2)}) copy-start(bf16[1024,64]{0,1:T(8,128)(2,1)} %param.8) | copy-start | bytes 393220
  26.5 15.0 %copy-start.7 = (f32[4,273,128]{2,1,0:T(8,128)}, f32[4,273,128]{2,1,0:T(8,128)S(1)}, u32[]{:S(2)}) copy-start(f32[4,273,128]{2,1,0:T(8,128)S(1)} %get-tuple-element.331) | copy-start | bytes 1677316
  26.6 15.0 %collective-permute-start.2 = (bf16[4,273,128]{2,1,0:T(8,128)(2,1)S(1)}, bf16[4,273,128]{2,1,0:T(8,128)(2,1)S(1)}, u32[]{:S(2)}, u32[]{:S(2)}) collective-permute-start(bf16[4,273,128]{2,1,0:T(8,128)(2,1)S(1)} %convert_element_type.56), channel_id=1, source_target_pairs={{0,4},{4,8},{8,12},{1,5},{5,9},{9,13},{2,6},{6,10},{10,14},{3,7},{... | collective-permute-start | bytes 838664 | tf_op jit(solution)/shard_map/ppermute | solution.py:13
  28.8 7.7 %copy-start.9 = (f32[2,4,273,128]{3,2,1,0:T(8,128)S(1)}, f32[2,4,273,128]{3,2,1,0:T(8,128)}, u32[]{:S(2)}) copy-start(f32[2,4,273,128]{3,2,1,0:T(8,128)} %get-tuple-element.332) | copy-start | bytes 3354628
  31.1 6.7 %collective-permute-start.5 = (bf16[4,273]{1,0:T(4,128)(2,1)S(1)}, bf16[4,273]{1,0:T(4,128)(2,1)S(1)}, u32[]{:S(2)}, u32[]{:S(2)}) collective-permute-start(bf16[4,273]{1,0:T(4,128)(2,1)S(1)} %fusion.36), channel_id=1, source_target_pairs={{0,8},{4,12},{1,9},{5,13},{2,10},{6,14},{3,11},{7,15},{16,24},{20,... | collective-permute-start | bytes 6560 | tf_op jit(solution)/shard_map/ppermute | solution.py:13
  41.6 7.7 %copy-start.6 = (bf16[1024,512]{0,1:T(8,128)(2,1)S(1)}, bf16[1024,512]{0,1:T(8,128)(2,1)}, u32[]{:S(2)}) copy-start(bf16[1024,512]{0,1:T(8,128)(2,1)} %copy-done.5) | copy-start | bytes 3145732
  41.6 7.7 %copy-start.16 = (bf16[4,273,128]{2,1,0:T(8,128)(2,1)}, bf16[4,273,128]{2,1,0:T(8,128)(2,1)S(1)}, u32[]{:S(2)}) copy-start(bf16[4,273,128]{2,1,0:T(8,128)(2,1)S(1)} %collective-permute-done.2) | copy-start | bytes 838660
  42.3 60.6 %collective-permute-start.3 = (bf16[4,273,128]{2,1,0:T(8,128)(2,1)}, bf16[4,273,128]{2,1,0:T(8,128)(2,1)}, u32[]{:S(2)}, u32[]{:S(2)}) collective-permute-start(bf16[4,273,128]{2,1,0:T(8,128)(2,1)} %fusion.34), channel_id=1, source_target_pairs={{0,8},{4,12},{1,9},{5,13},{2,10},{6,14},{3,11},{7,15},{16,24},{20,... | collective-permute-start | bytes 838664 | tf_op jit(solution)/shard_map/ppermute | solution.py:13
  50.5 6.6 %copy-start = (bf16[1536,512]{0,1:T(8,128)(2,1)}, bf16[1536,512]{0,1:T(8,128)(2,1)S(1)}, u32[]{:S(2)}) copy-start(bf16[1536,512]{0,1:T(8,128)(2,1)S(1)} %get-tuple-element.469) | copy-start | bytes 4718596 | tf_op jit(solution)/shard_map/while
  54.7 1.8 %copy-start.17 = (f32[2,512,4]{1,2,0:T(4,128)S(1)}, f32[2,512,4]{1,2,0:T(4,128)}, u32[]{:S(2)}) copy-start(f32[2,512,4]{1,2,0:T(4,128)} %get-tuple-element.442) | copy-start | bytes 49156 | tf_op jit(solution)/shard_map/while
  58.8 3.5 %copy-start.2 = (bf16[1024,512]{0,1:T(8,128)(2,1)S(1)}, bf16[1024,512]{0,1:T(8,128)(2,1)}, u32[]{:S(2)}) copy-start(bf16[1024,512]{0,1:T(8,128)(2,1)} %get-tuple-element.419) | copy-start | bytes 3145732 | tf_op jit(solution)/shard_map/while
  69.9 6.5 %copy-start.1 = (bf16[1536,512]{0,1:T(8,128)(2,1)S(1)}, bf16[1536,512]{0,1:T(8,128)(2,1)}, u32[]{:S(2)}) copy-start(bf16[1536,512]{0,1:T(8,128)(2,1)} %copy-done) | copy-start | bytes 4718596 | tf_op jit(solution)/shard_map/while
  76.3 6.6 %copy-start = (bf16[1536,512]{0,1:T(8,128)(2,1)}, bf16[1536,512]{0,1:T(8,128)(2,1)S(1)}, u32[]{:S(2)}) copy-start(bf16[1536,512]{0,1:T(8,128)(2,1)S(1)} %get-tuple-element.469) | copy-start | bytes 4718596 | tf_op jit(solution)/shard_map/while
  84.6 3.5 %copy-start.2 = (bf16[1024,512]{0,1:T(8,128)(2,1)S(1)}, bf16[1024,512]{0,1:T(8,128)(2,1)}, u32[]{:S(2)}) copy-start(bf16[1024,512]{0,1:T(8,128)(2,1)} %get-tuple-element.419) | copy-start | bytes 3145732 | tf_op jit(solution)/shard_map/while
  95.7 6.4 %copy-start.1 = (bf16[1536,512]{0,1:T(8,128)(2,1)S(1)}, bf16[1536,512]{0,1:T(8,128)(2,1)}, u32[]{:S(2)}) copy-start(bf16[1536,512]{0,1:T(8,128)(2,1)} %copy-done) | copy-start | bytes 4718596 | tf_op jit(solution)/shard_map/while
  102.1 2.2 %copy-start.8 = (f32[2,4,273,128]{3,2,1,0:T(8,128)S(1)}, f32[2,4,273,128]{3,2,1,0:T(8,128)}, u32[]{:S(2)}) copy-start(f32[2,4,273,128]{3,2,1,0:T(8,128)} %reduce-window_subtract_fusion) | copy-start | bytes 3354628
  104.3 4.2 %copy-start.12 = (f32[2,512,4,128]{1,3,2,0:T(8,128)S(1)}, f32[2,512,4,128]{1,3,2,0:T(8,128)}, u32[]{:S(2)}) copy-start(f32[2,512,4,128]{1,3,2,0:T(8,128)} %get-tuple-element.199) | copy-start | bytes 6291460
  104.3 4.2 %copy-start.13 = (f32[2,512,4,128]{1,3,2,0:T(8,128)S(1)}, f32[2,512,4,128]{1,3,2,0:T(8,128)}, u32[]{:S(2)}) copy-start(f32[2,512,4,128]{1,3,2,0:T(8,128)} %get-tuple-element.201) | copy-start | bytes 6291460
  (9 other events, 11.1 us)
where the time goes:
time: 112 us
  matrix products  43.7 us (39%)
  local copies, waits for them, and re-layouts  25.9 us (23%)
  starting transfers between devices  25 us (22%)
  other arithmetic  14.7 us (13%)
  loops' own time  1.56 us (1%)
    ppermute x6, starting transfers between devices, shifted_2(): lax.ppermute(value, axis, [(source, source + steps) for source in range(i...  25 us
    sub x2, matrix products, one_block(): expo = jnp.exp(scores - top)  15.1 us
    dot_general x2, matrix products, one_block(): jnp.einsum('hij,jhe->ihe', weights, val_rows, preferred_element_type=jnp....  12.9 us
    unnamed x29, local copies, waits for them, and re-layouts  5.49 us
    dynamic_slice x4, local copies, waits for them, and re-layouts, one_block(): lax.dynamic_slice_in_dim(swa_query, block_idx * WINDOW, WINDOW, 0)  4.17 us
    dot_general x1, matrix products, body(): jnp.einsum('bihn,bhne->bihe', phi_query, carried_state, precision=highest)  4.15 us
    while x28, local copies, waits for them, and re-layouts  3.99 us
    dot_general x1, matrix products, body(): jnp.einsum('bjhn,bjhe->bhne', phi_key, value_blocks, preferred_element_ty...  3.92 us
  transfers between devices with their start and end apart: 6, of which 2 were waited for; matrix products, arithmetic and copies ran while one was open for 61% of the time, Pallas kernels for 0%

commit v1 on v0

v1 whole, which is shorter than its diff:
```python
import functools

import jax
import jax.numpy as jnp
from jax import lax
from jax.experimental import pallas as pl
from jax.experimental.pallas import tpu as pltpu
from jax.sharding import PartitionSpec as P

HEAD_DIM = 128
WINDOW = 512
TILE = 256
NEG = -1e30
LOG2E = 1.4426950408889634
BF = jnp.bfloat16
F32 = jnp.float32


def feature_rows(width):
    return -(-(width * (width + 1) // 2 + width + 1) // 16) * 16


def state_rows(heads, width):
    return heads * feature_rows(width) + 16


def nt(a, b):
    return lax.dot_general(a, b, (((1,), (1,)), ((), ())), preferred_element_type=F32)


def nn(a, b):
    return jnp.dot(a, b, preferred_element_type=F32)


def phi_rows(x, query):
    width, tokens = x.shape
    half = width // 2
    scale = 0.5**0.5 * width ** (-0.5)
    twice = jnp.concatenate([x, x], 0)
    rows = []
    for d in range(half):
        prod = ((x * twice[d : d + width]) * scale).astype(BF)
        if query and d:
            prod = prod * 2
        rows.append(prod)
    rows.append((x * width ** (-0.25)).astype(BF))
    cross = (x[:half] * x[half:]) * scale
    if query:
        cross = cross * 2
    pad = feature_rows(width) - (half * width + width + half)
    last = lax.broadcasted_iota(jnp.int32, (pad, tokens), 0)
    const = jnp.where(last == 0, 1.0, 0.0)
    rows.append(jnp.concatenate([cross, const], 0).astype(BF))
    return jnp.concatenate(rows, 0)


def with_ones(v):
    return jnp.concatenate([v, jnp.ones_like(v)], 1)


def state_kernel(kf_ref, v_ref, first_ref, own_ref, *, heads, width, blocks):
    feats = feature_rows(width)
    base = heads * feats
    kft = kf_ref[...].astype(F32).T
    ones = jnp.ones((16, WINDOW), BF)
    first_ref[base:, :] = jnp.zeros((16, HEAD_DIM), F32)
    own_ref[base:, :] = jnp.zeros((16, HEAD_DIM), BF)
    for h in range(heads):
        phi = phi_rows(kft[h * width : (h + 1) * width], False)
        total, norm = None, None
        for b in range(blocks):
            part = phi[:, b * WINDOW : (b + 1) * WINDOW]
            s = nn(part, v_ref[b * WINDOW : (b + 1) * WINDOW, h * HEAD_DIM : (h + 1) * HEAD_DIM])
            n = nt(ones, part)
            total = s if b == 0 else total + s
            norm = n if b == 0 else norm + n
            if b == 0:
                first_ref[h * feats : (h + 1) * feats, :] = s
                first_ref[base + 2 * h : base + 2 * h + 1, :] = n[:1, :HEAD_DIM]
                first_ref[base + 2 * h + 1 : base + 2 * h + 2, : feats - HEAD_DIM] = n[:1, HEAD_DIM:]
        own_ref[h * feats : (h + 1) * feats, :] = total.astype(BF)
        own_ref[base + 2 * h : base + 2 * h + 1, :] = norm[:1, :HEAD_DIM].astype(BF)
        own_ref[base + 2 * h + 1 : base + 2 * h + 2, : feats - HEAD_DIM] = norm[:1, HEAD_DIM:].astype(BF)


def softmax_part(q, tiles):
    scale = HEAD_DIM ** (-0.5) * LOG2E
    scores = []
    for key, _, mask in tiles:
        s = nt(q, key)
        scores.append(s if mask is None else jnp.where(mask, s, NEG))
    top = functools.reduce(jnp.maximum, scores)
    top = jnp.max(top, 1, keepdims=True)
    acc = None
    for s, (_, value, _) in zip(scores, tiles):
        p = jnp.exp2((s - top) * scale).astype(BF)
        part = nn(p, with_ones(value))
        acc = part if acc is None else acc + part
    return top, acc[:, :HEAD_DIM], acc[:, HEAD_DIM:]


def local_kernel(q_ref, k_ref, v_ref, qf_ref, kf_ref, num_ref, den_ref, win_ref, sum_ref, top_ref, phi_ref, *, width, blocks):
    h = pl.program_id(0)
    row = lax.broadcasted_iota(jnp.int32, (TILE, TILE), 0)
    col = lax.broadcasted_iota(jnp.int32, (TILE, TILE), 1)
    causal = col <= row
    beyond = col > row
    lane = lax.broadcasted_iota(jnp.int32, (TILE, qf_ref.shape[1]), 1)
    mine = (lane >= h * width) & (lane < (h + 1) * width)
    tokens = q_ref.shape[0]
    for start in range(0, tokens, TILE):
        at = slice(start, start + TILE)
        q = q_ref[at, :]
        tiles = []
        for back, mask in ((WINDOW, beyond), (WINDOW - TILE, None), (0, causal)):
            key_at = start - back
            if key_at >= 0:
                ks = slice(key_at, key_at + TILE)
                tiles.append((k_ref[ks, :], v_ref[ks, :], mask))
        top, out, total = softmax_part(q, tiles)
        if start >= WINDOW:
            win_ref[at, :] = out / total
        else:
            win_ref[at, :] = out
            sum_ref[at, :] = total
            top_ref[at, :] = jnp.broadcast_to(top, (TILE, HEAD_DIM))
        qf = jnp.where(mine, qf_ref[at, :], jnp.zeros((), BF))
        acc = None
        for key_at in range(start - start % WINDOW, start + TILE, TILE):
            ks = slice(key_at, key_at + TILE)
            r = nt(qf, kf_ref[ks, :])
            t = (r * (0.5 / width) + width ** (-0.5)) * r + 1.0
            if key_at == start:
                t = jnp.where(causal, t, 0.0)
            part = nn(t.astype(BF), with_ones(v_ref[ks, :]))
            acc = part if acc is None else acc + part
        num_ref[at, :] = acc[:, :HEAD_DIM]
        den_ref[at, :] = acc[:, HEAD_DIM:]
    @pl.when(h == 0)
    def _():
        qft = qf_ref[...].astype(F32).T
        for g in range(qf_ref.shape[1] // width):
            phi_ref[g] = phi_rows(qft[g * width : (g + 1) * width], True).astype(F32).T.astype(BF)


def final_kernel(later_ref, q_ref, hk_ref, hv_ref, num_ref, den_ref, win_ref, sum_ref, top_ref, phi_ref, prior_ref, first_ref, gain_ref, out_ref, *, heads, width, blocks):
    h = pl.program_id(0)
    feats = feature_rows(width)
    base = heads * feats
    row = lax.broadcasted_iota(jnp.int32, (TILE, TILE), 0)
    col = lax.broadcasted_iota(jnp.int32, (TILE, TILE), 1)
    beyond = col > row
    scale = HEAD_DIM ** (-0.5) * LOG2E
    state = prior_ref[pl.ds(pl.multiple_of(h * feats, 16), feats), :]
    norm = [prior_ref[pl.ds(base + 2 * h + i, 1), :] for i in range(2)]
    add_state = first_ref[pl.ds(pl.multiple_of(h * feats, 16), feats), :]
    add_norm = [first_ref[pl.ds(base + 2 * h + i, 1), :] for i in range(2)]
    gain = gain_ref[...]

    def rhs(state, norm):
        wide = jnp.concatenate([jnp.broadcast_to(n, (HEAD_DIM, HEAD_DIM)) for n in norm], 1)
        cols = wide.T[:feats]
        return jnp.concatenate([state.astype(BF), cols.astype(BF)], 1)

    for b in range(blocks):
        if b == 1:
            state = state + add_state
            norm = [a + c for a, c in zip(norm, add_norm)]
        both = rhs(state, norm)
        for start in range(b * WINDOW, (b + 1) * WINDOW, TILE):
            at = slice(start, start + TILE)
            lin = nn(phi_ref[0, at, :], both)
            mixed = (num_ref[at, :] + lin[:, :HEAD_DIM]) / (den_ref[at, :] + lin[:, HEAD_DIM:])
            if b == 0:
                tiles = []
                for key_at in range(start, WINDOW, TILE):
                    ks = slice(key_at, key_at + TILE)
                    tiles.append((hk_ref[ks, :], hv_ref[ks, :], beyond if key_at == start else None))
                top, out, total = softmax_part(q_ref[at, :], tiles)
                top = jnp.where(later_ref[0] > 0, top, 2 * NEG)
                mine = top_ref[at, :]
                most = jnp.maximum(mine, top)
                here = jnp.exp2((mine - most) * scale)
                there = jnp.exp2((top - most) * scale)
                window = (win_ref[at, :] * here + out * there) / (sum_ref[at, :] * here + total * there)
            else:
                window = win_ref[at, :]
            mixed = mixed + window
            power = jnp.mean(mixed * mixed, 1, keepdims=True)
            out_ref[at, :] = (mixed * lax.rsqrt(power + 1e-05) * gain).astype(BF)


def shifted(value, axis, steps):
    count = lax.axis_size(axis)
    return lax.ppermute(value, axis, [(i, i + steps) for i in range(count - steps)])


def body(q_feat, k_feat, swa_query, swa_key, values, gain):
    tokens, columns = swa_query.shape
    heads = columns // HEAD_DIM
    width = q_feat.shape[1] // heads
    blocks = tokens // WINDOW
    feats = feature_rows(width)
    rows = state_rows(heads, width)
    halo_key = shifted(swa_key[tokens - WINDOW :], "seq", 1)
    halo_value = shifted(values[tokens - WINDOW :], "seq", 1)

    whole = lambda a: pl.BlockSpec(a.shape, lambda h: (0,) * a.ndim)
    vmem = pl.BlockSpec(memory_space=pltpu.VMEM)
    limit = pltpu.CompilerParams(vmem_limit_bytes=40 << 20)
    first, own = pl.pallas_call(
        functools.partial(state_kernel, heads=heads, width=width, blocks=blocks),
        out_shape=(jax.ShapeDtypeStruct((rows, HEAD_DIM), F32), jax.ShapeDtypeStruct((rows, HEAD_DIM), BF)),
        in_specs=[vmem] * 2,
        out_specs=(vmem, vmem),
        compiler_params=limit,
        cost_estimate=pl.CostEstimate(flops=2 * tokens * feats * columns, bytes_accessed=2 << 20, transcendentals=0),
        name="states",
    )(k_feat, values)

    prior = shifted(own, "seq", 1).astype(F32)
    running = own.astype(F32) + prior
    distance = 2
    count = lax.axis_size("seq")
    if count > 1:
        distance = 1
        prior = None
        running = own
        while distance < count:
            got = shifted(running.astype(BF), "seq", distance).astype(F32)
            prior = got if prior is None else prior + got
            running = running.astype(F32) + got
            distance *= 2

    col = pl.BlockSpec((tokens, HEAD_DIM), lambda h: (0, h))
    near = pl.BlockSpec((WINDOW, HEAD_DIM), lambda h: (0, h))
    phi_spec = pl.BlockSpec((heads, tokens, feats), lambda h: (0, 0, 0))
    big = jax.ShapeDtypeStruct((tokens, columns), F32)
    small = jax.ShapeDtypeStruct((WINDOW, columns), F32)
    num, den, win, total, top, phi = pl.pallas_call(
        functools.partial(local_kernel, width=width, blocks=blocks),
        grid=(heads,),
        out_shape=(big, big, big, small, small, jax.ShapeDtypeStruct((heads, tokens, feats), BF)),
        in_specs=[col, col, col, whole(q_feat), whole(k_feat)],
        out_specs=(col, col, col, near, near, phi_spec),
        compiler_params=limit,
        cost_estimate=pl.CostEstimate(flops=8 << 30, bytes_accessed=12 << 20, transcendentals=4 << 20),
        name="local",
    )(swa_query, swa_key, values, q_feat, k_feat)

    later = (lax.axis_index("seq") > 0).astype(jnp.int32).reshape(1)
    gain_row = gain.reshape(1, columns)
    state_spec = pl.BlockSpec((rows, HEAD_DIM), lambda h: (0, 0))
    return pl.pallas_call(
        functools.partial(final_kernel, heads=heads, width=width, blocks=blocks),
        grid=(heads,),
        out_shape=jax.ShapeDtypeStruct((tokens, columns), BF),
        in_specs=[
            pl.BlockSpec(memory_space=pltpu.SMEM),
            near, near, near, col, col, col, near, near,
            pl.BlockSpec((1, tokens, feats), lambda h: (h, 0, 0)),
            state_spec, state_spec,
            pl.BlockSpec((1, HEAD_DIM), lambda h: (0, h)),
        ],
        out_specs=col,
        compiler_params=limit,
        cost_estimate=pl.CostEstimate(flops=2 << 30, bytes_accessed=12 << 20, transcendentals=1 << 20),
        name="final",
    )(later, swa_query, halo_key, halo_value, num, den, win, total, top, phi, prior, first, gain_row)


def solution(mesh):
    tokens = P(("groups", "seq"), "head")
    return jax.shard_map(
        body, mesh=mesh, in_specs=(tokens,) * 5 + (P("head"),), out_specs=tokens, check_vma=False
    )
```

time: 112 us -> 59.1 us (0.53)
  the two profiles are of different devices: /device:TPU:0 before, /device:TPU:26 now
where the time goes in v1:
time: 59.1 us; the launch traced here: 58.5 us
  local copies, waits for them, and re-layouts  23.6 us (40%)
  Pallas kernels  17.6 us (30%)
  waiting for transfers between devices  10.1 us (17%)
  starting transfers between devices  5.13 us (9%)
  other arithmetic  1.77 us (3%)
    unnamed x46, local copies, waits for them, and re-layouts  21.9 us
    pallas_call x1, Pallas kernels, body(): pl.pallas_call(functools.partial(local_kernel, width=width, blocks=blocks...  10.3 us
    ppermute x4, waiting for transfers between devices, shifted(): lax.ppermute(value, axis, [(i, i + steps) for i in range(count - steps)])  10.1 us
    pallas_call x1, Pallas kernels, body(): pl.pallas_call(functools.partial(final_kernel, heads=heads, width=width,...  6.49 us
    ppermute x4, starting transfers between devices, shifted(): lax.ppermute(value, axis, [(i, i + steps) for i in range(count - steps)])  5.13 us
  transfers between devices with their start and end apart: 4, of which 2 were waited for; matrix products, arithmetic and copies ran while one was open for 7% of the time, Pallas kernels for 18%

profile of v1, /device:TPU:26, one launch (start us, length us, event | category | flops | bytes accessed | tf_op | source)
XLA Modules:
  0.0 58.5 jit_solution(12722706347097277094)
XLA Ops:
  0.0 1.1 %copy.8.kf_ref = bf16[1024,64]{1,0:T(8,128)(2,1)S(1)} copy(bf16[1024,64]{0,1:T(8,128)(2,1)} %param.7) | data formatting | bytes 262144 | tf_op args[1]
  1.1 1.2 %copy-done = bf16[1024,512]{1,0:T(8,128)(2,1)S(1)} copy-done((bf16[1024,512]{1,0:T(8,128)(2,1)S(1)}, bf16[1024,512]{1,0:T(8,128)(2,1)}, u32[]{:S(2)}) %copy-start) | copy-done | bytes 1048600
  3.2 1.3 %collective-permute-start.2 = (bf16[656,128]{1,0:T(8,128)(2,1)S(1)}, bf16[656,128]{1,0:T(8,128)(2,1)S(1)}, u32[]{:S(2)}, u32[]{:S(2)}) collective-permute-start(bf16[656,128]{1,0:T(8,128)(2,1)S(1)} %get-tuple-element.19), channel_id=1, source_target_pairs={{0,4},{4,8},{8,12},{1,5},{5,9},{9,13},{2,6},{6,10},{10,14},{3,7},{... | collective-permute-start | bytes 503816 | tf_op jit(solution)/shard_map/ppermute | solution.py:195
  5.4 1.3 %collective-permute-start.1 = (bf16[512,512]{1,0:T(8,128)(2,1)}, bf16[512,512]{1,0:T(8,128)(2,1)}, u32[]{:S(2)}, u32[]{:S(2)}) collective-permute-start(bf16[512,512]{1,0:T(8,128)(2,1)} %slice.7), channel_id=1, source_target_pairs={{0,4},{4,8},{8,12},{1,5},{5,9},{9,13},{2,6},{6,10},{10,14},{3,7},{... | collective-permute-start | bytes 1572872 | tf_op jit(solution)/shard_map/ppermute | solution.py:195
  7.6 1.3 %collective-permute-start = (bf16[512,512]{1,0:T(8,128)(2,1)}, bf16[512,512]{1,0:T(8,128)(2,1)}, u32[]{:S(2)}, u32[]{:S(2)}) collective-permute-start(bf16[512,512]{1,0:T(8,128)(2,1)} %slice.6), channel_id=1, source_target_pairs={{0,4},{4,8},{8,12},{1,5},{5,9},{9,13},{2,6},{6,10},{10,14},{3,7},{... | collective-permute-start | bytes 1572872 | tf_op jit(solution)/shard_map/ppermute | solution.py:195
  9.7 1.9 %collective-permute-done.2 = bf16[656,128]{1,0:T(8,128)(2,1)S(1)} collective-permute-done((bf16[656,128]{1,0:T(8,128)(2,1)S(1)}, bf16[656,128]{1,0:T(8,128)(2,1)S(1)}, u32[]{:S(2)}, u32[]{:S(2)}) %collective-permute-start.2) | collective-permute-done | bytes 167968 | tf_op jit(solution)/shard_map/ppermute | solution.py:195
  12.4 1.3 %collective-permute-start.3 = (bf16[656,128]{1,0:T(8,128)(2,1)}, bf16[656,128]{1,0:T(8,128)(2,1)}, u32[]{:S(2)}, u32[]{:S(2)}) collective-permute-start(bf16[656,128]{1,0:T(8,128)(2,1)} %fusion), channel_id=1, source_target_pairs={{0,8},{4,12},{1,9},{5,13},{2,10},{6,14},{3,11},{7,15},{16,24},{20,... | collective-permute-start | bytes 503816 | tf_op jit(solution)/shard_map/ppermute | solution.py:195
  13.7 1.2 %copy-done.8 = bf16[1024,512]{1,0:T(8,128)(2,1)S(1)} copy-done((bf16[1024,512]{1,0:T(8,128)(2,1)S(1)}, bf16[1024,512]{1,0:T(8,128)(2,1)}, u32[]{:S(2)}) %copy-start.8) | copy-done | bytes 1048600
  15.9 1.2 %copy-done.18 = bf16[1024,512]{1,0:T(8,128)(2,1)S(1)} copy-done((bf16[1024,512]{1,0:T(8,128)(2,1)S(1)}, bf16[1024,512]{1,0:T(8,128)(2,1)}, u32[]{:S(2)}) %copy-start.18) | copy-done | bytes 1048600
  17.1 10.3 %local.1 = (f32[1024,512]{1,0:T(8,128)S(1)}, f32[1024,512]{1,0:T(8,128)S(1)}, f32[1024,512]{1,0:T(8,128)S(1)}, f32[512,512]{1,0:T(8,128)S(1)}, f32[512,512]{1,0:...) custom-call(bf16[1024,512]{1,0:T(8,128)(2,1)S(1)} %copy-done.8, bf16[1024,512]{1,0:T(8,128)(2,1)S(1)} %copy-done.18, ...), custom_call_target="tpu_custom_call" | custom-call | flops 8589934592 | bytes 12582912 | tf_op jit(solution)/shard_map/local/pallas_call | solution.py:240
  27.4 1.3 %copy-done.2 = f32[1024,512]{1,0:T(8,128)} copy-done((f32[1024,512]{1,0:T(8,128)}, f32[1024,512]{1,0:T(8,128)S(1)}, u32[]{:S(2)}) %copy-start.2) | copy-done | bytes 2097176
  28.7 1.3 %copy-done.4 = f32[1024,512]{1,0:T(8,128)} copy-done((f32[1024,512]{1,0:T(8,128)}, f32[1024,512]{1,0:T(8,128)S(1)}, u32[]{:S(2)}) %copy-start.4) | copy-done | bytes 2097176
  30.0 1.4 %copy-done.6 = bf16[4,1024,160]{2,1,0:T(8,128)(2,1)} copy-done((bf16[4,1024,160]{2,1,0:T(8,128)(2,1)}, bf16[4,1024,160]{2,1,0:T(8,128)(2,1)S(1)}, u32[]{:S(2)}) %copy-start.6) | copy-done | bytes 1310744
  31.4 1.0 %copy-done.10 = f32[512,512]{1,0:T(8,128)} copy-done((f32[512,512]{1,0:T(8,128)}, f32[512,512]{1,0:T(8,128)S(1)}, u32[]{:S(2)}) %copy-start.10) | copy-done | bytes 1048600
  33.3 8.2 %collective-permute-done.3 = bf16[656,128]{1,0:T(8,128)(2,1)} collective-permute-done((bf16[656,128]{1,0:T(8,128)(2,1)}, bf16[656,128]{1,0:T(8,128)(2,1)}, u32[]{:S(2)}, u32[]{:S(2)}) %collective-permute-start.3) | collective-permute-done | bytes 167968 | tf_op jit(solution)/shard_map/ppermute | solution.py:195
  41.5 1.0 %convert_add_fusion.prior_ref = f32[656,128]{1,0:T(8,128)S(1)} fusion(bf16[656,128]{1,0:T(8,128)(2,1)} %copy-done.20, bf16[656,128]{1,0:T(8,128)(2,1)} %collective-permute-done.3), kind=kLoop, calls=%fused_computation | loop fusion | flops 251904 | bytes 671744 | tf_op jit(solution)/shard_map/add | solution.py:231
  42.6 1.6 %copy-done.3 = f32[1024,512]{1,0:T(8,128)S(1)} copy-done((f32[1024,512]{1,0:T(8,128)S(1)}, f32[1024,512]{1,0:T(8,128)}, u32[]{:S(2)}) %copy-start.3) | copy-done | bytes 2097176
  44.2 1.6 %copy-done.5 = f32[1024,512]{1,0:T(8,128)S(1)} copy-done((f32[1024,512]{1,0:T(8,128)S(1)}, f32[1024,512]{1,0:T(8,128)}, u32[]{:S(2)}) %copy-start.5) | copy-done | bytes 2097176
  45.8 1.6 %copy-done.7 = bf16[4,1024,160]{2,1,0:T(8,128)(2,1)S(1)} copy-done((bf16[4,1024,160]{2,1,0:T(8,128)(2,1)S(1)}, bf16[4,1024,160]{2,1,0:T(8,128)(2,1)}, u32[]{:S(2)}) %copy-start.7) | copy-done | bytes 1310744
  47.4 1.2 %copy-done.9 = bf16[1024,512]{1,0:T(8,128)(2,1)S(1)} copy-done((bf16[1024,512]{1,0:T(8,128)(2,1)S(1)}, bf16[1024,512]{1,0:T(8,128)(2,1)}, u32[]{:S(2)}) %copy-start.9) | copy-done | bytes 1048600
  48.6 1.2 %copy-done.11 = f32[512,512]{1,0:T(8,128)S(1)} copy-done((f32[512,512]{1,0:T(8,128)S(1)}, f32[512,512]{1,0:T(8,128)}, u32[]{:S(2)}) %copy-start.11) | copy-done | bytes 1048600
  49.8 1.2 %copy-done.13 = f32[512,512]{1,0:T(8,128)S(1)} copy-done((f32[512,512]{1,0:T(8,128)S(1)}, f32[512,512]{1,0:T(8,128)}, u32[]{:S(2)}) %copy-start.13) | copy-done | bytes 1048600
  51.0 1.0 %copy-done.15 = f32[656,128]{1,0:T(8,128)S(1)} copy-done((f32[656,128]{1,0:T(8,128)S(1)}, f32[656,128]{1,0:T(8,128)}, u32[]{:S(2)}) %copy-start.15) | copy-done | bytes 335896
  52.0 6.5 %final.1 = bf16[1024,512]{1,0:T(8,128)(2,1)} custom-call(s32[1]{0:T(128)} %bitcast.later_ref, bf16[1024,512]{1,0:T(8,128)(2,1)S(1)} %copy-done.9, bf16[512,512]{1,0:T(8,128)(2,1)} %collective-permute-done.hk_ref, bf16[512,512]{1,0:T(8,128)(2,1)} %collective-permute-done.1.hv_ref, f32[1024,512]{1,0:T(8,128)S(1)} %get-tuple-element.13.num_ref, ...), custom_call_target="tpu_custom_call" | custom-call | flops 2147483648 | bytes 12582912 | tf_op jit(solution)/shard_map/final/pallas_call | solution.py:254
  (37 shorter events, 6.1 us)
Async XLA Ops:
  0.0 8.8 %copy-start.21 = (bf16[1024,64]{0,1:T(8,128)(2,1)S(1)}, bf16[1024,64]{0,1:T(8,128)(2,1)}, u32[]{:S(2)}) copy-start(bf16[1024,64]{0,1:T(8,128)(2,1)} %param.6) | copy-start | bytes 393220
  1.1 1.2 %copy-start = (bf16[1024,512]{1,0:T(8,128)(2,1)S(1)}, bf16[1024,512]{1,0:T(8,128)(2,1)}, u32[]{:S(2)}) copy-start(bf16[1024,512]{1,0:T(8,128)(2,1)} %v_ref.3) | copy-start | bytes 3145732
  2.4 4.4 %copy-start.17 = (bf16[1024,512]{1,0:T(8,128)(2,1)S(1)}, bf16[1024,512]{1,0:T(8,128)(2,1)}, u32[]{:S(2)}) copy-start(bf16[1024,512]{1,0:T(8,128)(2,1)} %k_ref.1) | copy-start | bytes 3145732
  2.4 11.3 %copy-start.1 = (bf16[1024,512]{1,0:T(8,128)(2,1)S(1)}, bf16[1024,512]{1,0:T(8,128)(2,1)}, u32[]{:S(2)}) copy-start(bf16[1024,512]{1,0:T(8,128)(2,1)} %v_ref.3) | copy-start | bytes 3145732
  3.2 2.2 %copy-start.14 = (f32[656,128]{1,0:T(8,128)}, f32[656,128]{1,0:T(8,128)S(1)}, u32[]{:S(2)}) copy-start(f32[656,128]{1,0:T(8,128)S(1)} %get-tuple-element.20.first_ref) | copy-start | bytes 1007620
  3.2 8.4 %collective-permute-start.2 = (bf16[656,128]{1,0:T(8,128)(2,1)S(1)}, bf16[656,128]{1,0:T(8,128)(2,1)S(1)}, u32[]{:S(2)}, u32[]{:S(2)}) collective-permute-start(bf16[656,128]{1,0:T(8,128)(2,1)S(1)} %get-tuple-element.19), channel_id=1, source_target_pairs={{0,4},{4,8},{8,12},{1,5},{5,9},{9,13},{2,6},{6,10},{10,14},{3,7},{... | collective-permute-start | bytes 503816 | tf_op jit(solution)/shard_map/ppermute | solution.py:195
  5.4 37.1 %collective-permute-start.1 = (bf16[512,512]{1,0:T(8,128)(2,1)}, bf16[512,512]{1,0:T(8,128)(2,1)}, u32[]{:S(2)}, u32[]{:S(2)}) collective-permute-start(bf16[512,512]{1,0:T(8,128)(2,1)} %slice.7), channel_id=1, source_target_pairs={{0,4},{4,8},{8,12},{1,5},{5,9},{9,13},{2,6},{6,10},{10,14},{3,7},{... | collective-permute-start | bytes 1572872 | tf_op jit(solution)/shard_map/ppermute | solution.py:195
  7.6 35.0 %collective-permute-start = (bf16[512,512]{1,0:T(8,128)(2,1)}, bf16[512,512]{1,0:T(8,128)(2,1)}, u32[]{:S(2)}, u32[]{:S(2)}) collective-permute-start(bf16[512,512]{1,0:T(8,128)(2,1)} %slice.6), channel_id=1, source_target_pairs={{0,4},{4,8},{8,12},{1,5},{5,9},{9,13},{2,6},{6,10},{10,14},{3,7},{... | collective-permute-start | bytes 1572872 | tf_op jit(solution)/shard_map/ppermute | solution.py:195
  12.4 29.1 %collective-permute-start.3 = (bf16[656,128]{1,0:T(8,128)(2,1)}, bf16[656,128]{1,0:T(8,128)(2,1)}, u32[]{:S(2)}, u32[]{:S(2)}) collective-permute-start(bf16[656,128]{1,0:T(8,128)(2,1)} %fusion), channel_id=1, source_target_pairs={{0,8},{4,12},{1,9},{5,13},{2,10},{6,14},{3,11},{7,15},{16,24},{20,... | collective-permute-start | bytes 503816 | tf_op jit(solution)/shard_map/ppermute | solution.py:195
  13.7 1.2 %copy-start.8 = (bf16[1024,512]{1,0:T(8,128)(2,1)S(1)}, bf16[1024,512]{1,0:T(8,128)(2,1)}, u32[]{:S(2)}) copy-start(bf16[1024,512]{1,0:T(8,128)(2,1)} %q_ref.3) | copy-start | bytes 3145732
  15.9 1.2 %copy-start.18 = (bf16[1024,512]{1,0:T(8,128)(2,1)S(1)}, bf16[1024,512]{1,0:T(8,128)(2,1)}, u32[]{:S(2)}) copy-start(bf16[1024,512]{1,0:T(8,128)(2,1)} %k_ref.1) | copy-start | bytes 3145732
  17.1 25.5 %copy-start.19 = (f32[512]{0:T(512)S(1)}, f32[512]{0:T(512)}, u32[]{:S(2)}) copy-start(f32[512]{0:T(512)} %param.11) | copy-start | bytes 6148
  27.4 1.3 %copy-start.2 = (f32[1024,512]{1,0:T(8,128)}, f32[1024,512]{1,0:T(8,128)S(1)}, u32[]{:S(2)}) copy-start(f32[1024,512]{1,0:T(8,128)S(1)} %get-tuple-element.14.den_ref) | copy-start | bytes 6291460
  28.7 1.3 %copy-start.4 = (f32[1024,512]{1,0:T(8,128)}, f32[1024,512]{1,0:T(8,128)S(1)}, u32[]{:S(2)}) copy-start(f32[1024,512]{1,0:T(8,128)S(1)} %get-tuple-element.15.win_ref) | copy-start | bytes 6291460
  30.0 1.4 %copy-start.6 = (bf16[4,1024,160]{2,1,0:T(8,128)(2,1)}, bf16[4,1024,160]{2,1,0:T(8,128)(2,1)S(1)}, u32[]{:S(2)}) copy-start(bf16[4,1024,160]{2,1,0:T(8,128)(2,1)S(1)} %get-tuple-element.18.phi_ref) | copy-start | bytes 3932164
  31.4 1.0 %copy-start.10 = (f32[512,512]{1,0:T(8,128)}, f32[512,512]{1,0:T(8,128)S(1)}, u32[]{:S(2)}) copy-start(f32[512,512]{1,0:T(8,128)S(1)} %get-tuple-element.16.sum_ref) | copy-start | bytes 3145732
  32.4 1.0 %copy-start.12 = (f32[512,512]{1,0:T(8,128)}, f32[512,512]{1,0:T(8,128)S(1)}, u32[]{:S(2)}) copy-start(f32[512,512]{1,0:T(8,128)S(1)} %get-tuple-element.17.top_ref) | copy-start | bytes 3145732
  42.6 1.6 %copy-start.3 = (f32[1024,512]{1,0:T(8,128)S(1)}, f32[1024,512]{1,0:T(8,128)}, u32[]{:S(2)}) copy-start(f32[1024,512]{1,0:T(8,128)} %copy-done.2) | copy-start | bytes 6291460
  44.2 1.6 %copy-start.5 = (f32[1024,512]{1,0:T(8,128)S(1)}, f32[1024,512]{1,0:T(8,128)}, u32[]{:S(2)}) copy-start(f32[1024,512]{1,0:T(8,128)} %copy-done.4) | copy-start | bytes 6291460
  45.8 1.6 %copy-start.7 = (bf16[4,1024,160]{2,1,0:T(8,128)(2,1)S(1)}, bf16[4,1024,160]{2,1,0:T(8,128)(2,1)}, u32[]{:S(2)}) copy-start(bf16[4,1024,160]{2,1,0:T(8,128)(2,1)} %copy-done.6) | copy-start | bytes 3932164
  47.4 1.2 %copy-start.9 = (bf16[1024,512]{1,0:T(8,128)(2,1)S(1)}, bf16[1024,512]{1,0:T(8,128)(2,1)}, u32[]{:S(2)}) copy-start(bf16[1024,512]{1,0:T(8,128)(2,1)} %q_ref.3) | copy-start | bytes 3145732
  48.6 1.2 %copy-start.11 = (f32[512,512]{1,0:T(8,128)S(1)}, f32[512,512]{1,0:T(8,128)}, u32[]{:S(2)}) copy-start(f32[512,512]{1,0:T(8,128)} %copy-done.10) | copy-start | bytes 3145732
  49.8 1.2 %copy-start.13 = (f32[512,512]{1,0:T(8,128)S(1)}, f32[512,512]{1,0:T(8,128)}, u32[]{:S(2)}) copy-start(f32[512,512]{1,0:T(8,128)} %copy-done.12) | copy-start | bytes 3145732
  51.0 1.0 %copy-start.15 = (f32[656,128]{1,0:T(8,128)S(1)}, f32[656,128]{1,0:T(8,128)}, u32[]{:S(2)}) copy-start(f32[656,128]{1,0:T(8,128)} %copy-done.14) | copy-start | bytes 1007620
  (2 other events, 1.7 us)

commit v2 on v1

v2 whole, which is shorter than its diff:
```python
import functools

import jax
import jax.numpy as jnp
from jax import lax
from jax.experimental import pallas as pl
from jax.experimental.pallas import tpu as pltpu
from jax.sharding import PartitionSpec as P

HEAD_DIM = 128
WINDOW = 512
TILE = 256
NEG = -1e30
SCALE = HEAD_DIM ** (-0.5) * 1.4426950408889634
BF = jnp.bfloat16
F32 = jnp.float32
GRANT = 16 << 20


def feature_rows(width):
    return -(-(width * (width + 1) // 2 + width + 1) // 16) * 16


def state_rows(heads, width):
    return heads * feature_rows(width) + 16


def nt(a, b):
    return lax.dot_general(a, b, (((1,), (1,)), ((), ())), preferred_element_type=F32)


def nn(a, b):
    return jnp.dot(a, b, preferred_element_type=F32)


def phi_rows(x, query):
    width, tokens = x.shape
    half = width // 2
    scale = 0.5**0.5 * width ** (-0.5)
    twice = jnp.concatenate([x, x], 0)
    rows = []
    for d in range(half):
        prod = ((x * twice[d : d + width]) * scale).astype(BF)
        if query and d:
            prod = prod * 2
        rows.append(prod)
    rows.append((x * width ** (-0.25)).astype(BF))
    cross = (x[:half] * x[half:]) * scale
    if query:
        cross = cross * 2
    pad = feature_rows(width) - (half * width + width + half)
    last = lax.broadcasted_iota(jnp.int32, (pad, tokens), 0)
    const = jnp.where(last == 0, 1.0, 0.0)
    rows.append(jnp.concatenate([cross, const], 0).astype(BF))
    return jnp.concatenate(rows, 0)


def with_ones(v):
    return jnp.concatenate([v, jnp.ones_like(v)], 1)


def lanes_of(h, count=1):
    return pl.ds(pl.multiple_of(h * HEAD_DIM, HEAD_DIM), count * HEAD_DIM)


def causal_masks():
    row = lax.broadcasted_iota(jnp.int32, (TILE, TILE), 0)
    col = lax.broadcasted_iota(jnp.int32, (TILE, TILE), 1)
    return col <= row, col > row


def prepare_kernel(kf_ref, q_ref, k_ref, v_ref, kv_ref, qb_ref, own_ref, first_ref, v_buf, sems, *, heads, width, blocks):
    feats = feature_rows(width)
    base = heads * feats
    tokens = v_buf.shape[0]
    ahead = heads // 2 * HEAD_DIM
    tail = pl.ds(tokens - WINDOW, WINDOW)
    copies = [
        pltpu.make_async_copy(v_ref, v_buf, sems.at[0]),
        pltpu.make_async_copy(k_ref.at[tail, :ahead], kv_ref.at[:WINDOW], sems.at[1]),
        pltpu.make_async_copy(v_ref.at[tail, :ahead], kv_ref.at[WINDOW:], sems.at[2]),
        pltpu.make_async_copy(q_ref.at[:WINDOW, ahead:], qb_ref, sems.at[3]),
    ]
    for copy in copies:
        copy.start()
    ones = jnp.ones((16, WINDOW), BF)
    first_ref[base:, :] = jnp.zeros((16, HEAD_DIM), F32)
    own_ref[base:, :] = jnp.zeros((16, HEAD_DIM), BF)
    copies[0].wait()
    for h in range(heads):
        phi = phi_rows(kf_ref[h * width : (h + 1) * width, :].astype(F32), False)
        total, norm = None, None
        for b in range(blocks):
            part = phi[:, b * WINDOW : (b + 1) * WINDOW]
            s = nn(part, v_buf[b * WINDOW : (b + 1) * WINDOW, h * HEAD_DIM : (h + 1) * HEAD_DIM])
            n = nt(ones, part)
            total = s if b == 0 else total + s
            norm = n if b == 0 else norm + n
            if b == 0:
                first_ref[h * feats : (h + 1) * feats, :] = s
                first_ref[base + 2 * h : base + 2 * h + 1, :] = n[:1, :HEAD_DIM]
                first_ref[base + 2 * h + 1 : base + 2 * h + 2, : feats - HEAD_DIM] = n[:1, HEAD_DIM:]
        own_ref[h * feats : (h + 1) * feats, :] = total.astype(BF)
        own_ref[base + 2 * h : base + 2 * h + 1, :] = norm[:1, :HEAD_DIM].astype(BF)
        own_ref[base + 2 * h + 1 : base + 2 * h + 2, : feats - HEAD_DIM] = norm[:1, HEAD_DIM:].astype(BF)
    for copy in copies[1:]:
        copy.wait()


def softmax_part(q, tiles):
    scores = []
    for key, _, mask in tiles:
        s = nt(q, key)
        scores.append(s if mask is None else jnp.where(mask, s, NEG))
    top = functools.reduce(jnp.maximum, scores)
    top = jnp.max(top, 1, keepdims=True)
    acc = None
    for s, (_, value, _) in zip(scores, tiles):
        p = jnp.exp2((s - top) * SCALE).astype(BF)
        part = nn(p, with_ones(value))
        acc = part if acc is None else acc + part
    return top, acc[:, :HEAD_DIM], acc[:, HEAD_DIM:]


def local_kernel(q_ref, k_ref, v_ref, qf_ref, kf_ref, num_ref, den_ref, win_ref, sum_ref, top_ref, phi_ref, *, start_head, width):
    causal, beyond = causal_masks()
    tokens = q_ref.shape[0]
    feats = feature_rows(width)

    def head(g, carry):
        h = g + start_head
        rows = pl.ds(pl.multiple_of(h * width, width), width)
        phi = phi_rows(qf_ref[rows, :].astype(F32), True).astype(F32).T.astype(BF)
        phi_ref[g] = phi
        kf = kf_ref[rows, :]
        kf = jnp.concatenate([kf, jnp.zeros((feats - HEAD_DIM - width, tokens), BF)], 0)
        for start in range(0, tokens, TILE):
            at = slice(start, start + TILE)
            tiles = []
            for back, mask in ((WINDOW, beyond), (WINDOW - TILE, None), (0, causal)):
                key_at = start - back
                if key_at >= 0:
                    ks = slice(key_at, key_at + TILE)
                    tiles.append((k_ref[ks, lanes_of(h)], v_ref[ks, lanes_of(h)], mask))
            top, out, total = softmax_part(q_ref[at, lanes_of(h)], tiles)
            if start >= WINDOW:
                win_ref[at, lanes_of(g)] = out / total
            else:
                win_ref[at, lanes_of(g)] = out
                sum_ref[at, lanes_of(g)] = total
                top_ref[at, lanes_of(g)] = jnp.broadcast_to(top, (TILE, HEAD_DIM))
            qf = phi[at, HEAD_DIM:]
            acc = None
            for key_at in range(start - start % WINDOW, start + TILE, TILE):
                ks = slice(key_at, key_at + TILE)
                r = nn(qf, kf[:, ks])
                half = width ** (-0.25)
                t = (r * (0.5 * half * half) + half) * r + 1.0
                if key_at == start:
                    t = jnp.where(causal, t, 0.0)
                part = nn(t.astype(BF), with_ones(v_ref[ks, lanes_of(h)]))
                acc = part if acc is None else acc + part
            num_ref[at, lanes_of(g)] = acc[:, :HEAD_DIM]
            den_ref[at, lanes_of(g)] = acc[:, HEAD_DIM:]
        return carry

    lax.fori_loop(0, num_ref.shape[1] // HEAD_DIM, head, 0)


def beyond_tiles(start, keys, values, beyond):
    tiles = []
    for key_at in range(start, WINDOW, TILE):
        ks = slice(key_at, key_at + TILE)
        tiles.append((keys(ks), values(ks), beyond if key_at == start else None))
    return tiles


def serve_kernel(qb_ref, k_ref, v_ref, out_ref, *, behind):
    _, beyond = causal_masks()
    base = k_ref.shape[0] - WINDOW
    count = qb_ref.shape[1] // HEAD_DIM
    lane = lax.broadcasted_iota(jnp.int32, (TILE, HEAD_DIM), 1)
    for start in range(0, WINDOW, TILE):
        at = slice(start, start + TILE)
        stats = jnp.zeros((TILE, HEAD_DIM), F32)
        for g in range(count):
            cols = slice((behind + g) * HEAD_DIM, (behind + g + 1) * HEAD_DIM)
            tiles = beyond_tiles(
                start,
                lambda ks: k_ref[base + ks.start : base + ks.stop, cols],
                lambda ks: v_ref[base + ks.start : base + ks.stop, cols],
                beyond,
            )
            top, out, total = softmax_part(qb_ref[at, g * HEAD_DIM : (g + 1) * HEAD_DIM], tiles)
            out_ref[at, g * HEAD_DIM : (g + 1) * HEAD_DIM] = out.astype(BF)
            stats = jnp.where(lane == g, top, stats)
            stats = jnp.where(lane == count + g, total, stats)
        stats = stats.T[: 2 * count]
        high = stats.astype(BF).astype(F32)
        middle = (stats - high).astype(BF).astype(F32)
        low = stats - high - middle
        pad = jnp.zeros((16 - 6 * count, TILE), F32)
        rows = jnp.concatenate([high, middle, low, pad], 0)
        line = WINDOW + start // TILE * 16
        out_ref[line : line + 16, :] = rows.astype(BF)


def final_kernel(later_ref, q_ref, kv_ref, ob_ref, *refs, heads, width, blocks):
    halves = [refs[:6], refs[6:12]]
    prior_ref, first_ref, gain_ref, out_ref = refs[12:]
    count = heads // 2
    feats = feature_rows(width)
    base = heads * feats
    _, beyond = causal_masks()

    def rhs(state, norm):
        wide = jnp.concatenate([jnp.broadcast_to(n, (HEAD_DIM, HEAD_DIM)) for n in norm], 1)
        cols = wide.T[:feats]
        return jnp.concatenate([state.astype(BF), cols.astype(BF)], 1)

    def one(g, part):
        h = g + part * count
        num_ref, den_ref, win_ref, sum_ref, top_ref, phi_ref = halves[part]
        rows = pl.ds(pl.multiple_of(h * feats, 16), feats)
        state = prior_ref[rows, :]
        norm = [prior_ref[pl.ds(base + 2 * h + i, 1), :] for i in range(2)]
        gain = gain_ref[:, lanes_of(h)]
        for b in range(blocks):
            if b == 1:
                state = state + first_ref[rows, :]
                norm = [n + first_ref[pl.ds(base + 2 * h + i, 1), :] for i, n in enumerate(norm)]
            both = rhs(state, norm)
            for start in range(b * WINDOW, (b + 1) * WINDOW, TILE):
                at = slice(start, start + TILE)
                lin = nn(phi_ref[g, at, :], both)
                mixed = (num_ref[at, lanes_of(g)] + lin[:, :HEAD_DIM]) / (den_ref[at, lanes_of(g)] + lin[:, HEAD_DIM:])
                window = win_ref[at, lanes_of(g)]
                if b == 0:
                    if part == 0:
                        tiles = beyond_tiles(
                            start,
                            lambda ks: kv_ref[ks, lanes_of(g)],
                            lambda ks: kv_ref[WINDOW + ks.start : WINDOW + ks.stop, lanes_of(g)],
                            beyond,
                        )
                        top, out, total = softmax_part(q_ref[at, lanes_of(h)], tiles)
                    else:
                        line = WINDOW + start // TILE * 16
                        stats = ob_ref[line : line + 16, :].astype(F32)
                        n = 2 * count
                        stats = stats[:n] + stats[n : 2 * n] + stats[2 * n : 3 * n]
                        stats = jnp.concatenate([stats, jnp.zeros((HEAD_DIM - n, TILE), F32)], 0).T
                        lane = lax.broadcasted_iota(jnp.int32, (TILE, HEAD_DIM), 1)
                        top = jnp.sum(jnp.where(lane == g, stats, 0.0), 1, keepdims=True)
                        total = jnp.sum(jnp.where(lane == count + g, stats, 0.0), 1, keepdims=True)
                        out = ob_ref[at, lanes_of(g)].astype(F32)
                    top = jnp.where(later_ref[0] > 0, top, 2 * NEG)
                    mine = top_ref[at, lanes_of(g)]
                    most = jnp.maximum(mine, top)
                    here = jnp.exp2((mine - most) * SCALE)
                    there = jnp.exp2((top - most) * SCALE)
                    window = (window * here + out * there) / (sum_ref[at, lanes_of(g)] * here + total * there)
                mixed = mixed + window
                power = jnp.mean(mixed * mixed, 1, keepdims=True)
                out_ref[at, lanes_of(h)] = (mixed * lax.rsqrt(power + 1e-05) * gain).astype(BF)

    def pair(g, carry):
        one(g, 0)
        one(g, 1)
        return carry

    lax.fori_loop(0, count, pair, 0)


def shifted(value, axis, steps):
    count = lax.axis_size(axis)
    pairs = [(i, i + steps) for i in range(count) if 0 <= i + steps < count]
    return lax.ppermute(value, axis, pairs)


def body(q_feat, k_feat, swa_query, swa_key, values, gain):
    tokens, columns = swa_query.shape
    heads = columns // HEAD_DIM
    half = heads // 2
    width = q_feat.shape[1] // heads
    blocks = tokens // WINDOW
    feats = feature_rows(width)
    rows = state_rows(heads, width)
    count = lax.axis_size("seq")
    vmem = pl.BlockSpec(memory_space=pltpu.VMEM)
    hbm = pl.BlockSpec(memory_space=pltpu.HBM)
    grant = pltpu.CompilerParams(vmem_limit_bytes=GRANT)
    qft, kft = q_feat.T, k_feat.T

    kv, qb, own, first = pl.pallas_call(
        functools.partial(prepare_kernel, heads=heads, width=width, blocks=blocks),
        out_shape=(
            jax.ShapeDtypeStruct((2 * WINDOW, half * HEAD_DIM), BF),
            jax.ShapeDtypeStruct((WINDOW, half * HEAD_DIM), BF),
            jax.ShapeDtypeStruct((rows, HEAD_DIM), BF),
            jax.ShapeDtypeStruct((rows, HEAD_DIM), F32),
        ),
        in_specs=[vmem, hbm, hbm, hbm],
        out_specs=(hbm, hbm, vmem, vmem),
        scratch_shapes=[pltpu.VMEM((tokens, columns), BF), pltpu.SemaphoreType.DMA((4,))],
        compiler_params=grant,
        cost_estimate=pl.CostEstimate(flops=1 << 30, bytes_accessed=3 << 20, transcendentals=0),
        name="prepare",
    )(kft, swa_query, swa_key, values)

    def local(start_head):
        wide = jax.ShapeDtypeStruct((tokens, half * HEAD_DIM), F32)
        near = jax.ShapeDtypeStruct((WINDOW, half * HEAD_DIM), F32)
        return pl.pallas_call(
            functools.partial(local_kernel, start_head=start_head, width=width),
            out_shape=(wide, wide, wide, near, near, jax.ShapeDtypeStruct((half, tokens, feats), BF)),
            in_specs=[vmem] * 5,
            out_specs=(vmem,) * 6,
            compiler_params=grant,
            cost_estimate=pl.CostEstimate(flops=4 << 30, bytes_accessed=6 << 20, transcendentals=2 << 20),
            name="local",
        )(swa_query, swa_key, values, qft, kft)

    if count <= 4:
        running, prior = own, None
        for i in range(count - 1):
            got = lax.ppermute(running, "seq", [(i, i + 1)])
            prior = got.astype(F32) if prior is None else prior + got.astype(F32)
            running = own + got
            if i == 0:
                halo = shifted(kv, "seq", 1)
                asked = shifted(qb, "seq", -1)
    else:
        running, prior, distance = own, None, 1
        halo = shifted(kv, "seq", 1)
        asked = shifted(qb, "seq", -1)
        while distance < count:
            got = shifted(running.astype(BF), "seq", distance).astype(F32)
            prior = got if prior is None else prior + got
            running = running.astype(F32) + got
            distance *= 2

    local_a = local(0)
    answer = pl.pallas_call(
        functools.partial(serve_kernel, behind=half),
        out_shape=jax.ShapeDtypeStruct((WINDOW + 16 * (WINDOW // TILE), half * HEAD_DIM), BF),
        in_specs=[vmem] * 3,
        out_specs=vmem,
        compiler_params=grant,
        cost_estimate=pl.CostEstimate(flops=1 << 30, bytes_accessed=2 << 20, transcendentals=1 << 19),
        name="serve",
    )(asked, swa_key, values)
    answered = shifted(answer, "seq", 1)
    local_b = local(half)

    later = (lax.axis_index("seq") > 0).astype(jnp.int32).reshape(1)
    return pl.pallas_call(
        functools.partial(final_kernel, heads=heads, width=width, blocks=blocks),
        out_shape=jax.ShapeDtypeStruct((tokens, columns), BF),
        in_specs=[pl.BlockSpec(memory_space=pltpu.SMEM)] + [vmem] * 18,
        out_specs=vmem,
        compiler_params=grant,
        cost_estimate=pl.CostEstimate(flops=2 << 30, bytes_accessed=12 << 20, transcendentals=1 << 20),
        name="final",
    )(later, swa_query, halo, answered, *local_a, *local_b, prior, first, gain.reshape(1, columns))


def solution(mesh):
    tokens = P(("groups", "seq"), "head")
    return jax.shard_map(
        body, mesh=mesh, in_specs=(tokens,) * 5 + (P("head"),), out_specs=tokens, check_vma=False
    )
```

time: 59.1 us -> 61.5 us (1.041)
  the two profiles are of different devices: /device:TPU:26 before, /device:TPU:22 now
where the time goes in v2:
time: 61.5 us; the launch traced here: 60.7 us
  local copies, waits for them, and re-layouts  22 us (36%)
  Pallas kernels  16.2 us (26%)
  starting transfers between devices  11.8 us (19%)
  waiting for transfers between devices  8.53 us (14%)
  other arithmetic  1.99 us (3%)
    unnamed x62, local copies, waits for them, and re-layouts  22 us
    ppermute x3, waiting for transfers between devices, body(): got = lax.ppermute(running, 'seq', [(i, i + 1)])  8.52 us
    pallas_call x2, Pallas kernels, local(): pl.pallas_call(functools.partial(local_kernel, start_head=start_head, wid...  8.2 us
    ppermute x3, starting transfers between devices, shifted(): return lax.ppermute(value, axis, pairs)  7.91 us
    pallas_call x1, Pallas kernels, body(): pl.pallas_call(functools.partial(final_kernel, heads=heads, width=width,...  5.36 us
    ppermute x3, starting transfers between devices, body(): got = lax.ppermute(running, 'seq', [(i, i + 1)])  3.9 us
    pallas_call x1, Pallas kernels, body(): pl.pallas_call(functools.partial(serve_kernel, behind=half), out_shape=ja...  1.68 us
  transfers between devices with their start and end apart: 6, of which 1 were waited for; matrix products, arithmetic and copies ran while one was open for 3% of the time, Pallas kernels for 16%

profile of v2, /device:TPU:22, one launch (start us, length us, event | category | flops | bytes accessed | tf_op | source)
XLA Modules:
  0.0 60.7 jit_solution(7057628360553057649)
XLA Ops:
  0.0 1.2 %copy-done = bf16[1024,512]{1,0:T(8,128)(2,1)S(1)} copy-done((bf16[1024,512]{1,0:T(8,128)(2,1)S(1)}, bf16[1024,512]{1,0:T(8,128)(2,1)}, u32[]{:S(2)}) %copy-start) | copy-done | bytes 1048600
  1.2 1.2 %copy-done.23 = bf16[1024,512]{1,0:T(8,128)(2,1)S(1)} copy-done((bf16[1024,512]{1,0:T(8,128)(2,1)S(1)}, bf16[1024,512]{1,0:T(8,128)(2,1)}, u32[]{:S(2)}) %copy-start.23) | copy-done | bytes 1048600
  2.5 1.2 %copy-done.25 = bf16[1024,512]{1,0:T(8,128)(2,1)S(1)} copy-done((bf16[1024,512]{1,0:T(8,128)(2,1)S(1)}, bf16[1024,512]{1,0:T(8,128)(2,1)}, u32[]{:S(2)}) %copy-start.25) | copy-done | bytes 1048600
  6.2 3.0 %collective-permute-start.1 = (bf16[512,256]{1,0:T(8,128)(2,1)S(1)}, bf16[512,256]{1,0:T(8,128)(2,1)S(1)}, u32[]{:S(2)}, u32[]{:S(2)}) collective-permute-start(bf16[512,256]{1,0:T(8,128)(2,1)S(1)} %get-tuple-element.22), channel_id=1, source_target_pairs={{4,0},{8,4},{12,8},{5,1},{9,5},{13,9},{6,2},{10,6},{14,10},{7,3},{... | collective-permute-start | bytes 786440 | tf_op jit(solution)/shard_map/ppermute | solution.py:278
  9.2 3.0 %collective-permute-start = (bf16[1024,256]{1,0:T(8,128)(2,1)}, bf16[1024,256]{1,0:T(8,128)(2,1)}, u32[]{:S(2)}, u32[]{:S(2)}) collective-permute-start(bf16[1024,256]{1,0:T(8,128)(2,1)} %get-tuple-element.21), channel_id=1, source_target_pairs={{0,4},{4,8},{8,12},{1,5},{5,9},{9,13},{2,6},{6,10},{10,14},{3,7},{... | collective-permute-start | bytes 1572872 | tf_op jit(solution)/shard_map/ppermute | solution.py:278
  12.9 1.3 %collective-permute-start.4 = (bf16[656,128]{1,0:T(8,128)(2,1)S(1)}, bf16[656,128]{1,0:T(8,128)(2,1)S(1)}, u32[]{:S(2)}, u32[]{:S(2)}) collective-permute-start(bf16[656,128]{1,0:T(8,128)(2,1)S(1)} %add.12), channel_id=1, source_target_pairs={{4,8},{5,9},{6,10},{7,11},{20,24},{21,25},{22,26},{23,27}} | collective-permute-start | bytes 503816 | tf_op jit(solution)/shard_map/ppermute | solution.py:327
  14.2 4.1 %local.3 = (f32[1024,256]{1,0:T(8,128)S(1)}, f32[1024,256]{1,0:T(8,128)S(1)}, f32[1024,256]{1,0:T(8,128)S(1)}, f32[512,256]{1,0:T(8,128)S(1)}, f32[512,256]{1,0:...) custom-call(bf16[1024,512]{1,0:T(8,128)(2,1)S(1)} %copy-done, bf16[1024,512]{1,0:T(8,128)(2,1)S(1)} %copy-done.23, ...), custom_call_target="tpu_custom_call" | custom-call | flops 4294967296 | bytes 6291456 | tf_op jit(solution)/shard_map/local/pallas_call | solution.py:314
  18.4 1.7 %serve.1 = bf16[544,256]{1,0:T(8,128)(2,1)} custom-call(bf16[512,256]{1,0:T(8,128)(2,1)S(1)} %collective-permute-done.1.qb_ref, bf16[1024,512]{1,0:T(8,128)(2,1)S(1)} %copy-done.24, bf16[1024,512]{1,0:T(8,128)(2,1)S(1)} %copy-done.26), custom_call_target="tpu_custom_call" | custom-call | flops 1073741824 | bytes 2097152 | tf_op jit(solution)/shard_map/serve/pallas_call | solution.py:344
  20.1 1.9 %collective-permute-start.2 = (bf16[544,256]{1,0:T(8,128)(2,1)}, bf16[544,256]{1,0:T(8,128)(2,1)}, u32[]{:S(2)}, u32[]{:S(2)}) collective-permute-start(bf16[544,256]{1,0:T(8,128)(2,1)} %serve.1), channel_id=1, source_target_pairs={{0,4},{4,8},{8,12},{1,5},{5,9},{9,13},{2,6},{6,10},{10,14},{3,7},{... | collective-permute-start | bytes 835592 | tf_op jit(solution)/shard_map/ppermute | solution.py:278
  22.0 8.5 %collective-permute-done.4 = bf16[656,128]{1,0:T(8,128)(2,1)S(1)} collective-permute-done((bf16[656,128]{1,0:T(8,128)(2,1)S(1)}, bf16[656,128]{1,0:T(8,128)(2,1)S(1)}, u32[]{:S(2)}, u32[]{:S(2)}) %collective-permute-start.4) | collective-permute-done | bytes 167968 | tf_op jit(solution)/shard_map/ppermute | solution.py:327
  31.2 1.9 %collective-permute-start.5 = (bf16[656,128]{1,0:T(8,128)(2,1)}, bf16[656,128]{1,0:T(8,128)(2,1)}, u32[]{:S(2)}, u32[]{:S(2)}) collective-permute-start(bf16[656,128]{1,0:T(8,128)(2,1)} %add.14), channel_id=1, source_target_pairs={{8,12},{9,13},{10,14},{11,15},{24,28},{25,29},{26,30},{27,31}} | collective-permute-start | bytes 503816 | tf_op jit(solution)/shard_map/ppermute | solution.py:327
  33.2 4.1 %local.2 = (f32[1024,256]{1,0:T(8,128)S(1)}, f32[1024,256]{1,0:T(8,128)S(1)}, f32[1024,256]{1,0:T(8,128)S(1)}, f32[512,256]{1,0:T(8,128)S(1)}, f32[512,256]{1,0:...) custom-call(bf16[1024,512]{1,0:T(8,128)(2,1)S(1)} %copy-done.1, bf16[1024,512]{1,0:T(8,128)(2,1)S(1)} %copy-done.24, ...), custom_call_target="tpu_custom_call" | custom-call | flops 4294967296 | bytes 6291456 | tf_op jit(solution)/shard_map/local/pallas_call | solution.py:314
  40.3 1.0 %copy-done.12 = bf16[2,1024,160]{2,1,0:T(8,128)(2,1)} copy-done((bf16[2,1024,160]{2,1,0:T(8,128)(2,1)}, bf16[2,1024,160]{2,1,0:T(8,128)(2,1)S(1)}, u32[]{:S(2)}) %copy-start.12) | copy-done | bytes 655384
  43.0 1.2 %convert_add_fusion.refs_12_ = f32[656,128]{1,0:T(8,128)S(1)} fusion(bf16[656,128]{1,0:T(8,128)(2,1)} %collective-permute-done.5, bf16[656,128]{1,0:T(8,128)(2,1)} %copy-done.30, bf16[656,128]{1,0:T(8,128)(2,1)} %copy-done.29), kind=kLoop, calls=%fused_computation | loop fusion | flops 419840 | bytes 839680 | tf_op jit(solution)/shard_map/add | solution.py:328
  44.9 1.2 %copy-done.3 = f32[1024,256]{1,0:T(8,128)S(1)} copy-done((f32[1024,256]{1,0:T(8,128)S(1)}, f32[1024,256]{1,0:T(8,128)}, u32[]{:S(2)}) %copy-start.3) | copy-done | bytes 1048600
  46.1 1.2 %copy-done.5 = bf16[2,1024,160]{2,1,0:T(8,128)(2,1)S(1)} copy-done((bf16[2,1024,160]{2,1,0:T(8,128)(2,1)S(1)}, bf16[2,1024,160]{2,1,0:T(8,128)(2,1)}, u32[]{:S(2)}) %copy-start.5) | copy-done | bytes 655384
  47.3 1.2 %copy-done.7 = f32[1024,256]{1,0:T(8,128)S(1)} copy-done((f32[1024,256]{1,0:T(8,128)S(1)}, f32[1024,256]{1,0:T(8,128)}, u32[]{:S(2)}) %copy-start.7) | copy-done | bytes 1048600
  48.6 1.2 %copy-done.9 = f32[1024,256]{1,0:T(8,128)S(1)} copy-done((f32[1024,256]{1,0:T(8,128)S(1)}, f32[1024,256]{1,0:T(8,128)}, u32[]{:S(2)}) %copy-start.9) | copy-done | bytes 1048600
  49.8 1.2 %copy-done.11 = f32[1024,256]{1,0:T(8,128)S(1)} copy-done((f32[1024,256]{1,0:T(8,128)S(1)}, f32[1024,256]{1,0:T(8,128)}, u32[]{:S(2)}) %copy-start.11) | copy-done | bytes 1048600
  51.0 1.2 %copy-done.13 = bf16[2,1024,160]{2,1,0:T(8,128)(2,1)S(1)} copy-done((bf16[2,1024,160]{2,1,0:T(8,128)(2,1)S(1)}, bf16[2,1024,160]{2,1,0:T(8,128)(2,1)}, u32[]{:S(2)}) %copy-start.13) | copy-done | bytes 655384
  52.2 1.0 %copy-done.17 = f32[512,256]{1,0:T(8,128)S(1)} copy-done((f32[512,256]{1,0:T(8,128)S(1)}, f32[512,256]{1,0:T(8,128)}, u32[]{:S(2)}) %copy-start.17) | copy-done | bytes 524312
  53.3 1.0 %copy-done.19 = f32[512,256]{1,0:T(8,128)S(1)} copy-done((f32[512,256]{1,0:T(8,128)S(1)}, f32[512,256]{1,0:T(8,128)}, u32[]{:S(2)}) %copy-start.19) | copy-done | bytes 524312
  54.3 1.0 %copy-done.21 = f32[512,256]{1,0:T(8,128)S(1)} copy-done((f32[512,256]{1,0:T(8,128)S(1)}, f32[512,256]{1,0:T(8,128)}, u32[]{:S(2)}) %copy-start.21) | copy-done | bytes 524312
  55.4 5.4 %final.1 = bf16[1024,512]{1,0:T(8,128)(2,1)} custom-call(s32[1]{0:T(128)} %bitcast.later_ref, bf16[1024,512]{1,0:T(8,128)(2,1)S(1)} %copy-done.1, bf16[1024,256]{1,0:T(8,128)(2,1)} %collective-permute-done.kv_ref, bf16[544,256]{1,0:T(8,128)(2,1)} %collective-permute-done.2.ob_ref, f32[1024,256]{1,0:T(8,128)S(1)} %copy-done.7, f32[1024,256]{1,0:T(8,128)S(1)} %copy-done.9, ...), custom_call_target="tpu_custom_call" | custom-call | flops 2147483648 | bytes 12582912 | tf_op jit(solution)/shard_map/final/pallas_call | solution.py:357
  (58 shorter events, 9.3 us)
Async XLA Ops:
  0.0 1.2 %copy-start = (bf16[1024,512]{1,0:T(8,128)(2,1)S(1)}, bf16[1024,512]{1,0:T(8,128)(2,1)}, u32[]{:S(2)}) copy-start(bf16[1024,512]{1,0:T(8,128)(2,1)} %q_ref.7) | copy-start | bytes 3145732
  1.2 1.2 %copy-start.23 = (bf16[1024,512]{1,0:T(8,128)(2,1)S(1)}, bf16[1024,512]{1,0:T(8,128)(2,1)}, u32[]{:S(2)}) copy-start(bf16[1024,512]{1,0:T(8,128)(2,1)} %k_ref.7) | copy-start | bytes 3145732
  2.5 1.2 %copy-start.25 = (bf16[1024,512]{1,0:T(8,128)(2,1)S(1)}, bf16[1024,512]{1,0:T(8,128)(2,1)}, u32[]{:S(2)}) copy-start(bf16[1024,512]{1,0:T(8,128)(2,1)} %v_ref.7) | copy-start | bytes 3145732
  5.5 6.7 %collective-permute-start.3 = (bf16[656,128]{1,0:T(8,128)(2,1)S(1)}, bf16[656,128]{1,0:T(8,128)(2,1)S(1)}, u32[]{:S(2)}, u32[]{:S(2)}) collective-permute-start(bf16[656,128]{1,0:T(8,128)(2,1)S(1)} %get-tuple-element.35), channel_id=1, source_target_pairs={{0,4},{1,5},{2,6},{3,7},{16,20},{17,21},{18,22},{19,23}} | collective-permute-start | bytes 503816 | tf_op jit(solution)/shard_map/ppermute | solution.py:327
  6.2 12.1 %collective-permute-start.1 = (bf16[512,256]{1,0:T(8,128)(2,1)S(1)}, bf16[512,256]{1,0:T(8,128)(2,1)S(1)}, u32[]{:S(2)}, u32[]{:S(2)}) collective-permute-start(bf16[512,256]{1,0:T(8,128)(2,1)S(1)} %get-tuple-element.22), channel_id=1, source_target_pairs={{4,0},{8,4},{12,8},{5,1},{9,5},{13,9},{6,2},{10,6},{14,10},{7,3},{... | collective-permute-start | bytes 786440 | tf_op jit(solution)/shard_map/ppermute | solution.py:278
  9.2 5.0 %copy-start.28 = (bf16[1024,64]{0,1:T(8,128)(2,1)S(1)}, bf16[1024,64]{0,1:T(8,128)(2,1)}, u32[]{:S(2)}) copy-start(bf16[1024,64]{0,1:T(8,128)(2,1)} %param.6) | copy-start | bytes 393220
  9.2 35.0 %collective-permute-start = (bf16[1024,256]{1,0:T(8,128)(2,1)}, bf16[1024,256]{1,0:T(8,128)(2,1)}, u32[]{:S(2)}, u32[]{:S(2)}) collective-permute-start(bf16[1024,256]{1,0:T(8,128)(2,1)} %get-tuple-element.21), channel_id=1, source_target_pairs={{0,4},{4,8},{8,12},{1,5},{5,9},{9,13},{2,6},{6,10},{10,14},{3,7},{... | collective-permute-start | bytes 1572872 | tf_op jit(solution)/shard_map/ppermute | solution.py:278
  12.9 17.6 %collective-permute-start.4 = (bf16[656,128]{1,0:T(8,128)(2,1)S(1)}, bf16[656,128]{1,0:T(8,128)(2,1)S(1)}, u32[]{:S(2)}, u32[]{:S(2)}) collective-permute-start(bf16[656,128]{1,0:T(8,128)(2,1)S(1)} %add.12), channel_id=1, source_target_pairs={{4,8},{5,9},{6,10},{7,11},{20,24},{21,25},{22,26},{23,27}} | collective-permute-start | bytes 503816 | tf_op jit(solution)/shard_map/ppermute | solution.py:327
  14.2 4.2 %copy-start.24 = (bf16[1024,512]{1,0:T(8,128)(2,1)S(1)}, bf16[1024,512]{1,0:T(8,128)(2,1)}, u32[]{:S(2)}) copy-start(bf16[1024,512]{1,0:T(8,128)(2,1)} %k_ref.7) | copy-start | bytes 3145732
  14.2 4.2 %copy-start.26 = (bf16[1024,512]{1,0:T(8,128)(2,1)S(1)}, bf16[1024,512]{1,0:T(8,128)(2,1)}, u32[]{:S(2)}) copy-start(bf16[1024,512]{1,0:T(8,128)(2,1)} %v_ref.7) | copy-start | bytes 3145732
  18.3 1.8 %copy-start.2 = (f32[1024,256]{1,0:T(8,128)}, f32[1024,256]{1,0:T(8,128)S(1)}, u32[]{:S(2)}) copy-start(f32[1024,256]{1,0:T(8,128)S(1)} %get-tuple-element.31.refs_8_) | copy-start | bytes 3145732
  18.3 1.8 %copy-start.4 = (bf16[2,1024,160]{2,1,0:T(8,128)(2,1)}, bf16[2,1024,160]{2,1,0:T(8,128)(2,1)S(1)}, u32[]{:S(2)}) copy-start(bf16[2,1024,160]{2,1,0:T(8,128)(2,1)S(1)} %get-tuple-element.34.refs_11_) | copy-start | bytes 1966084
  18.3 1.8 %copy-start.14 = (f32[512,256]{1,0:T(8,128)}, f32[512,256]{1,0:T(8,128)S(1)}, u32[]{:S(2)}) copy-start(f32[512,256]{1,0:T(8,128)S(1)} %get-tuple-element.32.refs_9_) | copy-start | bytes 1572868
  18.3 1.7 %copy-start.16 = (f32[512,256]{1,0:T(8,128)}, f32[512,256]{1,0:T(8,128)S(1)}, u32[]{:S(2)}) copy-start(f32[512,256]{1,0:T(8,128)S(1)} %get-tuple-element.33.refs_10_) | copy-start | bytes 1572868
  18.3 14.9 %copy-start.1 = (bf16[1024,512]{1,0:T(8,128)(2,1)S(1)}, bf16[1024,512]{1,0:T(8,128)(2,1)}, u32[]{:S(2)}) copy-start(bf16[1024,512]{1,0:T(8,128)(2,1)} %q_ref.7) | copy-start | bytes 3145732
  20.1 24.1 %collective-permute-start.2 = (bf16[544,256]{1,0:T(8,128)(2,1)}, bf16[544,256]{1,0:T(8,128)(2,1)}, u32[]{:S(2)}, u32[]{:S(2)}) collective-permute-start(bf16[544,256]{1,0:T(8,128)(2,1)} %serve.1), channel_id=1, source_target_pairs={{0,4},{4,8},{8,12},{1,5},{5,9},{9,13},{2,6},{6,10},{10,14},{3,7},{... | collective-permute-start | bytes 835592 | tf_op jit(solution)/shard_map/ppermute | solution.py:278
  31.2 11.7 %collective-permute-start.5 = (bf16[656,128]{1,0:T(8,128)(2,1)}, bf16[656,128]{1,0:T(8,128)(2,1)}, u32[]{:S(2)}, u32[]{:S(2)}) collective-permute-start(bf16[656,128]{1,0:T(8,128)(2,1)} %add.14), channel_id=1, source_target_pairs={{8,12},{9,13},{10,14},{11,15},{24,28},{25,29},{26,30},{27,31}} | collective-permute-start | bytes 503816 | tf_op jit(solution)/shard_map/ppermute | solution.py:327
  43.0 1.3 %copy-start.15 = (f32[512,256]{1,0:T(8,128)S(1)}, f32[512,256]{1,0:T(8,128)}, u32[]{:S(2)}) copy-start(f32[512,256]{1,0:T(8,128)} %copy-done.14) | copy-start | bytes 1572868
  44.9 1.2 %copy-start.3 = (f32[1024,256]{1,0:T(8,128)S(1)}, f32[1024,256]{1,0:T(8,128)}, u32[]{:S(2)}) copy-start(f32[1024,256]{1,0:T(8,128)} %copy-done.2) | copy-start | bytes 3145732
  46.1 1.2 %copy-start.5 = (bf16[2,1024,160]{2,1,0:T(8,128)(2,1)S(1)}, bf16[2,1024,160]{2,1,0:T(8,128)(2,1)}, u32[]{:S(2)}) copy-start(bf16[2,1024,160]{2,1,0:T(8,128)(2,1)} %copy-done.4) | copy-start | bytes 1966084
  47.3 1.2 %copy-start.7 = (f32[1024,256]{1,0:T(8,128)S(1)}, f32[1024,256]{1,0:T(8,128)}, u32[]{:S(2)}) copy-start(f32[1024,256]{1,0:T(8,128)} %copy-done.6) | copy-start | bytes 3145732
  48.6 1.2 %copy-start.9 = (f32[1024,256]{1,0:T(8,128)S(1)}, f32[1024,256]{1,0:T(8,128)}, u32[]{:S(2)}) copy-start(f32[1024,256]{1,0:T(8,128)} %copy-done.8) | copy-start | bytes 3145732
  49.8 1.2 %copy-start.11 = (f32[1024,256]{1,0:T(8,128)S(1)}, f32[1024,256]{1,0:T(8,128)}, u32[]{:S(2)}) copy-start(f32[1024,256]{1,0:T(8,128)} %copy-done.10) | copy-start | bytes 3145732
  51.0 1.2 %copy-start.13 = (bf16[2,1024,160]{2,1,0:T(8,128)(2,1)S(1)}, bf16[2,1024,160]{2,1,0:T(8,128)(2,1)}, u32[]{:S(2)}) copy-start(bf16[2,1024,160]{2,1,0:T(8,128)(2,1)} %copy-done.12) | copy-start | bytes 1966084
  (13 other events, 11.8 us)

commit v3 on v2

--- a/solution.py
+++ b/solution.py
@@ -199,15 +199,15 @@
         high = stats.astype(BF).astype(F32)
         middle = (stats - high).astype(BF).astype(F32)
         low = stats - high - middle
-        pad = jnp.zeros((16 - 6 * count, TILE), F32)
+        pad = jnp.ones((16 - 6 * count, TILE), F32)
         rows = jnp.concatenate([high, middle, low, pad], 0)
         line = WINDOW + start // TILE * 16
         out_ref[line : line + 16, :] = rows.astype(BF)
 
 
-def final_kernel(later_ref, q_ref, kv_ref, ob_ref, *refs, heads, width, blocks):
+def final_kernel(q_ref, kv_ref, ob_ref, *refs, heads, width, blocks):
     halves = [refs[:6], refs[6:12]]
-    prior_ref, first_ref, gain_ref, out_ref = refs[12:]
+    *prior_refs, first_ref, gain_ref, out_ref = refs[12:]
     count = heads // 2
     feats = feature_rows(width)
     base = heads * feats
@@ -218,12 +218,17 @@
         cols = wide.T[:feats]
         return jnp.concatenate([state.astype(BF), cols.astype(BF)], 1)
 
+    later = ob_ref[WINDOW + 15 : WINDOW + 16, :1].astype(F32) > 0
+    tail = functools.reduce(jnp.add, [ref[base:, :].astype(F32) for ref in prior_refs])
+    line_of = lax.broadcasted_iota(jnp.int32, (16, HEAD_DIM), 0)
+
     def one(g, part):
         h = g + part * count
+        tails = [jnp.sum(jnp.where(line_of == 2 * h + i, tail, 0.0), 0, keepdims=True) for i in range(2)]
         num_ref, den_ref, win_ref, sum_ref, top_ref, phi_ref = halves[part]
         rows = pl.ds(pl.multiple_of(h * feats, 16), feats)
-        state = prior_ref[rows, :]
-        norm = [prior_ref[pl.ds(base + 2 * h + i, 1), :] for i in range(2)]
+        state = functools.reduce(jnp.add, [ref[rows, :].astype(F32) for ref in prior_refs])
+        norm = [tails[0], tails[1]]
         gain = gain_ref[:, lanes_of(h)]
         for b in range(blocks):
             if b == 1:
@@ -254,7 +259,7 @@
                         top = jnp.sum(jnp.where(lane == g, stats, 0.0), 1, keepdims=True)
                         total = jnp.sum(jnp.where(lane == count + g, stats, 0.0), 1, keepdims=True)
                         out = ob_ref[at, lanes_of(g)].astype(F32)
-                    top = jnp.where(later_ref[0] > 0, top, 2 * NEG)
+                    top = jnp.where(later, top, 2 * NEG)
                     mine = top_ref[at, lanes_of(g)]
                     most = jnp.maximum(mine, top)
                     here = jnp.exp2((mine - most) * SCALE)
@@ -306,7 +311,7 @@
         compiler_params=grant,
         cost_estimate=pl.CostEstimate(flops=1 << 30, bytes_accessed=3 << 20, transcendentals=0),
         name="prepare",
-    )(kft, swa_query, swa_key, values)
+    )(kft, *[pltpu.with_memory_space_constraint(a, pltpu.HBM) for a in (swa_query, swa_key, values)])
 
     def local(start_head):
         wide = jax.ShapeDtypeStruct((tokens, half * HEAD_DIM), F32)
@@ -322,22 +327,22 @@
         )(swa_query, swa_key, values, qft, kft)
 
     if count <= 4:
-        running, prior = own, None
+        running, prior = own, []
         for i in range(count - 1):
             got = lax.ppermute(running, "seq", [(i, i + 1)])
-            prior = got.astype(F32) if prior is None else prior + got.astype(F32)
+            prior.append(got)
             running = own + got
             if i == 0:
                 halo = shifted(kv, "seq", 1)
                 asked = shifted(qb, "seq", -1)
     else:
-        running, prior, distance = own, None, 1
+        running, prior, distance = own, [], 1
         halo = shifted(kv, "seq", 1)
         asked = shifted(qb, "seq", -1)
         while distance < count:
-            got = shifted(running.astype(BF), "seq", distance).astype(F32)
-            prior = got if prior is None else prior + got
-            running = running.astype(F32) + got
+            got = shifted(running, "seq", distance)
+            prior.append(got)
+            running = running + got
             distance *= 2
 
     local_a = local(0)
@@ -353,16 +358,15 @@
     answered = shifted(answer, "seq", 1)
     local_b = local(half)
 
-    later = (lax.axis_index("seq") > 0).astype(jnp.int32).reshape(1)
     return pl.pallas_call(
         functools.partial(final_kernel, heads=heads, width=width, blocks=blocks),
         out_shape=jax.ShapeDtypeStruct((tokens, columns), BF),
-        in_specs=[pl.BlockSpec(memory_space=pltpu.SMEM)] + [vmem] * 18,
+        in_specs=[vmem] * (17 + len(prior)),
         out_specs=vmem,
         compiler_params=grant,
         cost_estimate=pl.CostEstimate(flops=2 << 30, bytes_accessed=12 << 20, transcendentals=1 << 20),
         name="final",
-    )(later, swa_query, halo, answered, *local_a, *local_b, prior, first, gain.reshape(1, columns))
+    )(swa_query, halo, answered, *local_a, *local_b, *prior, first, gain.reshape(1, columns))
 
 
 def solution(mesh):

time: 61.5 us -> 39.3 us (0.64)
  the two profiles are of different devices: /device:TPU:22 before, /device:TPU:16 now
where the time goes in v3:
time: 39.3 us; the launch traced here: 39.1 us
  Pallas kernels  16.4 us (42%)
  starting transfers between devices  11.2 us (28%)
  waiting for transfers between devices  9.68 us (25%)
  local copies, waits for them, and re-layouts  1.6 us (4%)
    ppermute x3, waiting for transfers between devices, body(): got = lax.ppermute(running, 'seq', [(i, i + 1)])  9.67 us
    pallas_call x2, Pallas kernels, local(): pl.pallas_call(functools.partial(local_kernel, start_head=start_head, wid...  8.21 us
    ppermute x3, starting transfers between devices, shifted(): return lax.ppermute(value, axis, pairs)  7.9 us
    pallas_call x1, Pallas kernels, body(): pl.pallas_call(functools.partial(final_kernel, heads=heads, width=width,...  4.99 us
    ppermute x3, starting transfers between devices, body(): got = lax.ppermute(running, 'seq', [(i, i + 1)])  3.26 us
    pallas_call x1, Pallas kernels, body(): pl.pallas_call(functools.partial(prepare_kernel, heads=heads, width=width...  2.19 us
    unnamed x12, local copies, waits for them, and re-layouts  1.6 us
    pallas_call x1, Pallas kernels, body(): pl.pallas_call(functools.partial(serve_kernel, behind=half), out_shape=ja...  0.97 us
  transfers between devices with their start and end apart: 6, of which 1 were waited for; matrix products, arithmetic and copies ran while one was open for 0% of the time, Pallas kernels for 23%

profile of v3, /device:TPU:16, one launch (start us, length us, event | category | flops | bytes accessed | tf_op | source)
XLA Modules:
  0.0 39.1 jit_solution(10235371590331099343)
XLA Ops:
  0.0 0.9 %copy-done.4 = bf16[1024,64]{0,1:T(8,128)(2,1)S(1)} copy-done((bf16[1024,64]{0,1:T(8,128)(2,1)S(1)}, bf16[1024,64]{0,1:T(8,128)(2,1)}, u32[]{:S(2)}) %copy-start.4) | copy-done | bytes 131096
  0.9 2.2 %prepare.1 = (bf16[1024,256]{1,0:T(8,128)(2,1)S(1)}, bf16[512,256]{1,0:T(8,128)(2,1)S(1)}, bf16[656,128]{1,0:T(8,128)(2,1)S(1)}, f32[656,128]{1,0:T(8,128)S(1)}) custom-call(bf16[64,1024]{1,0:T(8,128)(2,1)S(1)} %bitcast.4, bf16[1024,512]{1,0:T(8,128)(2,1)} %q_ref.7, bf16[1024,512]{1,0:T(8,128)(2,1)} %k_ref.7, bf16[1024,512]{1,0:T(8,128)(2,1)} %v_ref.7), custom_call_target="tpu_custom_call" | custom-call | flops 1073741824 | bytes 3145728 | tf_op jit(solution)/shard_map/prepare/pallas_call | solution.py:300
  3.1 0.7 %collective-permute-start.3 = (bf16[656,128]{1,0:T(8,128)(2,1)S(1)}, bf16[656,128]{1,0:T(8,128)(2,1)S(1)}, u32[]{:S(2)}, u32[]{:S(2)}) collective-permute-start(bf16[656,128]{1,0:T(8,128)(2,1)S(1)} %get-tuple-element.35), channel_id=1, source_target_pairs={{0,4},{1,5},{2,6},{3,7},{16,20},{17,21},{18,22},{19,23}} | collective-permute-start | bytes 503816 | tf_op jit(solution)/shard_map/ppermute | solution.py:332
  3.8 3.0 %collective-permute-start.1 = (bf16[512,256]{1,0:T(8,128)(2,1)S(1)}, bf16[512,256]{1,0:T(8,128)(2,1)S(1)}, u32[]{:S(2)}, u32[]{:S(2)}) collective-permute-start(bf16[512,256]{1,0:T(8,128)(2,1)S(1)} %get-tuple-element.22), channel_id=1, source_target_pairs={{4,0},{8,4},{12,8},{5,1},{9,5},{13,9},{6,2},{10,6},{14,10},{7,3},{... | collective-permute-start | bytes 786440 | tf_op jit(solution)/shard_map/ppermute | solution.py:283
  6.8 0.0 copy-start.5
  6.8 3.0 %collective-permute-start = (bf16[1024,256]{1,0:T(8,128)(2,1)S(1)}, bf16[1024,256]{1,0:T(8,128)(2,1)S(1)}, u32[]{:S(2)}, u32[]{:S(2)}) collective-permute-start(bf16[1024,256]{1,0:T(8,128)(2,1)S(1)} %get-tuple-element.21), channel_id=1, source_target_pairs={{0,4},{4,8},{8,12},{1,5},{5,9},{9,13},{2,6},{6,10},{10,14},{3,7},{... | collective-permute-start | bytes 1572872 | tf_op jit(solution)/shard_map/ppermute | solution.py:283
  9.8 0.0 collective-permute-done.3.refs_12_
  9.9 1.3 %collective-permute-start.4 = (bf16[656,128]{1,0:T(8,128)(2,1)S(1)}, bf16[656,128]{1,0:T(8,128)(2,1)S(1)}, u32[]{:S(2)}, u32[]{:S(2)}) collective-permute-start(bf16[656,128]{1,0:T(8,128)(2,1)S(1)} %add.6), channel_id=1, source_target_pairs={{4,8},{5,9},{6,10},{7,11},{20,24},{21,25},{22,26},{23,27}} | collective-permute-start | bytes 503816 | tf_op jit(solution)/shard_map/ppermute | solution.py:332
  11.2 0.0 copy-done
  11.2 0.0 copy-done.2
  11.2 0.0 copy-done.3
  11.2 4.1 %local.3 = (f32[1024,256]{1,0:T(8,128)S(1)}, f32[1024,256]{1,0:T(8,128)S(1)}, f32[1024,256]{1,0:T(8,128)S(1)}, f32[512,256]{1,0:T(8,128)S(1)}, f32[512,256]{1,0:...) custom-call(bf16[1024,512]{1,0:T(8,128)(2,1)S(1)} %copy-done, bf16[1024,512]{1,0:T(8,128)(2,1)S(1)} %copy-done.2, ...), custom_call_target="tpu_custom_call" | custom-call | flops 4294967296 | bytes 6291456 | tf_op jit(solution)/shard_map/local/pallas_call | solution.py:319
  15.3 0.0 collective-permute-done.1.qb_ref
  15.3 1.0 %serve.1 = bf16[544,256]{1,0:T(8,128)(2,1)S(1)} custom-call(bf16[512,256]{1,0:T(8,128)(2,1)S(1)} %collective-permute-done.1.qb_ref, bf16[1024,512]{1,0:T(8,128)(2,1)S(1)} %copy-done.2, bf16[1024,512]{1,0:T(8,128)(2,1)S(1)} %copy-done.3), custom_call_target="tpu_custom_call" | custom-call | flops 1073741824 | bytes 2097152 | tf_op jit(solution)/shard_map/serve/pallas_call | solution.py:349
  16.3 1.9 %collective-permute-start.2 = (bf16[544,256]{1,0:T(8,128)(2,1)S(1)}, bf16[544,256]{1,0:T(8,128)(2,1)S(1)}, u32[]{:S(2)}, u32[]{:S(2)}) collective-permute-start(bf16[544,256]{1,0:T(8,128)(2,1)S(1)} %serve.1), channel_id=1, source_target_pairs={{0,4},{4,8},{8,12},{1,5},{5,9},{9,13},{2,6},{6,10},{10,14},{3,7},{... | collective-permute-start | bytes 835592 | tf_op jit(solution)/shard_map/ppermute | solution.py:283
  18.2 9.7 %collective-permute-done.4.refs_13_ = bf16[656,128]{1,0:T(8,128)(2,1)S(1)} collective-permute-done((bf16[656,128]{1,0:T(8,128)(2,1)S(1)}, bf16[656,128]{1,0:T(8,128)(2,1)S(1)}, u32[]{:S(2)}, u32[]{:S(2)}) %collective-permute-start.4) | collective-permute-done | bytes 167968 | tf_op jit(solution)/shard_map/ppermute | solution.py:332
  28.0 1.3 %collective-permute-start.5 = (bf16[656,128]{1,0:T(8,128)(2,1)S(1)}, bf16[656,128]{1,0:T(8,128)(2,1)S(1)}, u32[]{:S(2)}, u32[]{:S(2)}) collective-permute-start(bf16[656,128]{1,0:T(8,128)(2,1)S(1)} %add.7), channel_id=1, source_target_pairs={{8,12},{9,13},{10,14},{11,15},{24,28},{25,29},{26,30},{27,31}} | collective-permute-start | bytes 503816 | tf_op jit(solution)/shard_map/ppermute | solution.py:332
  29.3 4.1 %local.2 = (f32[1024,256]{1,0:T(8,128)S(1)}, f32[1024,256]{1,0:T(8,128)S(1)}, f32[1024,256]{1,0:T(8,128)S(1)}, f32[512,256]{1,0:T(8,128)S(1)}, f32[512,256]{1,0:...) custom-call(bf16[1024,512]{1,0:T(8,128)(2,1)S(1)} %copy-done, bf16[1024,512]{1,0:T(8,128)(2,1)S(1)} %copy-done.2, ...), custom_call_target="tpu_custom_call" | custom-call | flops 4294967296 | bytes 6291456 | tf_op jit(solution)/shard_map/local/pallas_call | solution.py:319
  33.4 0.0 collective-permute-done.5.refs_14_
  33.4 0.0 collective-permute-done.kv_ref
  33.4 0.0 collective-permute-done.2.ob_ref
  33.4 0.0 copy-start.1
  33.4 0.7 %copy-done.1 = f32[512]{0:T(512)S(1)} copy-done((f32[512]{0:T(512)S(1)}, f32[512]{0:T(512)}, u32[]{:S(2)}) %copy-start.1) | copy-done | bytes 2072
  34.1 5.0 %final.1 = bf16[1024,512]{1,0:T(8,128)(2,1)} custom-call(bf16[1024,512]{1,0:T(8,128)(2,1)S(1)} %copy-done, bf16[1024,256]{1,0:T(8,128)(2,1)S(1)} %collective-permute-done.kv_ref, bf16[544,256]{1,0:T(8,128)(2,1)S(1)} %collective-permute-done.2.ob_ref, f32[1024,256]{1,0:T(8,128)S(1)} %get-tuple-element.23.refs_0_, f32[1024,256]{1,0:T(8,128)S(1)} %get-tuple-element.24.refs_1_, ...), custom_call_target="tpu_custom_call" | custom-call | flops 2147483648 | bytes 12582912 | tf_op jit(solution)/shard_map/final/pallas_call | solution.py:361
  (7 shorter events, 0.1 us)
Async XLA Ops:
  0.0 0.9 %copy-start.4 = (bf16[1024,64]{0,1:T(8,128)(2,1)S(1)}, bf16[1024,64]{0,1:T(8,128)(2,1)}, u32[]{:S(2)}) copy-start(bf16[1024,64]{0,1:T(8,128)(2,1)} %param.7) | copy-start | bytes 393220
  0.9 10.3 %copy-start = (bf16[1024,512]{1,0:T(8,128)(2,1)S(1)}, bf16[1024,512]{1,0:T(8,128)(2,1)}, u32[]{:S(2)}) copy-start(bf16[1024,512]{1,0:T(8,128)(2,1)} %q_ref.7) | copy-start | bytes 3145732
  0.9 10.3 %copy-start.2 = (bf16[1024,512]{1,0:T(8,128)(2,1)S(1)}, bf16[1024,512]{1,0:T(8,128)(2,1)}, u32[]{:S(2)}) copy-start(bf16[1024,512]{1,0:T(8,128)(2,1)} %k_ref.7) | copy-start | bytes 3145732
  0.9 10.3 %copy-start.3 = (bf16[1024,512]{1,0:T(8,128)(2,1)S(1)}, bf16[1024,512]{1,0:T(8,128)(2,1)}, u32[]{:S(2)}) copy-start(bf16[1024,512]{1,0:T(8,128)(2,1)} %v_ref.7) | copy-start | bytes 3145732
  3.1 6.7 %collective-permute-start.3 = (bf16[656,128]{1,0:T(8,128)(2,1)S(1)}, bf16[656,128]{1,0:T(8,128)(2,1)S(1)}, u32[]{:S(2)}, u32[]{:S(2)}) collective-permute-start(bf16[656,128]{1,0:T(8,128)(2,1)S(1)} %get-tuple-element.35), channel_id=1, source_target_pairs={{0,4},{1,5},{2,6},{3,7},{16,20},{17,21},{18,22},{19,23}} | collective-permute-start | bytes 503816 | tf_op jit(solution)/shard_map/ppermute | solution.py:332
  3.8 11.5 %collective-permute-start.1 = (bf16[512,256]{1,0:T(8,128)(2,1)S(1)}, bf16[512,256]{1,0:T(8,128)(2,1)S(1)}, u32[]{:S(2)}, u32[]{:S(2)}) collective-permute-start(bf16[512,256]{1,0:T(8,128)(2,1)S(1)} %get-tuple-element.22), channel_id=1, source_target_pairs={{4,0},{8,4},{12,8},{5,1},{9,5},{13,9},{6,2},{10,6},{14,10},{7,3},{... | collective-permute-start | bytes 786440 | tf_op jit(solution)/shard_map/ppermute | solution.py:283
  6.8 4.4 %copy-start.5 = (bf16[1024,64]{0,1:T(8,128)(2,1)S(1)}, bf16[1024,64]{0,1:T(8,128)(2,1)}, u32[]{:S(2)}) copy-start(bf16[1024,64]{0,1:T(8,128)(2,1)} %param.6) | copy-start | bytes 393220
  6.8 26.6 %collective-permute-start = (bf16[1024,256]{1,0:T(8,128)(2,1)S(1)}, bf16[1024,256]{1,0:T(8,128)(2,1)S(1)}, u32[]{:S(2)}, u32[]{:S(2)}) collective-permute-start(bf16[1024,256]{1,0:T(8,128)(2,1)S(1)} %get-tuple-element.21), channel_id=1, source_target_pairs={{0,4},{4,8},{8,12},{1,5},{5,9},{9,13},{2,6},{6,10},{10,14},{3,7},{... | collective-permute-start | bytes 1572872 | tf_op jit(solution)/shard_map/ppermute | solution.py:283
  9.9 18.0 %collective-permute-start.4 = (bf16[656,128]{1,0:T(8,128)(2,1)S(1)}, bf16[656,128]{1,0:T(8,128)(2,1)S(1)}, u32[]{:S(2)}, u32[]{:S(2)}) collective-permute-start(bf16[656,128]{1,0:T(8,128)(2,1)S(1)} %add.6), channel_id=1, source_target_pairs={{4,8},{5,9},{6,10},{7,11},{20,24},{21,25},{22,26},{23,27}} | collective-permute-start | bytes 503816 | tf_op jit(solution)/shard_map/ppermute | solution.py:332
  16.3 17.1 %collective-permute-start.2 = (bf16[544,256]{1,0:T(8,128)(2,1)S(1)}, bf16[544,256]{1,0:T(8,128)(2,1)S(1)}, u32[]{:S(2)}, u32[]{:S(2)}) collective-permute-start(bf16[544,256]{1,0:T(8,128)(2,1)S(1)} %serve.1), channel_id=1, source_target_pairs={{0,4},{4,8},{8,12},{1,5},{5,9},{9,13},{2,6},{6,10},{10,14},{3,7},{... | collective-permute-start | bytes 835592 | tf_op jit(solution)/shard_map/ppermute | solution.py:283
  28.0 5.4 %collective-permute-start.5 = (bf16[656,128]{1,0:T(8,128)(2,1)S(1)}, bf16[656,128]{1,0:T(8,128)(2,1)S(1)}, u32[]{:S(2)}, u32[]{:S(2)}) collective-permute-start(bf16[656,128]{1,0:T(8,128)(2,1)S(1)} %add.7), channel_id=1, source_target_pairs={{8,12},{9,13},{10,14},{11,15},{24,28},{25,29},{26,30},{27,31}} | collective-permute-start | bytes 503816 | tf_op jit(solution)/shard_map/ppermute | solution.py:332
  33.4 0.7 %copy-start.1 = (f32[512]{0:T(512)S(1)}, f32[512]{0:T(512)}, u32[]{:S(2)}) copy-start(f32[512]{0:T(512)} %param.11) | copy-start | bytes 6148

commit v4 on v3

v4 whole, which is shorter than its diff:
```python
import functools

import jax
import jax.numpy as jnp
from jax import lax
from jax.experimental import pallas as pl
from jax.experimental.pallas import tpu as pltpu
from jax.sharding import PartitionSpec as P

HEAD_DIM = 128
WINDOW = 512
TILE = 256
NEG = -1e30
SCALE = HEAD_DIM ** (-0.5) * 1.4426950408889634
BF = jnp.bfloat16
F32 = jnp.float32
GRANT = 16 << 20
LA = 1 << 30
LB = 4 << 30
SV = 1 << 30
PR = 1 << 30
RL = 1 << 17


def feature_rows(width):
    return -(-(width * (width + 1) // 2 + width + 1) // 16) * 16


def state_rows(heads, width):
    return heads * feature_rows(width) + 16


def nt(a, b):
    return lax.dot_general(a, b, (((1,), (1,)), ((), ())), preferred_element_type=F32)


def nn(a, b):
    return jnp.dot(a, b, preferred_element_type=F32)


def phi_rows(x, query):
    width, tokens = x.shape
    half = width // 2
    scale = 0.5**0.5 * width ** (-0.5)
    twice = jnp.concatenate([x, x], 0)
    rows = []
    for d in range(half):
        prod = ((x * twice[d : d + width]) * scale).astype(BF)
        if query and d:
            prod = prod * 2
        rows.append(prod)
    rows.append((x * width ** (-0.25)).astype(BF))
    cross = (x[:half] * x[half:]) * scale
    if query:
        cross = cross * 2
    pad = feature_rows(width) - (half * width + width + half)
    last = lax.broadcasted_iota(jnp.int32, (pad, tokens), 0)
    const = jnp.where(last == 0, 1.0, 0.0)
    rows.append(jnp.concatenate([cross, const], 0).astype(BF))
    return jnp.concatenate(rows, 0)


def with_ones(v):
    return jnp.concatenate([v, jnp.ones_like(v)], 1)


def lanes_of(h, count=1):
    return pl.ds(pl.multiple_of(h * HEAD_DIM, HEAD_DIM), count * HEAD_DIM)


def causal_masks():
    row = lax.broadcasted_iota(jnp.int32, (TILE, TILE), 0)
    col = lax.broadcasted_iota(jnp.int32, (TILE, TILE), 1)
    return col <= row, col > row


def prepare_kernel(kf_hbm, q_hbm, k_hbm, v_hbm, kp_ref, vp_ref, qb_ref, own_ref, before_ref, kf_ref, v_ref, sems, *, heads, width):
    feats = feature_rows(width)
    base = heads * feats
    tokens = v_ref.shape[0]
    ahead = heads // 2 * HEAD_DIM
    tail = pl.ds(tokens - WINDOW, WINDOW)
    copies = [
        pltpu.make_async_copy(kf_hbm, kf_ref, sems.at[0]),
        pltpu.make_async_copy(v_hbm, v_ref, sems.at[1]),
        pltpu.make_async_copy(k_hbm.at[tail, :ahead], kp_ref, sems.at[2]),
        pltpu.make_async_copy(v_hbm.at[tail, :ahead], vp_ref, sems.at[3]),
        pltpu.make_async_copy(q_hbm.at[:WINDOW, ahead:], qb_ref, sems.at[4]),
    ]
    for copy in copies:
        copy.start()
    ones = jnp.ones((16, tokens), BF)
    own_ref[base:, :] = jnp.zeros((16, HEAD_DIM), BF)
    copies[0].wait()
    copies[1].wait()
    for h in range(heads):
        phi = phi_rows(kf_ref[h * width : (h + 1) * width, :].astype(F32), False)
        total = None
        for t in range(tokens // TILE):
            at = slice(t * TILE, (t + 1) * TILE)
            s = nn(phi[:, at], with_ones(v_ref[at, h * HEAD_DIM : (h + 1) * HEAD_DIM]))
            total = s if t == 0 else total + s
            if t < tokens // TILE - 1:
                before_ref[t, h * feats : (h + 1) * feats, :] = total
        norm = nt(ones, phi)
        own_ref[h * feats : (h + 1) * feats, :] = total[:, :HEAD_DIM].astype(BF)
        own_ref[base + 2 * h : base + 2 * h + 1, :] = norm[:1, :HEAD_DIM].astype(BF)
        own_ref[base + 2 * h + 1 : base + 2 * h + 2, : feats - HEAD_DIM] = norm[:1, HEAD_DIM:].astype(BF)
    for copy in copies[2:]:
        copy.wait()
    top = kp_ref[:16, :]
    row = lax.broadcasted_iota(jnp.int32, top.shape, 0)
    kp_ref[:16, :] = jnp.where(row == 0, jnp.ones((), BF), top)


def softmax_parts(jobs, ahead=2):
    scores = []
    for i in range(len(jobs)):
        while len(scores) < min(len(jobs), i + 1 + ahead):
            query, key = jobs[len(scores)][:2]
            scores.append(nt(query(), key()))
        _, _, value, first, last, use = jobs[i]
        s, scores[i] = scores[i], None
        parts = [s[:, at : at + TILE] for at in range(0, s.shape[1], TILE)]
        if first is not None:
            parts[0] = jnp.where(first, parts[0], NEG)
        if last is not None:
            parts[-1] = jnp.where(last, parts[-1], NEG)
        top = jnp.max(functools.reduce(jnp.maximum, parts), 1, keepdims=True)
        p = jnp.concatenate([jnp.exp2((part - top) * SCALE).astype(BF) for part in parts], 1)
        acc = nn(p, with_ones(value()))
        use(top, acc[:, :HEAD_DIM], acc[:, HEAD_DIM:])


def local_kernel(q_ref, k_ref, v_ref, qf_ref, kf_ref, num_ref, den_ref, win_ref, sum_ref, top_ref, phi_ref, *, start_head, width):
    causal, beyond = causal_masks()
    tokens = q_ref.shape[0]
    feats = feature_rows(width)

    jobs = []

    def job(g, start):
        h = g + start_head
        at = slice(start, start + TILE)
        keys = slice(max(0, start - WINDOW), start + TILE)
        lanes = slice(g * HEAD_DIM, (g + 1) * HEAD_DIM)
        wide = slice(h * HEAD_DIM, (h + 1) * HEAD_DIM)

        def use(top, out, total):
            if start >= WINDOW:
                win_ref[at, lanes] = out / total
            else:
                win_ref[at, lanes] = out
                sum_ref[at, lanes] = total
                top_ref[at, lanes] = jnp.broadcast_to(top, (TILE, HEAD_DIM))
            r = nn(phi_ref[g, at, HEAD_DIM:], kfs[g][:, at])
            part = width ** (-0.25)
            t = jnp.where(causal, (r * (0.5 * part * part) + part) * r + 1.0, 0.0)
            both = nn(t.astype(BF), with_ones(v_ref[at, wide]))
            num_ref[at, lanes] = both[:, :HEAD_DIM]
            den_ref[at, lanes] = both[:, HEAD_DIM:]

        first = beyond if start >= WINDOW else None
        jobs.append((lambda: q_ref[at, wide], lambda: k_ref[keys, wide], lambda: v_ref[keys, wide], first, causal, use))

    kfs = []
    for g in range(num_ref.shape[1] // HEAD_DIM):
        h = g + start_head
        rows = slice(h * width, (h + 1) * width)
        phi_ref[g] = phi_rows(qf_ref[rows, :].astype(F32), True).astype(F32).T.astype(BF)
        kfs.append(jnp.concatenate([kf_ref[rows, :], jnp.zeros((feats - HEAD_DIM - width, tokens), BF)], 0))
        for start in range(0, tokens, TILE):
            job(g, start)
    softmax_parts(jobs)


def serve_kernel(qb_ref, k_ref, v_ref, out_ref, *, behind):
    _, beyond = causal_masks()
    base = k_ref.shape[0] - WINDOW
    count = qb_ref.shape[1] // HEAD_DIM
    lane = lax.broadcasted_iota(jnp.int32, (TILE, HEAD_DIM), 1)
    jobs = []
    stats = [jnp.zeros((TILE, HEAD_DIM), F32) for _ in range(WINDOW // TILE)]

    def job(start, g):
        at = slice(start, start + TILE)
        keys = slice(base + start, base + WINDOW)
        lanes = slice(g * HEAD_DIM, (g + 1) * HEAD_DIM)
        wide = slice((behind + g) * HEAD_DIM, (behind + g + 1) * HEAD_DIM)

        def use(top, out, total):
            out_ref[at, lanes] = out.astype(BF)
            stat = jnp.where(lane == g, top, stats[start // TILE])
            stats[start // TILE] = jnp.where(lane == count + g, total, stat)

        jobs.append((lambda: qb_ref[at, lanes], lambda: k_ref[keys, wide], lambda: v_ref[keys, wide], beyond, None, use))

    for start in range(0, WINDOW, TILE):
        for g in range(count):
            job(start, g)
    softmax_parts(jobs)
    for i, stat in enumerate(stats):
        stat = stat.T[: 2 * count]
        high = stat.astype(BF).astype(F32)
        middle = (stat - high).astype(BF).astype(F32)
        low = stat - high - middle
        pad = jnp.ones((16 - 6 * count, TILE), F32)
        rows = jnp.concatenate([high, middle, low, pad], 0)
        out_ref[WINDOW + 16 * i : WINDOW + 16 * (i + 1), :] = rows.astype(BF)


def merged(window, mine, total, top, out, count, later):
    top = jnp.where(later, top, 2 * NEG)
    most = jnp.maximum(mine, top)
    here = jnp.exp2((mine - most) * SCALE)
    there = jnp.exp2((top - most) * SCALE)
    return (window * here + out * there) / (total * here + count * there)


def normed(mixed, gain):
    power = jnp.mean(mixed * mixed, 1, keepdims=True)
    return (mixed * lax.rsqrt(power + 1e-05) * gain).astype(BF)


def first_final_kernel(q_ref, kp_ref, vp_ref, *refs, heads, width):
    halves = [refs[:6], refs[6:10]]
    *prior_refs, before_ref, gain_hbm, out_hbm, lin_ref, gain_b_ref, gain_ref, near_ref, out_ref, sems = refs[10:]
    count = heads // 2
    tokens = q_ref.shape[0]
    feats = feature_rows(width)
    base = heads * feats
    fetch = pltpu.make_async_copy(gain_hbm, gain_ref, sems.at[heads])
    fetch.start()
    _, beyond = causal_masks()
    later = kp_ref[:1, :1].astype(F32) > 0
    jobs = []

    def job(g, start):
        at = slice(start, start + TILE)
        keys = slice(start, WINDOW)
        cols = slice(g * HEAD_DIM, (g + 1) * HEAD_DIM)
        win_ref, _, sum_ref, top_ref = halves[0][2:]

        def use(top, out, total):
            near_ref[at, cols] = merged(win_ref[at, cols], top_ref[at, cols], sum_ref[at, cols], top, out, total, later)

        jobs.append((lambda: q_ref[at, cols], lambda: kp_ref[keys, cols], lambda: vp_ref[keys, cols], beyond, None, use))

    for g in range(count):
        for start in range(0, WINDOW, TILE):
            job(g, start)

    def prior(rows):
        return functools.reduce(jnp.add, [ref[rows, :].astype(F32) for ref in prior_refs])

    tail = jnp.concatenate([prior(slice(base, base + 16)), jnp.zeros((HEAD_DIM - 16, HEAD_DIM), F32)], 0).T

    def state(h):
        norm = [
            jnp.broadcast_to(tail[:, 2 * h : 2 * h + 1], (HEAD_DIM, HEAD_DIM)),
            jnp.broadcast_to(tail[: feats - HEAD_DIM, 2 * h + 1 : 2 * h + 2], (feats - HEAD_DIM, HEAD_DIM)),
        ]
        return jnp.concatenate([prior(slice(h * feats, (h + 1) * feats)), jnp.concatenate(norm, 0)], 1)

    softmax_parts(jobs)
    order = [(h, start) for h in list(range(count, heads)) + list(range(count)) for start in range(0, tokens, TILE)]
    states, lins, copies = {}, [], []
    for i, (h, start) in enumerate(order):
        while len(lins) < min(len(order), i + 2):
            hn, sn = order[len(lins)]
            rows = slice(hn * feats, (hn + 1) * feats)
            if hn not in states:
                states[hn] = state(hn)
            both = states[hn] if sn == 0 else states[hn] + before_ref[sn // TILE - 1, rows, :]
            lins.append(nn(halves[hn // count][3][hn % count, sn : sn + TILE, :], both.astype(BF)))
        lin, lins[i] = lins[i], None
        part, g = h // count, h % count
        num_ref, den_ref, win_ref = halves[part][:3]
        at = slice(start, start + TILE)
        cols = slice(g * HEAD_DIM, (g + 1) * HEAD_DIM)
        wide = slice(h * HEAD_DIM, (h + 1) * HEAD_DIM)
        mixed = (num_ref[at, cols] + lin[:, :HEAD_DIM]) / (den_ref[at, cols] + lin[:, HEAD_DIM:])
        if start < WINDOW and part == 1:
            lin_ref[at, cols] = mixed
        else:
            if not copies and start == WINDOW:
                fetch.wait()
                gain_b_ref[...] = gain_ref[:, count * HEAD_DIM :]
            window = near_ref[at, cols] if start < WINDOW else win_ref[at, cols]
            out_ref[at, wide] = normed(mixed + window, gain_ref[:, wide])
        if start + TILE == tokens:
            area = (pl.ds(WINDOW * part, tokens - WINDOW * part), pl.ds(h * HEAD_DIM, HEAD_DIM))
            copies.append(pltpu.make_async_copy(out_ref.at[area], out_hbm.at[area], sems.at[h]))
            copies[-1].start()
    for copy in copies:
        copy.wait()


def last_final_kernel(ob_ref, lin_ref, win_ref, sum_ref, top_ref, gain_ref, _, out_hbm, out_ref, sems):
    count = lin_ref.shape[1] // HEAD_DIM
    ahead = out_hbm.shape[1] - count * HEAD_DIM
    later = ob_ref[WINDOW + 15 : WINDOW + 16, :1].astype(F32) > 0
    copies = []
    stats = []
    for i in range(WINDOW // TILE):
        got = ob_ref[WINDOW + 16 * i : WINDOW + 16 * (i + 1), :].astype(F32)
        n = 2 * count
        got = got[:n] + got[n : 2 * n] + got[2 * n : 3 * n]
        stats.append(jnp.concatenate([got, jnp.zeros((HEAD_DIM - n, TILE), F32)], 0).T)
    for start in range(0, WINDOW, TILE):
        at = slice(start, start + TILE)
        stat = stats[start // TILE]
        for g in range(count):
            cols = slice(g * HEAD_DIM, (g + 1) * HEAD_DIM)
            out = ob_ref[at, cols].astype(F32)
            window = merged(win_ref[at, cols], top_ref[at, cols], sum_ref[at, cols], stat[:, g : g + 1], out, stat[:, count + g : count + g + 1], later)
            out_ref[at, cols] = normed(lin_ref[at, cols] + window, gain_ref[:, cols])
        copy = pltpu.make_async_copy(out_ref.at[at, :], out_hbm.at[at, ahead:], sems.at[start // TILE])
        copy.start()
        copies.append(copy)
    for copy in copies:
        copy.wait()


def relay_kernel(own_ref, got_ref, _, sum_ref, pass_ref):
    sum_ref[...] = own_ref[...] + got_ref[...]


def shifted(value, axis, steps):
    count = lax.axis_size(axis)
    pairs = [(i, i + steps) for i in range(count) if 0 <= i + steps < count]
    return lax.ppermute(value, axis, pairs)


def body(q_feat, k_feat, swa_query, swa_key, values, gain):
    tokens, columns = swa_query.shape
    heads = columns // HEAD_DIM
    half = heads // 2
    width = q_feat.shape[1] // heads
    feats = feature_rows(width)
    rows = state_rows(heads, width)
    count = lax.axis_size("seq")
    vmem = pl.BlockSpec(memory_space=pltpu.VMEM)
    hbm = pl.BlockSpec(memory_space=pltpu.HBM)
    grant = pltpu.CompilerParams(vmem_limit_bytes=GRANT)
    qft, kft = q_feat.T, k_feat.T

    in_hbm = lambda *arrays: [pltpu.with_memory_space_constraint(a, pltpu.HBM) for a in arrays]
    kp, vp, qb, own, before = pl.pallas_call(
        functools.partial(prepare_kernel, heads=heads, width=width),
        out_shape=(
            jax.ShapeDtypeStruct((WINDOW, half * HEAD_DIM), BF),
            jax.ShapeDtypeStruct((WINDOW, half * HEAD_DIM), BF),
            jax.ShapeDtypeStruct((WINDOW, half * HEAD_DIM), BF),
            jax.ShapeDtypeStruct((rows, HEAD_DIM), BF),
            jax.ShapeDtypeStruct((tokens // TILE - 1, heads * feats, 2 * HEAD_DIM), F32),
        ),
        in_specs=[hbm] * 4,
        out_specs=(vmem,) * 5,
        scratch_shapes=[
            pltpu.VMEM(kft.shape, BF),
            pltpu.VMEM((tokens, columns), BF),
            pltpu.SemaphoreType.DMA((5,)),
        ],
        compiler_params=grant,
        cost_estimate=pl.CostEstimate(flops=1 << 30, bytes_accessed=3 << 20, transcendentals=0),
        name="prepare",
    )(*in_hbm(kft, swa_query, swa_key, values))

    def local(start_head, flops):
        wide = jax.ShapeDtypeStruct((tokens, half * HEAD_DIM), F32)
        near = jax.ShapeDtypeStruct((WINDOW, half * HEAD_DIM), F32)
        return pl.pallas_call(
            functools.partial(local_kernel, start_head=start_head, width=width),
            out_shape=(wide, wide, wide, near, near, jax.ShapeDtypeStruct((half, tokens, feats), BF)),
            in_specs=[vmem] * 5,
            out_specs=(vmem,) * 6,
            compiler_params=grant,
            cost_estimate=pl.CostEstimate(flops=flops, bytes_accessed=1 << 20, transcendentals=1 << 10),
            name="local",
        )(swa_query, swa_key, values, qft, kft)

    if count <= 4:
        running, prior = own, []
        for i in range(count - 1):
            got = lax.ppermute(running, "seq", [(i, i + 1)])
            prior.append(got)
            running = own + got
            if i == 0:
                asked = shifted(qb, "seq", -1)
                running, vp = pl.pallas_call(
                    relay_kernel,
                    out_shape=(jax.ShapeDtypeStruct(own.shape, BF), jax.ShapeDtypeStruct(vp.shape, BF)),
                    in_specs=[vmem] * 3,
                    out_specs=(vmem,) * 2,
                    input_output_aliases={2: 1},
                    compiler_params=grant,
                    cost_estimate=pl.CostEstimate(flops=RL, bytes_accessed=1 << 19, transcendentals=0),
                    name="relay",
                )(own, got, vp)
                halo = shifted(kp, "seq", 1), shifted(vp, "seq", 1)
    else:
        running, prior, distance = own, [], 1
        halo = shifted(kp, "seq", 1), shifted(vp, "seq", 1)
        asked = shifted(qb, "seq", -1)
        while distance < count:
            got = shifted(running, "seq", distance)
            prior.append(got)
            running = running + got
            distance *= 2

    local_a = local(0, LA)
    answer = pl.pallas_call(
        functools.partial(serve_kernel, behind=half),
        out_shape=jax.ShapeDtypeStruct((WINDOW + 16 * (WINDOW // TILE), half * HEAD_DIM), BF),
        in_specs=[vmem] * 3,
        out_specs=vmem,
        compiler_params=grant,
        cost_estimate=pl.CostEstimate(flops=SV, bytes_accessed=1 << 20, transcendentals=1 << 10),
        name="serve",
    )(asked, swa_key, values)
    answered = shifted(answer, "seq", 1)
    local_b = local(half, LB)

    num_a, den_a, win_a, sum_a, top_a, phi_a = local_a
    num_b, den_b, win_b, sum_b, top_b, phi_b = local_b
    gain_row = in_hbm(gain.reshape(1, columns))
    operands = (swa_query, *halo, num_a, den_a, win_a, phi_a, sum_a, top_a, num_b, den_b, win_b, phi_b, *prior, before)
    out, lin, gain_b = pl.pallas_call(
        functools.partial(first_final_kernel, heads=heads, width=width),
        out_shape=(
            jax.ShapeDtypeStruct((tokens, columns), BF),
            jax.ShapeDtypeStruct((WINDOW, half * HEAD_DIM), F32),
            jax.ShapeDtypeStruct((1, half * HEAD_DIM), F32),
        ),
        in_specs=[vmem] * len(operands) + [hbm],
        out_specs=(hbm, vmem, vmem),
        scratch_shapes=[
            pltpu.VMEM((1, columns), F32),
            pltpu.VMEM((WINDOW, half * HEAD_DIM), F32),
            pltpu.VMEM((tokens, columns), BF),
            pltpu.SemaphoreType.DMA((heads + 1,)),
        ],
        compiler_params=grant,
        cost_estimate=pl.CostEstimate(flops=2 << 30, bytes_accessed=12 << 20, transcendentals=1 << 20),
        name="final",
    )(*operands, *gain_row)
    return pl.pallas_call(
        last_final_kernel,
        out_shape=jax.ShapeDtypeStruct((tokens, columns), BF),
        in_specs=[vmem] * 6 + [hbm],
        out_specs=hbm,
        scratch_shapes=[
            pltpu.VMEM((WINDOW, half * HEAD_DIM), BF),
            pltpu.SemaphoreType.DMA((WINDOW // TILE,)),
        ],
        input_output_aliases={6: 0},
        compiler_params=grant,
        cost_estimate=pl.CostEstimate(flops=1 << 20, bytes_accessed=3 << 20, transcendentals=1 << 19),
        name="last",
    )(answered, lin, win_b, sum_b, top_b, gain_b, out)


def solution(mesh):
    tokens = P(("groups", "seq"), "head")
    return jax.shard_map(
        body, mesh=mesh, in_specs=(tokens,) * 5 + (P("head"),), out_specs=tokens, check_vma=False
    )
```

time: 39.3 us -> 31.9 us (0.81)
  the two profiles are of different devices: /device:TPU:16 before, /device:TPU:0 now
where the time goes in v4:
time: 31.9 us; the launch traced here: 31.6 us
  starting transfers between devices  16.1 us (50%)
  Pallas kernels  13.1 us (41%)
  waiting for transfers between devices  2.07 us (6%)
    ppermute x4, starting transfers between devices, shifted(): return lax.ppermute(value, axis, pairs)  9.84 us
    ppermute x3, starting transfers between devices, body(): got = lax.ppermute(running, 'seq', [(i, i + 1)])  6.3 us
    pallas_call x2, Pallas kernels, local(): pl.pallas_call(functools.partial(local_kernel, start_head=start_head, wid...  4.87 us
    pallas_call x1, Pallas kernels, body(): pl.pallas_call(functools.partial(first_final_kernel, heads=heads, width=w...  3.35 us
    pallas_call x1, Pallas kernels, body(): pl.pallas_call(functools.partial(prepare_kernel, heads=heads, width=width...  2.32 us
    ppermute x3, waiting for transfers between devices, body(): got = lax.ppermute(running, 'seq', [(i, i + 1)])  2.06 us
    pallas_call x1, Pallas kernels, body(): pl.pallas_call(last_final_kernel, out_shape=jax.ShapeDtypeStruct((tokens,...  1.78 us
    pallas_call x1, Pallas kernels, body(): pl.pallas_call(functools.partial(serve_kernel, behind=half), out_shape=ja...  0.75 us
  transfers between devices with their start and end apart: 7, of which 1 were waited for; matrix products, arithmetic and copies ran while one was open for 0% of the time, Pallas kernels for 28%

profile of v4, /device:TPU:0, one launch (start us, length us, event | category | flops | bytes accessed | tf_op | source)
XLA Modules:
  0.0 31.6 jit_solution(5064990366803874274)
XLA Ops:
  0.0 2.3 %prepare.1 = (bf16[512,256]{1,0:T(8,128)(2,1)S(1)}, bf16[512,256]{1,0:T(8,128)(2,1)S(1)}, bf16[512,256]{1,0:T(8,128)(2,1)S(1)}, bf16[656,128]{1,0:T(8,128)(2,1)S(1)}, f32[3,640,256]{2,1,0:T(8,128)S(1)}) custom-call(bf16[64,1024]{1,0:T(8,128)(2,1)} %bitcast.3, bf16[1024,512]{1,0:T(8,128)(2,1)} %q_ref.5, bf16[1024,512]{1,0:T(8,128)(2,1)} %k_ref.5, ...), custom_call_target="tpu_custom_call" | custom-call | flops 1073741824 | bytes 3145728 | tf_op jit(solution)/shard_map/prepare/pallas_call | solution.py:349
  2.3 5.0 %collective-permute-start.3 = (bf16[656,128]{1,0:T(8,128)(2,1)S(1)}, bf16[656,128]{1,0:T(8,128)(2,1)S(1)}, u32[]{:S(2)}, u32[]{:S(2)}) collective-permute-start(bf16[656,128]{1,0:T(8,128)(2,1)S(1)} %get-tuple-element.29.own_ref), channel_id=1, source_target_pairs={{0,4},{1,5},{2,6},{3,7},{16,20},{17,21},{18,22},{19,23}} | collective-permute-start | bytes 503816 | tf_op jit(solution)/shard_map/ppermute | solution.py:386
  7.3 1.3 %collective-permute-start.2 = (bf16[512,256]{1,0:T(8,128)(2,1)S(1)}, bf16[512,256]{1,0:T(8,128)(2,1)S(1)}, u32[]{:S(2)}, u32[]{:S(2)}) collective-permute-start(bf16[512,256]{1,0:T(8,128)(2,1)S(1)} %get-tuple-element.28), channel_id=1, source_target_pairs={{0,4},{4,8},{8,12},{1,5},{5,9},{9,13},{2,6},{6,10},{10,14},{3,7},{... | collective-permute-start | bytes 786440 | tf_op jit(solution)/shard_map/ppermute | solution.py:332
  8.6 1.3 %collective-permute-start = (bf16[512,256]{1,0:T(8,128)(2,1)S(1)}, bf16[512,256]{1,0:T(8,128)(2,1)S(1)}, u32[]{:S(2)}, u32[]{:S(2)}) collective-permute-start(bf16[512,256]{1,0:T(8,128)(2,1)S(1)} %get-tuple-element.27), channel_id=1, source_target_pairs={{4,0},{8,4},{12,8},{5,1},{9,5},{13,9},{6,2},{10,6},{14,10},{7,3},{... | collective-permute-start | bytes 786440 | tf_op jit(solution)/shard_map/ppermute | solution.py:332
  9.9 2.1 %collective-permute-done.3.got_ref.refs_10_ = bf16[656,128]{1,0:T(8,128)(2,1)S(1)} collective-permute-done((bf16[656,128]{1,0:T(8,128)(2,1)S(1)}, bf16[656,128]{1,0:T(8,128)(2,1)S(1)}, u32[]{:S(2)}, u32[]{:S(2)}) %collective-permute-start.3) | collective-permute-done | bytes 167968 | tf_op jit(solution)/shard_map/ppermute | solution.py:386
  12.0 0.7 %collective-permute-start.5 = (bf16[656,128]{1,0:T(8,128)(2,1)S(1)}, bf16[656,128]{1,0:T(8,128)(2,1)S(1)}, u32[]{:S(2)}, u32[]{:S(2)}) collective-permute-start(bf16[656,128]{1,0:T(8,128)(2,1)S(1)} %get-tuple-element.42), channel_id=1, source_target_pairs={{4,8},{5,9},{6,10},{7,11},{20,24},{21,25},{22,26},{23,27}} | collective-permute-start | bytes 503816 | tf_op jit(solution)/shard_map/ppermute | solution.py:386
  12.7 5.0 %collective-permute-start.4 = (bf16[512,256]{1,0:T(8,128)(2,1)S(1)}, bf16[512,256]{1,0:T(8,128)(2,1)S(1)}, u32[]{:S(2)}, u32[]{:S(2)}) collective-permute-start(bf16[512,256]{1,0:T(8,128)(2,1)S(1)} %get-tuple-element.31), channel_id=1, source_target_pairs={{0,4},{4,8},{8,12},{1,5},{5,9},{9,13},{2,6},{6,10},{10,14},{3,7},{... | collective-permute-start | bytes 786440 | tf_op jit(solution)/shard_map/ppermute | solution.py:332
  17.7 0.0 copy-done
  17.7 0.0 copy-done.1
  17.7 0.0 copy-done.2
  17.8 0.0 copy-done.3
  17.8 2.4 %local.3 = (f32[1024,256]{1,0:T(8,128)S(1)}, f32[1024,256]{1,0:T(8,128)S(1)}, f32[1024,256]{1,0:T(8,128)S(1)}, f32[512,256]{1,0:T(8,128)S(1)}, f32[512,256]{1,0:...) custom-call(bf16[1024,512]{1,0:T(8,128)(2,1)S(1)} %copy-done, bf16[1024,512]{1,0:T(8,128)(2,1)S(1)} %copy-done.1, ...), custom_call_target="tpu_custom_call" | custom-call | flops 4294967296 | bytes 1048576 | tf_op jit(solution)/shard_map/local/pallas_call | solution.py:373
  20.2 0.0 collective-permute-done.5.refs_11_
  20.3 0.7 %collective-permute-start.6 = (bf16[656,128]{1,0:T(8,128)(2,1)S(1)}, bf16[656,128]{1,0:T(8,128)(2,1)S(1)}, u32[]{:S(2)}, u32[]{:S(2)}) collective-permute-start(bf16[656,128]{1,0:T(8,128)(2,1)S(1)} %add.3), channel_id=1, source_target_pairs={{8,12},{9,13},{10,14},{11,15},{24,28},{25,29},{26,30},{27,31}} | collective-permute-start | bytes 503816 | tf_op jit(solution)/shard_map/ppermute | solution.py:386
  21.0 0.0 collective-permute-done.qb_ref
  21.0 0.8 %serve.1 = bf16[544,256]{1,0:T(8,128)(2,1)S(1)} custom-call(bf16[512,256]{1,0:T(8,128)(2,1)S(1)} %collective-permute-done.qb_ref, bf16[1024,512]{1,0:T(8,128)(2,1)S(1)} %copy-done.1, bf16[1024,512]{1,0:T(8,128)(2,1)S(1)} %copy-done.2), custom_call_target="tpu_custom_call" | custom-call | flops 1073741824 | bytes 1048576 | tf_op jit(solution)/shard_map/serve/pallas_call | solution.py:413
  21.7 2.2 %collective-permute-start.1 = (bf16[544,256]{1,0:T(8,128)(2,1)S(1)}, bf16[544,256]{1,0:T(8,128)(2,1)S(1)}, u32[]{:S(2)}, u32[]{:S(2)}) collective-permute-start(bf16[544,256]{1,0:T(8,128)(2,1)S(1)} %serve.1), channel_id=1, source_target_pairs={{0,4},{4,8},{8,12},{1,5},{5,9},{9,13},{2,6},{6,10},{10,14},{3,7},{... | collective-permute-start | bytes 835592 | tf_op jit(solution)/shard_map/ppermute | solution.py:332
  23.9 2.4 %local.2 = (f32[1024,256]{1,0:T(8,128)S(1)}, f32[1024,256]{1,0:T(8,128)S(1)}, f32[1024,256]{1,0:T(8,128)S(1)}, f32[512,256]{1,0:T(8,128)S(1)}, f32[512,256]{1,0:...) custom-call(bf16[1024,512]{1,0:T(8,128)(2,1)S(1)} %copy-done, bf16[1024,512]{1,0:T(8,128)(2,1)S(1)} %copy-done.1, ...), custom_call_target="tpu_custom_call" | custom-call | flops 1073741824 | bytes 1048576 | tf_op jit(solution)/shard_map/local/pallas_call | solution.py:373
  26.4 0.0 collective-permute-done.2.kp_ref
  26.4 0.0 collective-permute-done.4.vp_ref
  26.4 0.0 collective-permute-done.6.refs_12_
  26.4 3.3 %final.1 = (bf16[1024,512]{1,0:T(8,128)(2,1)}, f32[512,256]{1,0:T(8,128)S(1)}, f32[1,256]{1,0:T(1,128)S(1)}) custom-call(bf16[1024,512]{1,0:T(8,128)(2,1)S(1)} %copy-done, bf16[512,256]{1,0:T(8,128)(2,1)S(1)} %collective-permute-done.2.kp_ref, bf16[512,256]{1,0:T(8,128)(2,1)S(1)} %collective-permute-done.4.vp_ref, ...), custom_call_target="tpu_custom_call" | custom-call | flops 2147483648 | bytes 12582912 | tf_op jit(solution)/shard_map/final/pallas_call | solution.py:429
  29.8 0.0 collective-permute-done.1.ob_ref
  29.8 1.8 %last.1 = bf16[1024,512]{1,0:T(8,128)(2,1)} custom-call(bf16[544,256]{1,0:T(8,128)(2,1)S(1)} %collective-permute-done.1.ob_ref, f32[512,256]{1,0:T(8,128)S(1)} %get-tuple-element.44.lin_ref, f32[1024,256]{1,0:T(8,128)S(1)} %get-tuple-element.40.refs_8_.win_ref, f32[512,256]{1,0:T(8,128)S(1)} %get-tuple-element.45.sum_ref, ...), custom_call_target="tpu_custom_call", output_to_operand_aliasing={{}: (6, {})} | custom-call | flops 1048576 | bytes 3145728 | tf_op jit(solution)/shard_map/last/pallas_call | solution.py:448
  (8 shorter events, 0.1 us)
Async XLA Ops:
  0.0 17.7 %copy-start = (bf16[1024,512]{1,0:T(8,128)(2,1)S(1)}, bf16[1024,512]{1,0:T(8,128)(2,1)}, u32[]{:S(2)}) copy-start(bf16[1024,512]{1,0:T(8,128)(2,1)} %q_ref.5) | copy-start | bytes 3145732
  0.0 17.7 %copy-start.1 = (bf16[1024,512]{1,0:T(8,128)(2,1)S(1)}, bf16[1024,512]{1,0:T(8,128)(2,1)}, u32[]{:S(2)}) copy-start(bf16[1024,512]{1,0:T(8,128)(2,1)} %k_ref.5) | copy-start | bytes 3145732
  0.0 17.7 %copy-start.2 = (bf16[1024,512]{1,0:T(8,128)(2,1)S(1)}, bf16[1024,512]{1,0:T(8,128)(2,1)}, u32[]{:S(2)}) copy-start(bf16[1024,512]{1,0:T(8,128)(2,1)} %v_ref.5) | copy-start | bytes 3145732
  0.0 17.8 %copy-start.3 = (bf16[1024,64]{0,1:T(8,128)(2,1)S(1)}, bf16[1024,64]{0,1:T(8,128)(2,1)}, u32[]{:S(2)}) copy-start(bf16[1024,64]{0,1:T(8,128)(2,1)} %param.7) | copy-start | bytes 393220
  0.0 17.8 %copy-start.4 = (bf16[1024,64]{0,1:T(8,128)(2,1)S(1)}, bf16[1024,64]{0,1:T(8,128)(2,1)}, u32[]{:S(2)}) copy-start(bf16[1024,64]{0,1:T(8,128)(2,1)} %param.6) | copy-start | bytes 393220
  2.3 9.6 %collective-permute-start.3 = (bf16[656,128]{1,0:T(8,128)(2,1)S(1)}, bf16[656,128]{1,0:T(8,128)(2,1)S(1)}, u32[]{:S(2)}, u32[]{:S(2)}) collective-permute-start(bf16[656,128]{1,0:T(8,128)(2,1)S(1)} %get-tuple-element.29.own_ref), channel_id=1, source_target_pairs={{0,4},{1,5},{2,6},{3,7},{16,20},{17,21},{18,22},{19,23}} | collective-permute-start | bytes 503816 | tf_op jit(solution)/shard_map/ppermute | solution.py:386
  7.3 19.1 %collective-permute-start.2 = (bf16[512,256]{1,0:T(8,128)(2,1)S(1)}, bf16[512,256]{1,0:T(8,128)(2,1)S(1)}, u32[]{:S(2)}, u32[]{:S(2)}) collective-permute-start(bf16[512,256]{1,0:T(8,128)(2,1)S(1)} %get-tuple-element.28), channel_id=1, source_target_pairs={{0,4},{4,8},{8,12},{1,5},{5,9},{9,13},{2,6},{6,10},{10,14},{3,7},{... | collective-permute-start | bytes 786440 | tf_op jit(solution)/shard_map/ppermute | solution.py:332
  8.6 12.3 %collective-permute-start = (bf16[512,256]{1,0:T(8,128)(2,1)S(1)}, bf16[512,256]{1,0:T(8,128)(2,1)S(1)}, u32[]{:S(2)}, u32[]{:S(2)}) collective-permute-start(bf16[512,256]{1,0:T(8,128)(2,1)S(1)} %get-tuple-element.27), channel_id=1, source_target_pairs={{4,0},{8,4},{12,8},{5,1},{9,5},{13,9},{6,2},{10,6},{14,10},{7,3},{... | collective-permute-start | bytes 786440 | tf_op jit(solution)/shard_map/ppermute | solution.py:332
  12.0 8.2 %collective-permute-start.5 = (bf16[656,128]{1,0:T(8,128)(2,1)S(1)}, bf16[656,128]{1,0:T(8,128)(2,1)S(1)}, u32[]{:S(2)}, u32[]{:S(2)}) collective-permute-start(bf16[656,128]{1,0:T(8,128)(2,1)S(1)} %get-tuple-element.42), channel_id=1, source_target_pairs={{4,8},{5,9},{6,10},{7,11},{20,24},{21,25},{22,26},{23,27}} | collective-permute-start | bytes 503816 | tf_op jit(solution)/shard_map/ppermute | solution.py:386
  12.7 13.7 %collective-permute-start.4 = (bf16[512,256]{1,0:T(8,128)(2,1)S(1)}, bf16[512,256]{1,0:T(8,128)(2,1)S(1)}, u32[]{:S(2)}, u32[]{:S(2)}) collective-permute-start(bf16[512,256]{1,0:T(8,128)(2,1)S(1)} %get-tuple-element.31), channel_id=1, source_target_pairs={{0,4},{4,8},{8,12},{1,5},{5,9},{9,13},{2,6},{6,10},{10,14},{3,7},{... | collective-permute-start | bytes 786440 | tf_op jit(solution)/shard_map/ppermute | solution.py:332
  20.3 6.1 %collective-permute-start.6 = (bf16[656,128]{1,0:T(8,128)(2,1)S(1)}, bf16[656,128]{1,0:T(8,128)(2,1)S(1)}, u32[]{:S(2)}, u32[]{:S(2)}) collective-permute-start(bf16[656,128]{1,0:T(8,128)(2,1)S(1)} %add.3), channel_id=1, source_target_pairs={{8,12},{9,13},{10,14},{11,15},{24,28},{25,29},{26,30},{27,31}} | collective-permute-start | bytes 503816 | tf_op jit(solution)/shard_map/ppermute | solution.py:386
  21.7 8.0 %collective-permute-start.1 = (bf16[544,256]{1,0:T(8,128)(2,1)S(1)}, bf16[544,256]{1,0:T(8,128)(2,1)S(1)}, u32[]{:S(2)}, u32[]{:S(2)}) collective-permute-start(bf16[544,256]{1,0:T(8,128)(2,1)S(1)} %serve.1), channel_id=1, source_target_pairs={{0,4},{4,8},{8,12},{1,5},{5,9},{9,13},{2,6},{6,10},{10,14},{3,7},{... | collective-permute-start | bytes 835592 | tf_op jit(solution)/shard_map/ppermute | solution.py:332

commit v5 on v4

--- a/solution.py
+++ b/solution.py
@@ -20,6 +20,7 @@
 SV = 1 << 30
 PR = 1 << 30
 RL = 1 << 17
+FN = 2 << 30
 
 
 def feature_rows(width):
@@ -80,33 +81,35 @@
     tokens = v_ref.shape[0]
     ahead = heads // 2 * HEAD_DIM
     tail = pl.ds(tokens - WINDOW, WINDOW)
+    fetch = pltpu.make_async_copy(kf_hbm, kf_ref, sems.at[3])
+    fetch.start()
+    whole = pltpu.make_async_copy(v_hbm, v_ref, sems.at[4])
+    whole.start()
     copies = [
-        pltpu.make_async_copy(kf_hbm, kf_ref, sems.at[0]),
-        pltpu.make_async_copy(v_hbm, v_ref, sems.at[1]),
-        pltpu.make_async_copy(k_hbm.at[tail, :ahead], kp_ref, sems.at[2]),
-        pltpu.make_async_copy(v_hbm.at[tail, :ahead], vp_ref, sems.at[3]),
-        pltpu.make_async_copy(q_hbm.at[:WINDOW, ahead:], qb_ref, sems.at[4]),
+        pltpu.make_async_copy(k_hbm.at[tail, :ahead], kp_ref, sems.at[0]),
+        pltpu.make_async_copy(v_hbm.at[tail, :ahead], vp_ref, sems.at[1]),
+        pltpu.make_async_copy(q_hbm.at[:WINDOW, ahead:], qb_ref, sems.at[2]),
     ]
     for copy in copies:
         copy.start()
-    ones = jnp.ones((16, tokens), BF)
-    own_ref[base:, :] = jnp.zeros((16, HEAD_DIM), BF)
-    copies[0].wait()
-    copies[1].wait()
+    fetch.wait()
+    phis = [phi_rows(kf_ref[h * width : (h + 1) * width, :].astype(F32), False) for h in range(heads)]
+    lane = lax.broadcasted_iota(jnp.int32, (feats, HEAD_DIM), 1)
+    norms = jnp.zeros((feats, HEAD_DIM), F32)
+    whole.wait()
     for h in range(heads):
-        phi = phi_rows(kf_ref[h * width : (h + 1) * width, :].astype(F32), False)
         total = None
         for t in range(tokens // TILE):
             at = slice(t * TILE, (t + 1) * TILE)
-            s = nn(phi[:, at], with_ones(v_ref[at, h * HEAD_DIM : (h + 1) * HEAD_DIM]))
+            s = nn(phis[h][:, at], with_ones(v_ref[at, h * HEAD_DIM : (h + 1) * HEAD_DIM]))
             total = s if t == 0 else total + s
             if t < tokens // TILE - 1:
                 before_ref[t, h * feats : (h + 1) * feats, :] = total
-        norm = nt(ones, phi)
         own_ref[h * feats : (h + 1) * feats, :] = total[:, :HEAD_DIM].astype(BF)
-        own_ref[base + 2 * h : base + 2 * h + 1, :] = norm[:1, :HEAD_DIM].astype(BF)
-        own_ref[base + 2 * h + 1 : base + 2 * h + 2, : feats - HEAD_DIM] = norm[:1, HEAD_DIM:].astype(BF)
-    for copy in copies[2:]:
+        norms = jnp.where(lane == h, total[:, HEAD_DIM:], norms)
+    norms = jnp.concatenate([norms, jnp.zeros((2 * HEAD_DIM - feats, HEAD_DIM), F32)], 0).T[:8]
+    own_ref[base:, :] = jnp.concatenate([norms[:, :HEAD_DIM], norms[:, HEAD_DIM:]], 0).astype(BF)
+    for copy in copies:
         copy.wait()
     top = kp_ref[:16, :]
     row = lax.broadcasted_iota(jnp.int32, top.shape, 0)
@@ -147,11 +150,9 @@
         wide = slice(h * HEAD_DIM, (h + 1) * HEAD_DIM)
 
         def use(top, out, total):
-            if start >= WINDOW:
-                win_ref[at, lanes] = out / total
-            else:
-                win_ref[at, lanes] = out
-                sum_ref[at, lanes] = total
+            win_ref[at, lanes] = out
+            sum_ref[at, lanes] = total
+            if start < WINDOW:
                 top_ref[at, lanes] = jnp.broadcast_to(top, (TILE, HEAD_DIM))
             r = nn(phi_ref[g, at, HEAD_DIM:], kfs[g][:, at])
             part = width ** (-0.25)
@@ -214,41 +215,49 @@
     most = jnp.maximum(mine, top)
     here = jnp.exp2((mine - most) * SCALE)
     there = jnp.exp2((top - most) * SCALE)
-    return (window * here + out * there) / (total * here + count * there)
-
-
-def normed(mixed, gain):
-    power = jnp.mean(mixed * mixed, 1, keepdims=True)
-    return (mixed * lax.rsqrt(power + 1e-05) * gain).astype(BF)
-
-
-def first_final_kernel(q_ref, kp_ref, vp_ref, *refs, heads, width):
-    halves = [refs[:6], refs[6:10]]
-    *prior_refs, before_ref, gain_hbm, out_hbm, lin_ref, gain_b_ref, gain_ref, near_ref, out_ref, sems = refs[10:]
+    return window * here + out * there, total * here + count * there
+
+
+def power_of(mixed):
+    return jnp.mean(mixed * mixed, 1, keepdims=True) + 1e-05
+
+
+def normed(mixed, power, gain):
+    return (mixed * lax.rsqrt(power) * gain).astype(BF)
+
+
+def halo_jobs(q_ref, kp_ref, vp_ref, win_ref, sum_ref, top_ref, near_ref, both_ref):
+    _, beyond = causal_masks()
+    later = kp_ref[:1, :1].astype(F32) > 0
+    jobs = []
+
+    def job(g, start):
+        at = slice(start, start + TILE)
+        keys = slice(start, WINDOW)
+        cols = slice(g * HEAD_DIM, (g + 1) * HEAD_DIM)
+
+        def use(top, out, total):
+            near_ref[at, cols], both_ref[at, cols] = merged(
+                win_ref[at, cols], top_ref[at, cols], sum_ref[at, cols], top, out, total, later
+            )
+
+        jobs.append((lambda: q_ref[at, cols], lambda: kp_ref[keys, cols], lambda: vp_ref[keys, cols], beyond, None, use))
+
+    for g in range(kp_ref.shape[1] // HEAD_DIM):
+        for start in range(0, WINDOW, TILE):
+            job(g, start)
+    return jobs
+
+
+def first_final_kernel(q_ref, kp_ref, vp_ref, top_ref, *refs, heads, width):
+    halves = [refs[:5], refs[5:10]]
+    *prior_refs, before_ref, gain_hbm, out_hbm, lin_ref, gain_b_ref, gain_ref, near_ref, both_ref, out_ref, sems = refs[10:]
     count = heads // 2
-    tokens = q_ref.shape[0]
+    tokens = halves[0][0].shape[0]
     feats = feature_rows(width)
     base = heads * feats
     fetch = pltpu.make_async_copy(gain_hbm, gain_ref, sems.at[heads])
     fetch.start()
-    _, beyond = causal_masks()
-    later = kp_ref[:1, :1].astype(F32) > 0
-    jobs = []
-
-    def job(g, start):
-        at = slice(start, start + TILE)
-        keys = slice(start, WINDOW)
-        cols = slice(g * HEAD_DIM, (g + 1) * HEAD_DIM)
-        win_ref, _, sum_ref, top_ref = halves[0][2:]
-
-        def use(top, out, total):
-            near_ref[at, cols] = merged(win_ref[at, cols], top_ref[at, cols], sum_ref[at, cols], top, out, total, later)
-
-        jobs.append((lambda: q_ref[at, cols], lambda: kp_ref[keys, cols], lambda: vp_ref[keys, cols], beyond, None, use))
-
-    for g in range(count):
-        for start in range(0, WINDOW, TILE):
-            job(g, start)
 
     def prior(rows):
         return functools.reduce(jnp.add, [ref[rows, :].astype(F32) for ref in prior_refs])
@@ -257,37 +266,42 @@
 
     def state(h):
         norm = [
-            jnp.broadcast_to(tail[:, 2 * h : 2 * h + 1], (HEAD_DIM, HEAD_DIM)),
-            jnp.broadcast_to(tail[: feats - HEAD_DIM, 2 * h + 1 : 2 * h + 2], (feats - HEAD_DIM, HEAD_DIM)),
+            jnp.broadcast_to(tail[:, h : h + 1], (HEAD_DIM, HEAD_DIM)),
+            jnp.broadcast_to(tail[: feats - HEAD_DIM, 8 + h : 9 + h], (feats - HEAD_DIM, HEAD_DIM)),
         ]
         return jnp.concatenate([prior(slice(h * feats, (h + 1) * feats)), jnp.concatenate(norm, 0)], 1)
 
-    softmax_parts(jobs)
+    softmax_parts(halo_jobs(q_ref, kp_ref, vp_ref, halves[0][2], halves[0][3], top_ref, near_ref, both_ref))
     order = [(h, start) for h in list(range(count, heads)) + list(range(count)) for start in range(0, tokens, TILE)]
     states, lins, copies = {}, [], []
     for i, (h, start) in enumerate(order):
-        while len(lins) < min(len(order), i + 2):
+        while len(lins) < min(len(order), i + 3):
             hn, sn = order[len(lins)]
             rows = slice(hn * feats, (hn + 1) * feats)
             if hn not in states:
                 states[hn] = state(hn)
             both = states[hn] if sn == 0 else states[hn] + before_ref[sn // TILE - 1, rows, :]
-            lins.append(nn(halves[hn // count][3][hn % count, sn : sn + TILE, :], both.astype(BF)))
+            lins.append(nn(halves[hn // count][4][hn % count, sn : sn + TILE, :], both.astype(BF)))
         lin, lins[i] = lins[i], None
         part, g = h // count, h % count
-        num_ref, den_ref, win_ref = halves[part][:3]
+        num_ref, den_ref, win_ref, sum_ref = halves[part][:4]
         at = slice(start, start + TILE)
         cols = slice(g * HEAD_DIM, (g + 1) * HEAD_DIM)
         wide = slice(h * HEAD_DIM, (h + 1) * HEAD_DIM)
-        mixed = (num_ref[at, cols] + lin[:, :HEAD_DIM]) / (den_ref[at, cols] + lin[:, HEAD_DIM:])
+        num = num_ref[at, cols] + lin[:, :HEAD_DIM]
+        den = den_ref[at, cols] + lin[:, HEAD_DIM:]
         if start < WINDOW and part == 1:
-            lin_ref[at, cols] = mixed
+            lin_ref[at, cols] = num / den
         else:
             if not copies and start == WINDOW:
                 fetch.wait()
                 gain_b_ref[...] = gain_ref[:, count * HEAD_DIM :]
-            window = near_ref[at, cols] if start < WINDOW else win_ref[at, cols]
-            out_ref[at, wide] = normed(mixed + window, gain_ref[:, wide])
+            if start < WINDOW:
+                window, total = near_ref[at, cols], both_ref[at, cols]
+            else:
+                window, total = win_ref[at, cols], sum_ref[at, cols]
+            mixed = num / den + window / total
+            out_ref[at, wide] = normed(mixed, power_of(mixed), gain_ref[:, wide])
         if start + TILE == tokens:
             area = (pl.ds(WINDOW * part, tokens - WINDOW * part), pl.ds(h * HEAD_DIM, HEAD_DIM))
             copies.append(pltpu.make_async_copy(out_ref.at[area], out_hbm.at[area], sems.at[h]))
@@ -300,26 +314,34 @@
     count = lin_ref.shape[1] // HEAD_DIM
     ahead = out_hbm.shape[1] - count * HEAD_DIM
     later = ob_ref[WINDOW + 15 : WINDOW + 16, :1].astype(F32) > 0
-    copies = []
     stats = []
+    n = 2 * count
     for i in range(WINDOW // TILE):
         got = ob_ref[WINDOW + 16 * i : WINDOW + 16 * (i + 1), :].astype(F32)
-        n = 2 * count
-        got = got[:n] + got[n : 2 * n] + got[2 * n : 3 * n]
-        stats.append(jnp.concatenate([got, jnp.zeros((HEAD_DIM - n, TILE), F32)], 0).T)
-    for start in range(0, WINDOW, TILE):
-        at = slice(start, start + TILE)
-        stat = stats[start // TILE]
-        for g in range(count):
-            cols = slice(g * HEAD_DIM, (g + 1) * HEAD_DIM)
-            out = ob_ref[at, cols].astype(F32)
-            window = merged(win_ref[at, cols], top_ref[at, cols], sum_ref[at, cols], stat[:, g : g + 1], out, stat[:, count + g : count + g + 1], later)
-            out_ref[at, cols] = normed(lin_ref[at, cols] + window, gain_ref[:, cols])
-        copy = pltpu.make_async_copy(out_ref.at[at, :], out_hbm.at[at, ahead:], sems.at[start // TILE])
-        copy.start()
-        copies.append(copy)
-    for copy in copies:
-        copy.wait()
+        stats.append(got[:n] + got[n : 2 * n] + got[2 * n : 3 * n])
+    stats.append(jnp.zeros((HEAD_DIM - n * len(stats), TILE), F32))
+    stats = jnp.concatenate(stats, 0).T
+    parts = [(start, g) for start in range(0, WINDOW, TILE) for g in range(count)]
+
+    def place(start, g):
+        return slice(start, start + TILE), slice(g * HEAD_DIM, (g + 1) * HEAD_DIM)
+
+    def stat(start, lane):
+        lane += start // TILE * n
+        return stats[:, lane : lane + 1]
+
+    windows = []
+    for start, g in parts:
+        at = place(start, g)
+        windows.append(merged(win_ref[at], top_ref[at], sum_ref[at], stat(start, g), ob_ref[at].astype(F32), stat(start, count + g), later))
+    mixed = [lin_ref[place(*part)] + window / total for part, (window, total) in zip(parts, windows)]
+    powers = [power_of(m) for m in mixed]
+    for part, m, power in zip(parts, mixed, powers):
+        at = place(*part)
+        out_ref[at] = normed(m, power, gain_ref[:, at[1]])
+    copy = pltpu.make_async_copy(out_ref, out_hbm.at[:WINDOW, ahead:], sems.at[0])
+    copy.start()
+    copy.wait()
 
 
 def relay_kernel(own_ref, got_ref, _, sum_ref, pass_ref):
@@ -372,7 +394,7 @@
         near = jax.ShapeDtypeStruct((WINDOW, half * HEAD_DIM), F32)
         return pl.pallas_call(
             functools.partial(local_kernel, start_head=start_head, width=width),
-            out_shape=(wide, wide, wide, near, near, jax.ShapeDtypeStruct((half, tokens, feats), BF)),
+            out_shape=(wide, wide, wide, wide, near, jax.ShapeDtypeStruct((half, tokens, feats), BF)),
             in_specs=[vmem] * 5,
             out_specs=(vmem,) * 6,
             compiler_params=grant,
@@ -425,24 +447,26 @@
     num_a, den_a, win_a, sum_a, top_a, phi_a = local_a
     num_b, den_b, win_b, sum_b, top_b, phi_b = local_b
     gain_row = in_hbm(gain.reshape(1, columns))
-    operands = (swa_query, *halo, num_a, den_a, win_a, phi_a, sum_a, top_a, num_b, den_b, win_b, phi_b, *prior, before)
+    near = jax.ShapeDtypeStruct((WINDOW, half * HEAD_DIM), F32)
+    operands = (swa_query, *halo, top_a, num_a, den_a, win_a, sum_a, phi_a, num_b, den_b, win_b, sum_b, phi_b, *prior, before)
     out, lin, gain_b = pl.pallas_call(
         functools.partial(first_final_kernel, heads=heads, width=width),
         out_shape=(
             jax.ShapeDtypeStruct((tokens, columns), BF),
-            jax.ShapeDtypeStruct((WINDOW, half * HEAD_DIM), F32),
+            near,
             jax.ShapeDtypeStruct((1, half * HEAD_DIM), F32),
         ),
         in_specs=[vmem] * len(operands) + [hbm],
         out_specs=(hbm, vmem, vmem),
         scratch_shapes=[
             pltpu.VMEM((1, columns), F32),
-            pltpu.VMEM((WINDOW, half * HEAD_DIM), F32),
+            pltpu.VMEM(near.shape, F32),
+            pltpu.VMEM(near.shape, F32),
             pltpu.VMEM((tokens, columns), BF),
             pltpu.SemaphoreType.DMA((heads + 1,)),
         ],
         compiler_params=grant,
-        cost_estimate=pl.CostEstimate(flops=2 << 30, bytes_accessed=12 << 20, transcendentals=1 << 20),
+        cost_estimate=pl.CostEstimate(flops=FN, bytes_accessed=12 << 20, transcendentals=1 << 20),
         name="final",
     )(*operands, *gain_row)
     return pl.pallas_call(
@@ -452,7 +476,7 @@
         out_specs=hbm,
         scratch_shapes=[
             pltpu.VMEM((WINDOW, half * HEAD_DIM), BF),
-            pltpu.SemaphoreType.DMA((WINDOW // TILE,)),
+            pltpu.SemaphoreType.DMA((1,)),
         ],
         input_output_aliases={6: 0},
         compiler_params=grant,

time: 31.9 us -> 31.4 us (0.984)
  Pallas kernels: 13.1 us -> 12.7 us
  transfers between devices with their start and end apart: 7 -> 7, of which waited for: 1 -> 1; matrix products, arithmetic and copies ran while one was open for 0% -> 0% of each run, Pallas kernels for 28% -> 29%
where the time goes in v5:
time: 31.4 us; the launch traced here: 31.1 us
  starting transfers between devices  16.1 us (51%)
  Pallas kernels  12.7 us (40%)
  waiting for transfers between devices  2.07 us (7%)
    ppermute x4, starting transfers between devices, shifted(): return lax.ppermute(value, axis, pairs)  9.83 us
    ppermute x3, starting transfers between devices, body(): got = lax.ppermute(running, 'seq', [(i, i + 1)])  6.3 us
    pallas_call x2, Pallas kernels, local(): pl.pallas_call(functools.partial(local_kernel, start_head=start_head, wid...  4.89 us
    pallas_call x1, Pallas kernels, body(): pl.pallas_call(functools.partial(first_final_kernel, heads=heads, width=w...  3.23 us
    pallas_call x1, Pallas kernels, body(): pl.pallas_call(functools.partial(prepare_kernel, heads=heads, width=width...  2.07 us
    ppermute x3, waiting for transfers between devices, body(): got = lax.ppermute(running, 'seq', [(i, i + 1)])  2.06 us
    pallas_call x1, Pallas kernels, body(): pl.pallas_call(last_final_kernel, out_shape=jax.ShapeDtypeStruct((tokens,...  1.68 us
    pallas_call x1, Pallas kernels, body(): pl.pallas_call(functools.partial(serve_kernel, behind=half), out_shape=ja...  0.75 us
  transfers between devices with their start and end apart: 7, of which 1 were waited for; matrix products, arithmetic and copies ran while one was open for 0% of the time, Pallas kernels for 29%

profile of v5, /device:TPU:0, one launch (start us, length us, event | category | flops | bytes accessed | tf_op | source)
XLA Modules:
  0.0 31.1 jit_solution(17090076355798479540)
XLA Ops:
  0.0 2.1 %prepare.1 = (bf16[512,256]{1,0:T(8,128)(2,1)S(1)}, bf16[512,256]{1,0:T(8,128)(2,1)S(1)}, bf16[512,256]{1,0:T(8,128)(2,1)S(1)}, bf16[656,128]{1,0:T(8,128)(2,1)S(1)}, f32[3,640,256]{2,1,0:T(8,128)S(1)}) custom-call(bf16[64,1024]{1,0:T(8,128)(2,1)} %bitcast.3, bf16[1024,512]{1,0:T(8,128)(2,1)} %q_ref.5, bf16[1024,512]{1,0:T(8,128)(2,1)} %k_ref.5, ...), custom_call_target="tpu_custom_call" | custom-call | flops 1073741824 | bytes 3145728 | tf_op jit(solution)/shard_map/prepare/pallas_call | solution.py:371
  2.1 5.0 %collective-permute-start.3 = (bf16[656,128]{1,0:T(8,128)(2,1)S(1)}, bf16[656,128]{1,0:T(8,128)(2,1)S(1)}, u32[]{:S(2)}, u32[]{:S(2)}) collective-permute-start(bf16[656,128]{1,0:T(8,128)(2,1)S(1)} %get-tuple-element.29.own_ref), channel_id=1, source_target_pairs={{0,4},{1,5},{2,6},{3,7},{16,20},{17,21},{18,22},{19,23}} | collective-permute-start | bytes 503816 | tf_op jit(solution)/shard_map/ppermute | solution.py:408
  7.1 1.3 %collective-permute-start.2 = (bf16[512,256]{1,0:T(8,128)(2,1)S(1)}, bf16[512,256]{1,0:T(8,128)(2,1)S(1)}, u32[]{:S(2)}, u32[]{:S(2)}) collective-permute-start(bf16[512,256]{1,0:T(8,128)(2,1)S(1)} %get-tuple-element.28), channel_id=1, source_target_pairs={{0,4},{4,8},{8,12},{1,5},{5,9},{9,13},{2,6},{6,10},{10,14},{3,7},{... | collective-permute-start | bytes 786440 | tf_op jit(solution)/shard_map/ppermute | solution.py:354
  8.4 1.3 %collective-permute-start = (bf16[512,256]{1,0:T(8,128)(2,1)S(1)}, bf16[512,256]{1,0:T(8,128)(2,1)S(1)}, u32[]{:S(2)}, u32[]{:S(2)}) collective-permute-start(bf16[512,256]{1,0:T(8,128)(2,1)S(1)} %get-tuple-element.27), channel_id=1, source_target_pairs={{4,0},{8,4},{12,8},{5,1},{9,5},{13,9},{6,2},{10,6},{14,10},{7,3},{... | collective-permute-start | bytes 786440 | tf_op jit(solution)/shard_map/ppermute | solution.py:354
  9.7 2.1 %collective-permute-done.3.got_ref.refs_10_ = bf16[656,128]{1,0:T(8,128)(2,1)S(1)} collective-permute-done((bf16[656,128]{1,0:T(8,128)(2,1)S(1)}, bf16[656,128]{1,0:T(8,128)(2,1)S(1)}, u32[]{:S(2)}, u32[]{:S(2)}) %collective-permute-start.3) | collective-permute-done | bytes 167968 | tf_op jit(solution)/shard_map/ppermute | solution.py:408
  11.8 0.7 %collective-permute-start.5 = (bf16[656,128]{1,0:T(8,128)(2,1)S(1)}, bf16[656,128]{1,0:T(8,128)(2,1)S(1)}, u32[]{:S(2)}, u32[]{:S(2)}) collective-permute-start(bf16[656,128]{1,0:T(8,128)(2,1)S(1)} %get-tuple-element.43), channel_id=1, source_target_pairs={{4,8},{5,9},{6,10},{7,11},{20,24},{21,25},{22,26},{23,27}} | collective-permute-start | bytes 503816 | tf_op jit(solution)/shard_map/ppermute | solution.py:408
  12.4 5.0 %collective-permute-start.4 = (bf16[512,256]{1,0:T(8,128)(2,1)S(1)}, bf16[512,256]{1,0:T(8,128)(2,1)S(1)}, u32[]{:S(2)}, u32[]{:S(2)}) collective-permute-start(bf16[512,256]{1,0:T(8,128)(2,1)S(1)} %get-tuple-element.31), channel_id=1, source_target_pairs={{0,4},{4,8},{8,12},{1,5},{5,9},{9,13},{2,6},{6,10},{10,14},{3,7},{... | collective-permute-start | bytes 786440 | tf_op jit(solution)/shard_map/ppermute | solution.py:354
  17.5 0.0 copy-done
  17.5 0.0 copy-done.1
  17.5 0.0 copy-done.2
  17.5 0.0 copy-done.3
  17.5 2.4 %local.3 = (f32[1024,256]{1,0:T(8,128)S(1)}, f32[1024,256]{1,0:T(8,128)S(1)}, f32[1024,256]{1,0:T(8,128)S(1)}, f32[1024,256]{1,0:T(8,128)S(1)}, f32[512,256]{1,0...) custom-call(bf16[1024,512]{1,0:T(8,128)(2,1)S(1)} %copy-done, bf16[1024,512]{1,0:T(8,128)(2,1)S(1)} %copy-done.1, ...), custom_call_target="tpu_custom_call" | custom-call | flops 4294967296 | bytes 1048576 | tf_op jit(solution)/shard_map/local/pallas_call | solution.py:395
  20.0 0.0 collective-permute-done.5.refs_11_
  20.0 0.7 %collective-permute-start.6 = (bf16[656,128]{1,0:T(8,128)(2,1)S(1)}, bf16[656,128]{1,0:T(8,128)(2,1)S(1)}, u32[]{:S(2)}, u32[]{:S(2)}) collective-permute-start(bf16[656,128]{1,0:T(8,128)(2,1)S(1)} %add.3), channel_id=1, source_target_pairs={{8,12},{9,13},{10,14},{11,15},{24,28},{25,29},{26,30},{27,31}} | collective-permute-start | bytes 503816 | tf_op jit(solution)/shard_map/ppermute | solution.py:408
  20.7 0.0 collective-permute-done.qb_ref
  20.7 0.8 %serve.1 = bf16[544,256]{1,0:T(8,128)(2,1)S(1)} custom-call(bf16[512,256]{1,0:T(8,128)(2,1)S(1)} %collective-permute-done.qb_ref, bf16[1024,512]{1,0:T(8,128)(2,1)S(1)} %copy-done.1, bf16[1024,512]{1,0:T(8,128)(2,1)S(1)} %copy-done.2), custom_call_target="tpu_custom_call" | custom-call | flops 1073741824 | bytes 1048576 | tf_op jit(solution)/shard_map/serve/pallas_call | solution.py:435
  21.5 2.2 %collective-permute-start.1 = (bf16[544,256]{1,0:T(8,128)(2,1)S(1)}, bf16[544,256]{1,0:T(8,128)(2,1)S(1)}, u32[]{:S(2)}, u32[]{:S(2)}) collective-permute-start(bf16[544,256]{1,0:T(8,128)(2,1)S(1)} %serve.1), channel_id=1, source_target_pairs={{0,4},{4,8},{8,12},{1,5},{5,9},{9,13},{2,6},{6,10},{10,14},{3,7},{... | collective-permute-start | bytes 835592 | tf_op jit(solution)/shard_map/ppermute | solution.py:354
  23.7 2.4 %local.2 = (f32[1024,256]{1,0:T(8,128)S(1)}, f32[1024,256]{1,0:T(8,128)S(1)}, f32[1024,256]{1,0:T(8,128)S(1)}, f32[1024,256]{1,0:T(8,128)S(1)}, f32[512,256]{1,0...) custom-call(bf16[1024,512]{1,0:T(8,128)(2,1)S(1)} %copy-done, bf16[1024,512]{1,0:T(8,128)(2,1)S(1)} %copy-done.1, ...), custom_call_target="tpu_custom_call" | custom-call | flops 1073741824 | bytes 1048576 | tf_op jit(solution)/shard_map/local/pallas_call | solution.py:395
  26.1 0.0 collective-permute-done.2.kp_ref
  26.2 0.0 collective-permute-done.4.vp_ref
  26.2 0.0 collective-permute-done.6.refs_12_
  26.2 3.2 %final.1 = (bf16[1024,512]{1,0:T(8,128)(2,1)}, f32[512,256]{1,0:T(8,128)S(1)}, f32[1,256]{1,0:T(1,128)S(1)}) custom-call(bf16[1024,512]{1,0:T(8,128)(2,1)S(1)} %copy-done, bf16[512,256]{1,0:T(8,128)(2,1)S(1)} %collective-permute-done.2.kp_ref, bf16[512,256]{1,0:T(8,128)(2,1)S(1)} %collective-permute-done.4.vp_ref, f32[512,256]{1,0:T(8,128)S(1)} %get-tuple-element.32.top_ref, ...), custom_call_target="tpu_custom_call" | custom-call | flops 2147483648 | bytes 12582912 | tf_op jit(solution)/shard_map/final/pallas_call | solution.py:452
  29.4 0.0 collective-permute-done.1.ob_ref
  29.4 1.7 %last.1 = bf16[1024,512]{1,0:T(8,128)(2,1)} custom-call(bf16[544,256]{1,0:T(8,128)(2,1)S(1)} %collective-permute-done.1.ob_ref, f32[512,256]{1,0:T(8,128)S(1)} %get-tuple-element.45.lin_ref, f32[1024,256]{1,0:T(8,128)S(1)} %get-tuple-element.40.refs_7_.win_ref, f32[1024,256]{1,0:T(8,128)S(1)} %get-tuple-element.41.refs_8_.sum_ref, ...), custom_call_target="tpu_custom_call", output_to_operand_aliasing={{}: (6, {})} | custom-call | flops 1048576 | bytes 3145728 | tf_op jit(solution)/shard_map/last/pallas_call | solution.py:472
  (8 shorter events, 0.1 us)
Async XLA Ops:
  0.0 17.5 %copy-start = (bf16[1024,512]{1,0:T(8,128)(2,1)S(1)}, bf16[1024,512]{1,0:T(8,128)(2,1)}, u32[]{:S(2)}) copy-start(bf16[1024,512]{1,0:T(8,128)(2,1)} %q_ref.5) | copy-start | bytes 3145732
  0.0 17.5 %copy-start.1 = (bf16[1024,512]{1,0:T(8,128)(2,1)S(1)}, bf16[1024,512]{1,0:T(8,128)(2,1)}, u32[]{:S(2)}) copy-start(bf16[1024,512]{1,0:T(8,128)(2,1)} %k_ref.5) | copy-start | bytes 3145732
  0.0 17.5 %copy-start.2 = (bf16[1024,512]{1,0:T(8,128)(2,1)S(1)}, bf16[1024,512]{1,0:T(8,128)(2,1)}, u32[]{:S(2)}) copy-start(bf16[1024,512]{1,0:T(8,128)(2,1)} %v_ref.5) | copy-start | bytes 3145732
  0.0 17.5 %copy-start.3 = (bf16[1024,64]{0,1:T(8,128)(2,1)S(1)}, bf16[1024,64]{0,1:T(8,128)(2,1)}, u32[]{:S(2)}) copy-start(bf16[1024,64]{0,1:T(8,128)(2,1)} %param.7) | copy-start | bytes 393220
  0.0 17.5 %copy-start.4 = (bf16[1024,64]{0,1:T(8,128)(2,1)S(1)}, bf16[1024,64]{0,1:T(8,128)(2,1)}, u32[]{:S(2)}) copy-start(bf16[1024,64]{0,1:T(8,128)(2,1)} %param.6) | copy-start | bytes 393220
  2.1 9.6 %collective-permute-start.3 = (bf16[656,128]{1,0:T(8,128)(2,1)S(1)}, bf16[656,128]{1,0:T(8,128)(2,1)S(1)}, u32[]{:S(2)}, u32[]{:S(2)}) collective-permute-start(bf16[656,128]{1,0:T(8,128)(2,1)S(1)} %get-tuple-element.29.own_ref), channel_id=1, source_target_pairs={{0,4},{1,5},{2,6},{3,7},{16,20},{17,21},{18,22},{19,23}} | collective-permute-start | bytes 503816 | tf_op jit(solution)/shard_map/ppermute | solution.py:408
  7.1 19.1 %collective-permute-start.2 = (bf16[512,256]{1,0:T(8,128)(2,1)S(1)}, bf16[512,256]{1,0:T(8,128)(2,1)S(1)}, u32[]{:S(2)}, u32[]{:S(2)}) collective-permute-start(bf16[512,256]{1,0:T(8,128)(2,1)S(1)} %get-tuple-element.28), channel_id=1, source_target_pairs={{0,4},{4,8},{8,12},{1,5},{5,9},{9,13},{2,6},{6,10},{10,14},{3,7},{... | collective-permute-start | bytes 786440 | tf_op jit(solution)/shard_map/ppermute | solution.py:354
  8.4 12.4 %collective-permute-start = (bf16[512,256]{1,0:T(8,128)(2,1)S(1)}, bf16[512,256]{1,0:T(8,128)(2,1)S(1)}, u32[]{:S(2)}, u32[]{:S(2)}) collective-permute-start(bf16[512,256]{1,0:T(8,128)(2,1)S(1)} %get-tuple-element.27), channel_id=1, source_target_pairs={{4,0},{8,4},{12,8},{5,1},{9,5},{13,9},{6,2},{10,6},{14,10},{7,3},{... | collective-permute-start | bytes 786440 | tf_op jit(solution)/shard_map/ppermute | solution.py:354
  11.8 8.2 %collective-permute-start.5 = (bf16[656,128]{1,0:T(8,128)(2,1)S(1)}, bf16[656,128]{1,0:T(8,128)(2,1)S(1)}, u32[]{:S(2)}, u32[]{:S(2)}) collective-permute-start(bf16[656,128]{1,0:T(8,128)(2,1)S(1)} %get-tuple-element.43), channel_id=1, source_target_pairs={{4,8},{5,9},{6,10},{7,11},{20,24},{21,25},{22,26},{23,27}} | collective-permute-start | bytes 503816 | tf_op jit(solution)/shard_map/ppermute | solution.py:408
  12.4 13.7 %collective-permute-start.4 = (bf16[512,256]{1,0:T(8,128)(2,1)S(1)}, bf16[512,256]{1,0:T(8,128)(2,1)S(1)}, u32[]{:S(2)}, u32[]{:S(2)}) collective-permute-start(bf16[512,256]{1,0:T(8,128)(2,1)S(1)} %get-tuple-element.31), channel_id=1, source_target_pairs={{0,4},{4,8},{8,12},{1,5},{5,9},{9,13},{2,6},{6,10},{10,14},{3,7},{... | collective-permute-start | bytes 786440 | tf_op jit(solution)/shard_map/ppermute | solution.py:354
  20.0 6.1 %collective-permute-start.6 = (bf16[656,128]{1,0:T(8,128)(2,1)S(1)}, bf16[656,128]{1,0:T(8,128)(2,1)S(1)}, u32[]{:S(2)}, u32[]{:S(2)}) collective-permute-start(bf16[656,128]{1,0:T(8,128)(2,1)S(1)} %add.3), channel_id=1, source_target_pairs={{8,12},{9,13},{10,14},{11,15},{24,28},{25,29},{26,30},{27,31}} | collective-permute-start | bytes 503816 | tf_op jit(solution)/shard_map/ppermute | solution.py:408
  21.5 7.9 %collective-permute-start.1 = (bf16[544,256]{1,0:T(8,128)(2,1)S(1)}, bf16[544,256]{1,0:T(8,128)(2,1)S(1)}, u32[]{:S(2)}, u32[]{:S(2)}) collective-permute-start(bf16[544,256]{1,0:T(8,128)(2,1)S(1)} %serve.1), channel_id=1, source_target_pairs={{0,4},{4,8},{8,12},{1,5},{5,9},{9,13},{2,6},{6,10},{10,14},{3,7},{... | collective-permute-start | bytes 835592 | tf_op jit(solution)/shard_map/ppermute | solution.py:354

commit v6 on v5

--- a/solution.py
+++ b/solution.py
@@ -15,12 +15,12 @@
 BF = jnp.bfloat16
 F32 = jnp.float32
 GRANT = 16 << 20
-LA = 1 << 30
-LB = 4 << 30
-SV = 1 << 30
+LA = 4194304000
+LB = 1048576000
+SV = 314572800
 PR = 1 << 30
-RL = 1 << 17
-FN = 2 << 30
+RL = 104857
+FN = 2097152000
 
 
 def feature_rows(width):
@@ -175,7 +175,7 @@
     softmax_parts(jobs)
 
 
-def serve_kernel(qb_ref, k_ref, v_ref, out_ref, *, behind):
+def serve_kernel(_, qb_ref, k_ref, v_ref, __, out_ref, *, behind):
     _, beyond = causal_masks()
     base = k_ref.shape[0] - WINDOW
     count = qb_ref.shape[1] // HEAD_DIM
@@ -402,45 +402,56 @@
             name="local",
         )(swa_query, swa_key, values, qft, kft)
 
+    local_a = local(0, LA)
+
+    def serve(asked):
+        return pl.pallas_call(
+            functools.partial(serve_kernel, behind=half),
+            out_shape=jax.ShapeDtypeStruct((WINDOW + 16 * (WINDOW // TILE), half * HEAD_DIM), BF),
+            in_specs=[vmem] * 5,
+            out_specs=vmem,
+            compiler_params=grant,
+            cost_estimate=pl.CostEstimate(flops=SV, bytes_accessed=1 << 20, transcendentals=1 << 10),
+            name="serve",
+        )(halo[0], asked, swa_key, values, local_a[4])
+
+    def relay(got, passed):
+        return pl.pallas_call(
+            relay_kernel,
+            out_shape=(jax.ShapeDtypeStruct(own.shape, BF), jax.ShapeDtypeStruct(passed.shape, BF)),
+            in_specs=[vmem] * 3,
+            out_specs=(vmem,) * 2,
+            input_output_aliases={2: 1},
+            compiler_params=grant,
+            cost_estimate=pl.CostEstimate(flops=RL, bytes_accessed=1 << 19, transcendentals=0),
+            name="relay",
+        )(own, got, passed)
+
     if count <= 4:
         running, prior = own, []
         for i in range(count - 1):
             got = lax.ppermute(running, "seq", [(i, i + 1)])
             prior.append(got)
-            running = own + got
             if i == 0:
+                halo_key = shifted(kp, "seq", 1)
                 asked = shifted(qb, "seq", -1)
-                running, vp = pl.pallas_call(
-                    relay_kernel,
-                    out_shape=(jax.ShapeDtypeStruct(own.shape, BF), jax.ShapeDtypeStruct(vp.shape, BF)),
-                    in_specs=[vmem] * 3,
-                    out_specs=(vmem,) * 2,
-                    input_output_aliases={2: 1},
-                    compiler_params=grant,
-                    cost_estimate=pl.CostEstimate(flops=RL, bytes_accessed=1 << 19, transcendentals=0),
-                    name="relay",
-                )(own, got, vp)
-                halo = shifted(kp, "seq", 1), shifted(vp, "seq", 1)
+                running, vp = relay(got, vp)
+                halo = halo_key, shifted(vp, "seq", 1)
+                answer = serve(asked)
+            elif i == 1:
+                running, answer = relay(got, answer)
+            else:
+                running = own + got
     else:
         running, prior, distance = own, [], 1
         halo = shifted(kp, "seq", 1), shifted(vp, "seq", 1)
-        asked = shifted(qb, "seq", -1)
+        answer = serve(shifted(qb, "seq", -1))
         while distance < count:
             got = shifted(running, "seq", distance)
             prior.append(got)
             running = running + got
             distance *= 2
 
-    local_a = local(0, LA)
-    answer = pl.pallas_call(
-        functools.partial(serve_kernel, behind=half),
-        out_shape=jax.ShapeDtypeStruct((WINDOW + 16 * (WINDOW // TILE), half * HEAD_DIM), BF),
-        in_specs=[vmem] * 3,
-        out_specs=vmem,
-        compiler_params=grant,
-        cost_estimate=pl.CostEstimate(flops=SV, bytes_accessed=1 << 20, transcendentals=1 << 10),
-        name="serve",
-    )(asked, swa_key, values)
     answered = shifted(answer, "seq", 1)
     local_b = local(half, LB)
 

time: 31.4 us -> 31 us (0.987)
    pallas_call x2 -> x3, Pallas kernels: 0.79 us -> 0.86 us  [the longest x1 0.75 us: serve(): pl.pallas_call(functools.partial(serve_kernel, behind=half), out_shape=ja...]
where the time goes in v6:
time: 31 us; the launch traced here: 30.8 us
  starting transfers between devices  15.8 us (51%)
  Pallas kernels  12.7 us (41%)
  waiting for transfers between devices  2.07 us (7%)
    ppermute x4, starting transfers between devices, shifted(): return lax.ppermute(value, axis, pairs)  9.55 us
    ppermute x3, starting transfers between devices, body(): got = lax.ppermute(running, 'seq', [(i, i + 1)])  6.3 us
    pallas_call x2, Pallas kernels, local(): pl.pallas_call(functools.partial(local_kernel, start_head=start_head, wid...  4.84 us
    pallas_call x1, Pallas kernels, body(): pl.pallas_call(functools.partial(first_final_kernel, heads=heads, width=w...  3.2 us
    pallas_call x1, Pallas kernels, body(): pl.pallas_call(functools.partial(prepare_kernel, heads=heads, width=width...  2.07 us
    ppermute x3, waiting for transfers between devices, body(): got = lax.ppermute(running, 'seq', [(i, i + 1)])  2.06 us
    pallas_call x1, Pallas kernels, body(): pl.pallas_call(last_final_kernel, out_shape=jax.ShapeDtypeStruct((tokens,...  1.69 us
    pallas_call x1, Pallas kernels, serve(): pl.pallas_call(functools.partial(serve_kernel, behind=half), out_shape=ja...  0.75 us
  transfers between devices with their start and end apart: 7, of which 1 were waited for; matrix products, arithmetic and copies ran while one was open for 0% of the time, Pallas kernels for 29%

profile of v6, /device:TPU:0, one launch (start us, length us, event | category | flops | bytes accessed | tf_op | source)
XLA Modules:
  0.0 30.8 jit_solution(14271477934642770170)
XLA Ops:
  0.0 2.1 %prepare.1 = (bf16[512,256]{1,0:T(8,128)(2,1)S(1)}, bf16[512,256]{1,0:T(8,128)(2,1)S(1)}, bf16[512,256]{1,0:T(8,128)(2,1)S(1)}, bf16[656,128]{1,0:T(8,128)(2,1)S(1)}, f32[3,640,256]{2,1,0:T(8,128)S(1)}) custom-call(bf16[64,1024]{1,0:T(8,128)(2,1)} %bitcast.3, bf16[1024,512]{1,0:T(8,128)(2,1)} %q_ref.5, bf16[1024,512]{1,0:T(8,128)(2,1)} %k_ref.5, ...), custom_call_target="tpu_custom_call" | custom-call | flops 1073741824 | bytes 3145728 | tf_op jit(solution)/shard_map/prepare/pallas_call | solution.py:371
  2.1 5.0 %collective-permute-start = (bf16[656,128]{1,0:T(8,128)(2,1)S(1)}, bf16[656,128]{1,0:T(8,128)(2,1)S(1)}, u32[]{:S(2)}, u32[]{:S(2)}) collective-permute-start(bf16[656,128]{1,0:T(8,128)(2,1)S(1)} %get-tuple-element.29.own_ref), channel_id=1, source_target_pairs={{0,4},{1,5},{2,6},{3,7},{16,20},{17,21},{18,22},{19,23}} | collective-permute-start | bytes 503816 | tf_op jit(solution)/shard_map/ppermute | solution.py:433
  7.1 1.3 %collective-permute-start.2 = (bf16[512,256]{1,0:T(8,128)(2,1)S(1)}, bf16[512,256]{1,0:T(8,128)(2,1)S(1)}, u32[]{:S(2)}, u32[]{:S(2)}) collective-permute-start(bf16[512,256]{1,0:T(8,128)(2,1)S(1)} %get-tuple-element.32), channel_id=1, source_target_pairs={{0,4},{4,8},{8,12},{1,5},{5,9},{9,13},{2,6},{6,10},{10,14},{3,7},{... | collective-permute-start | bytes 786440 | tf_op jit(solution)/shard_map/ppermute | solution.py:354
  8.4 1.3 %collective-permute-start.3 = (bf16[512,256]{1,0:T(8,128)(2,1)S(1)}, bf16[512,256]{1,0:T(8,128)(2,1)S(1)}, u32[]{:S(2)}, u32[]{:S(2)}) collective-permute-start(bf16[512,256]{1,0:T(8,128)(2,1)S(1)} %get-tuple-element.33), channel_id=1, source_target_pairs={{4,0},{8,4},{12,8},{5,1},{9,5},{13,9},{6,2},{10,6},{14,10},{7,3},{... | collective-permute-start | bytes 786440 | tf_op jit(solution)/shard_map/ppermute | solution.py:354
  9.7 2.1 %collective-permute-done.got_ref.refs_10_ = bf16[656,128]{1,0:T(8,128)(2,1)S(1)} collective-permute-done((bf16[656,128]{1,0:T(8,128)(2,1)S(1)}, bf16[656,128]{1,0:T(8,128)(2,1)S(1)}, u32[]{:S(2)}, u32[]{:S(2)}) %collective-permute-start) | collective-permute-done | bytes 167968 | tf_op jit(solution)/shard_map/ppermute | solution.py:433
  11.8 0.7 %collective-permute-start.1 = (bf16[656,128]{1,0:T(8,128)(2,1)S(1)}, bf16[656,128]{1,0:T(8,128)(2,1)S(1)}, u32[]{:S(2)}, u32[]{:S(2)}) collective-permute-start(bf16[656,128]{1,0:T(8,128)(2,1)S(1)} %get-tuple-element.31), channel_id=1, source_target_pairs={{4,8},{5,9},{6,10},{7,11},{20,24},{21,25},{22,26},{23,27}} | collective-permute-start | bytes 503816 | tf_op jit(solution)/shard_map/ppermute | solution.py:433
  12.4 5.0 %collective-permute-start.5 = (bf16[512,256]{1,0:T(8,128)(2,1)S(1)}, bf16[512,256]{1,0:T(8,128)(2,1)S(1)}, u32[]{:S(2)}, u32[]{:S(2)}) collective-permute-start(bf16[512,256]{1,0:T(8,128)(2,1)S(1)} %get-tuple-element.36), channel_id=1, source_target_pairs={{0,4},{4,8},{8,12},{1,5},{5,9},{9,13},{2,6},{6,10},{10,14},{3,7},{... | collective-permute-start | bytes 786440 | tf_op jit(solution)/shard_map/ppermute | solution.py:354
  17.5 0.0 copy-done
  17.5 0.0 copy-done.1
  17.5 0.0 copy-done.2
  17.5 2.4 %local.2 = (f32[1024,256]{1,0:T(8,128)S(1)}, f32[1024,256]{1,0:T(8,128)S(1)}, f32[1024,256]{1,0:T(8,128)S(1)}, f32[1024,256]{1,0:T(8,128)S(1)}, f32[512,256]{1,0...) custom-call(bf16[1024,512]{1,0:T(8,128)(2,1)S(1)} %copy-done, bf16[1024,512]{1,0:T(8,128)(2,1)S(1)} %copy-done.1, ...), custom_call_target="tpu_custom_call" | custom-call | flops 4194304000 | bytes 1048576 | tf_op jit(solution)/shard_map/local/pallas_call | solution.py:395
  20.0 0.0 collective-permute-done.2._.kp_ref
  20.0 0.0 collective-permute-done.3.qb_ref
  20.0 0.8 %serve.1._ = bf16[544,256]{1,0:T(8,128)(2,1)S(1)} custom-call(bf16[512,256]{1,0:T(8,128)(2,1)S(1)} %collective-permute-done.2._.kp_ref, bf16[512,256]{1,0:T(8,128)(2,1)S(1)} %collective-permute-done.3.qb_ref, bf16[1024,512]{1,0:T(8,128)(2,1)S(1)} %copy-done.1, bf16[1024,512]{1,0:T(8,128)(2,1)S(1)} %copy-done.2, f32[512,256]{1,0:T(8,128)S(1)} %get-tuple-element.34.__.top_ref), custom_call_target="tpu_custom_call" | custom-call | flops 314572800 | bytes 1048576 | tf_op jit(solution)/shard_map/serve/pallas_call | solution.py:408
  20.7 0.0 collective-permute-done.1.got_ref.refs_11_
  20.7 0.1 relay.3
  20.8 0.7 %collective-permute-start.6 = (bf16[656,128]{1,0:T(8,128)(2,1)S(1)}, bf16[656,128]{1,0:T(8,128)(2,1)S(1)}, u32[]{:S(2)}, u32[]{:S(2)}) collective-permute-start(bf16[656,128]{1,0:T(8,128)(2,1)S(1)} %get-tuple-element.47), channel_id=1, source_target_pairs={{8,12},{9,13},{10,14},{11,15},{24,28},{25,29},{26,30},{27,31}} | collective-permute-start | bytes 503816 | tf_op jit(solution)/shard_map/ppermute | solution.py:433
  21.5 1.9 %collective-permute-start.4 = (bf16[544,256]{1,0:T(8,128)(2,1)S(1)}, bf16[544,256]{1,0:T(8,128)(2,1)S(1)}, u32[]{:S(2)}, u32[]{:S(2)}) collective-permute-start(bf16[544,256]{1,0:T(8,128)(2,1)S(1)} %get-tuple-element.35), channel_id=1, source_target_pairs={{0,4},{4,8},{8,12},{1,5},{5,9},{9,13},{2,6},{6,10},{10,14},{3,7},{... | collective-permute-start | bytes 835592 | tf_op jit(solution)/shard_map/ppermute | solution.py:354
  23.4 2.4 %local.3 = (f32[1024,256]{1,0:T(8,128)S(1)}, f32[1024,256]{1,0:T(8,128)S(1)}, f32[1024,256]{1,0:T(8,128)S(1)}, f32[1024,256]{1,0:T(8,128)S(1)}, f32[512,256]{1,0...) custom-call(bf16[1024,512]{1,0:T(8,128)(2,1)S(1)} %copy-done, bf16[1024,512]{1,0:T(8,128)(2,1)S(1)} %copy-done.1, ...), custom_call_target="tpu_custom_call" | custom-call | flops 1048576000 | bytes 1048576 | tf_op jit(solution)/shard_map/local/pallas_call | solution.py:395
  25.8 0.0 collective-permute-done.5.vp_ref
  25.9 0.0 collective-permute-done.6.refs_12_
  25.9 3.2 %final.1 = (bf16[1024,512]{1,0:T(8,128)(2,1)}, f32[512,256]{1,0:T(8,128)S(1)}, f32[1,256]{1,0:T(1,128)S(1)}) custom-call(bf16[1024,512]{1,0:T(8,128)(2,1)S(1)} %copy-done, bf16[512,256]{1,0:T(8,128)(2,1)S(1)} %collective-permute-done.2._.kp_ref, bf16[512,256]{1,0:T(8,128)(2,1)S(1)} %collective-permute-done.5.vp_ref, ...), custom_call_target="tpu_custom_call" | custom-call | flops 2097152000 | bytes 12582912 | tf_op jit(solution)/shard_map/final/pallas_call | solution.py:463
  29.1 0.0 collective-permute-done.4.ob_ref
  29.1 1.7 %last.1 = bf16[1024,512]{1,0:T(8,128)(2,1)} custom-call(bf16[544,256]{1,0:T(8,128)(2,1)S(1)} %collective-permute-done.4.ob_ref, f32[512,256]{1,0:T(8,128)S(1)} %get-tuple-element.49.lin_ref, f32[1024,256]{1,0:T(8,128)S(1)} %get-tuple-element.44.refs_7_.win_ref, f32[1024,256]{1,0:T(8,128)S(1)} %get-tuple-element.45.refs_8_.sum_ref, ...), custom_call_target="tpu_custom_call", output_to_operand_aliasing={{}: (6, {})} | custom-call | flops 1048576 | bytes 3145728 | tf_op jit(solution)/shard_map/last/pallas_call | solution.py:483
  (8 shorter events, 0.1 us)
Async XLA Ops:
  0.0 17.5 %copy-start = (bf16[1024,512]{1,0:T(8,128)(2,1)S(1)}, bf16[1024,512]{1,0:T(8,128)(2,1)}, u32[]{:S(2)}) copy-start(bf16[1024,512]{1,0:T(8,128)(2,1)} %q_ref.5) | copy-start | bytes 3145732
  0.0 17.5 %copy-start.1 = (bf16[1024,512]{1,0:T(8,128)(2,1)S(1)}, bf16[1024,512]{1,0:T(8,128)(2,1)}, u32[]{:S(2)}) copy-start(bf16[1024,512]{1,0:T(8,128)(2,1)} %k_ref.5) | copy-start | bytes 3145732
  0.0 17.5 %copy-start.2 = (bf16[1024,512]{1,0:T(8,128)(2,1)S(1)}, bf16[1024,512]{1,0:T(8,128)(2,1)}, u32[]{:S(2)}) copy-start(bf16[1024,512]{1,0:T(8,128)(2,1)} %v_ref.5) | copy-start | bytes 3145732
  0.0 17.5 %copy-start.3 = (bf16[1024,64]{0,1:T(8,128)(2,1)S(1)}, bf16[1024,64]{0,1:T(8,128)(2,1)}, u32[]{:S(2)}) copy-start(bf16[1024,64]{0,1:T(8,128)(2,1)} %param.7) | copy-start | bytes 393220
  0.0 17.5 %copy-start.4 = (bf16[1024,64]{0,1:T(8,128)(2,1)S(1)}, bf16[1024,64]{0,1:T(8,128)(2,1)}, u32[]{:S(2)}) copy-start(bf16[1024,64]{0,1:T(8,128)(2,1)} %param.6) | copy-start | bytes 393220
  2.1 9.6 %collective-permute-start = (bf16[656,128]{1,0:T(8,128)(2,1)S(1)}, bf16[656,128]{1,0:T(8,128)(2,1)S(1)}, u32[]{:S(2)}, u32[]{:S(2)}) collective-permute-start(bf16[656,128]{1,0:T(8,128)(2,1)S(1)} %get-tuple-element.29.own_ref), channel_id=1, source_target_pairs={{0,4},{1,5},{2,6},{3,7},{16,20},{17,21},{18,22},{19,23}} | collective-permute-start | bytes 503816 | tf_op jit(solution)/shard_map/ppermute | solution.py:433
  7.1 12.9 %collective-permute-start.2 = (bf16[512,256]{1,0:T(8,128)(2,1)S(1)}, bf16[512,256]{1,0:T(8,128)(2,1)S(1)}, u32[]{:S(2)}, u32[]{:S(2)}) collective-permute-start(bf16[512,256]{1,0:T(8,128)(2,1)S(1)} %get-tuple-element.32), channel_id=1, source_target_pairs={{0,4},{4,8},{8,12},{1,5},{5,9},{9,13},{2,6},{6,10},{10,14},{3,7},{... | collective-permute-start | bytes 786440 | tf_op jit(solution)/shard_map/ppermute | solution.py:354
  8.4 11.6 %collective-permute-start.3 = (bf16[512,256]{1,0:T(8,128)(2,1)S(1)}, bf16[512,256]{1,0:T(8,128)(2,1)S(1)}, u32[]{:S(2)}, u32[]{:S(2)}) collective-permute-start(bf16[512,256]{1,0:T(8,128)(2,1)S(1)} %get-tuple-element.33), channel_id=1, source_target_pairs={{4,0},{8,4},{12,8},{5,1},{9,5},{13,9},{6,2},{10,6},{14,10},{7,3},{... | collective-permute-start | bytes 786440 | tf_op jit(solution)/shard_map/ppermute | solution.py:354
  11.8 9.0 %collective-permute-start.1 = (bf16[656,128]{1,0:T(8,128)(2,1)S(1)}, bf16[656,128]{1,0:T(8,128)(2,1)S(1)}, u32[]{:S(2)}, u32[]{:S(2)}) collective-permute-start(bf16[656,128]{1,0:T(8,128)(2,1)S(1)} %get-tuple-element.31), channel_id=1, source_target_pairs={{4,8},{5,9},{6,10},{7,11},{20,24},{21,25},{22,26},{23,27}} | collective-permute-start | bytes 503816 | tf_op jit(solution)/shard_map/ppermute | solution.py:433
  12.4 13.4 %collective-permute-start.5 = (bf16[512,256]{1,0:T(8,128)(2,1)S(1)}, bf16[512,256]{1,0:T(8,128)(2,1)S(1)}, u32[]{:S(2)}, u32[]{:S(2)}) collective-permute-start(bf16[512,256]{1,0:T(8,128)(2,1)S(1)} %get-tuple-element.36), channel_id=1, source_target_pairs={{0,4},{4,8},{8,12},{1,5},{5,9},{9,13},{2,6},{6,10},{10,14},{3,7},{... | collective-permute-start | bytes 786440 | tf_op jit(solution)/shard_map/ppermute | solution.py:354
  20.8 5.0 %collective-permute-start.6 = (bf16[656,128]{1,0:T(8,128)(2,1)S(1)}, bf16[656,128]{1,0:T(8,128)(2,1)S(1)}, u32[]{:S(2)}, u32[]{:S(2)}) collective-permute-start(bf16[656,128]{1,0:T(8,128)(2,1)S(1)} %get-tuple-element.47), channel_id=1, source_target_pairs={{8,12},{9,13},{10,14},{11,15},{24,28},{25,29},{26,30},{27,31}} | collective-permute-start | bytes 503816 | tf_op jit(solution)/shard_map/ppermute | solution.py:433
  21.5 7.6 %collective-permute-start.4 = (bf16[544,256]{1,0:T(8,128)(2,1)S(1)}, bf16[544,256]{1,0:T(8,128)(2,1)S(1)}, u32[]{:S(2)}, u32[]{:S(2)}) collective-permute-start(bf16[544,256]{1,0:T(8,128)(2,1)S(1)} %get-tuple-element.35), channel_id=1, source_target_pairs={{0,4},{4,8},{8,12},{1,5},{5,9},{9,13},{2,6},{6,10},{10,14},{3,7},{... | collective-permute-start | bytes 835592 | tf_op jit(solution)/shard_map/ppermute | solution.py:354

commit v7 on v6

--- a/solution.py
+++ b/solution.py
@@ -10,7 +10,7 @@
 HEAD_DIM = 128
 WINDOW = 512
 TILE = 256
-NEG = -1e30
+NEG = -(2.0**100)
 SCALE = HEAD_DIM ** (-0.5) * 1.4426950408889634
 BF = jnp.bfloat16
 F32 = jnp.float32
@@ -29,6 +29,10 @@
 
 def state_rows(heads, width):
     return heads * feature_rows(width) + 16
+
+
+def answer_rows(heads):
+    return -(-4 * heads * (WINDOW // TILE) // 16) * 16
 
 
 def nt(a, b):
@@ -116,7 +120,7 @@
     kp_ref[:16, :] = jnp.where(row == 0, jnp.ones((), BF), top)
 
 
-def softmax_parts(jobs, ahead=2):
+def softmax_parts(jobs, ahead=2, coarse=False):
     scores = []
     for i in range(len(jobs)):
         while len(scores) < min(len(jobs), i + 1 + ahead):
@@ -130,6 +134,8 @@
         if last is not None:
             parts[-1] = jnp.where(last, parts[-1], NEG)
         top = jnp.max(functools.reduce(jnp.maximum, parts), 1, keepdims=True)
+        if coarse:
+            top = top.astype(BF).astype(F32)
         p = jnp.concatenate([jnp.exp2((part - top) * SCALE).astype(BF) for part in parts], 1)
         acc = nn(p, with_ones(value()))
         use(top, acc[:, :HEAD_DIM], acc[:, HEAD_DIM:])
@@ -199,15 +205,17 @@
     for start in range(0, WINDOW, TILE):
         for g in range(count):
             job(start, g)
-    softmax_parts(jobs)
-    for i, stat in enumerate(stats):
+    softmax_parts(jobs, coarse=True)
+    rows = []
+    for stat in stats:
         stat = stat.T[: 2 * count]
-        high = stat.astype(BF).astype(F32)
-        middle = (stat - high).astype(BF).astype(F32)
-        low = stat - high - middle
-        pad = jnp.ones((16 - 6 * count, TILE), F32)
-        rows = jnp.concatenate([high, middle, low, pad], 0)
-        out_ref[WINDOW + 16 * i : WINDOW + 16 * (i + 1), :] = rows.astype(BF)
+        top, total = stat[:count], stat[count:]
+        high = total.astype(BF).astype(F32)
+        middle = (total - high).astype(BF).astype(F32)
+        rows += [top, high, middle, total - high - middle]
+    rows.append(jnp.zeros((out_ref.shape[0] - WINDOW - 4 * count * len(stats), TILE), F32))
+    rows = [part for part in rows if part.shape[0]]
+    out_ref[WINDOW:, :] = jnp.concatenate(rows, 0).astype(BF)
 
 
 def merged(window, mine, total, top, out, count, later):
@@ -313,13 +321,13 @@
 def last_final_kernel(ob_ref, lin_ref, win_ref, sum_ref, top_ref, gain_ref, _, out_hbm, out_ref, sems):
     count = lin_ref.shape[1] // HEAD_DIM
     ahead = out_hbm.shape[1] - count * HEAD_DIM
-    later = ob_ref[WINDOW + 15 : WINDOW + 16, :1].astype(F32) > 0
     stats = []
     n = 2 * count
+    got = ob_ref[WINDOW:, :].astype(F32)
     for i in range(WINDOW // TILE):
-        got = ob_ref[WINDOW + 16 * i : WINDOW + 16 * (i + 1), :].astype(F32)
-        stats.append(got[:n] + got[n : 2 * n] + got[2 * n : 3 * n])
-    stats.append(jnp.zeros((HEAD_DIM - n * len(stats), TILE), F32))
+        top, high, middle, low = (got[(4 * i + j) * count : (4 * i + j + 1) * count] for j in range(4))
+        stats += [top, high + middle + low]
+    stats.append(jnp.zeros((HEAD_DIM - count * len(stats), TILE), F32))
     stats = jnp.concatenate(stats, 0).T
     parts = [(start, g) for start in range(0, WINDOW, TILE) for g in range(count)]
 
@@ -333,7 +341,10 @@
     windows = []
     for start, g in parts:
         at = place(start, g)
-        windows.append(merged(win_ref[at], top_ref[at], sum_ref[at], stat(start, g), ob_ref[at].astype(F32), stat(start, count + g), later))
+        total = stat(start, count + g)
+        windows.append(
+            merged(win_ref[at], top_ref[at], sum_ref[at], stat(start, g), ob_ref[at].astype(F32), total, total > 0)
+        )
     mixed = [lin_ref[place(*part)] + window / total for part, (window, total) in zip(parts, windows)]
     powers = [power_of(m) for m in mixed]
     for part, m, power in zip(parts, mixed, powers):
@@ -407,7 +418,7 @@
     def serve(asked):
         return pl.pallas_call(
             functools.partial(serve_kernel, behind=half),
-            out_shape=jax.ShapeDtypeStruct((WINDOW + 16 * (WINDOW // TILE), half * HEAD_DIM), BF),
+            out_shape=jax.ShapeDtypeStruct((WINDOW + answer_rows(half), half * HEAD_DIM), BF),
             in_specs=[vmem] * 5,
             out_specs=vmem,
             compiler_params=grant,

time: 31 us -> 31 us (level)
  no operation moved by 1% of the time
where the time goes in v7:
time: 31 us; the launch traced here: 30.7 us
  starting transfers between devices  15.8 us (51%)
  Pallas kernels  12.6 us (41%)
  waiting for transfers between devices  2.07 us (7%)
    ppermute x4, starting transfers between devices, shifted(): return lax.ppermute(value, axis, pairs)  9.55 us
    ppermute x3, starting transfers between devices, body(): got = lax.ppermute(running, 'seq', [(i, i + 1)])  6.3 us
    pallas_call x2, Pallas kernels, local(): pl.pallas_call(functools.partial(local_kernel, start_head=start_head, wid...  4.8 us
    pallas_call x1, Pallas kernels, body(): pl.pallas_call(functools.partial(first_final_kernel, heads=heads, width=w...  3.38 us
    pallas_call x1, Pallas kernels, body(): pl.pallas_call(functools.partial(prepare_kernel, heads=heads, width=width...  2.07 us
    ppermute x3, waiting for transfers between devices, body(): got = lax.ppermute(running, 'seq', [(i, i + 1)])  2.06 us
    pallas_call x1, Pallas kernels, body(): pl.pallas_call(last_final_kernel, out_shape=jax.ShapeDtypeStruct((tokens,...  1.53 us
    pallas_call x1, Pallas kernels, serve(): pl.pallas_call(functools.partial(serve_kernel, behind=half), out_shape=ja...  0.75 us
  transfers between devices with their start and end apart: 7, of which 1 were waited for; matrix products, arithmetic and copies ran while one was open for 0% of the time, Pallas kernels for 29%

profile of v7, /device:TPU:0, one launch (start us, length us, event | category | flops | bytes accessed | tf_op | source)
XLA Modules:
  0.0 30.7 jit_solution(12846787954008045366)
XLA Ops:
  0.0 2.1 %prepare.1 = (bf16[512,256]{1,0:T(8,128)(2,1)S(1)}, bf16[512,256]{1,0:T(8,128)(2,1)S(1)}, bf16[512,256]{1,0:T(8,128)(2,1)S(1)}, bf16[656,128]{1,0:T(8,128)(2,1)S(1)}, f32[3,640,256]{2,1,0:T(8,128)S(1)}) custom-call(bf16[64,1024]{1,0:T(8,128)(2,1)} %bitcast.3, bf16[1024,512]{1,0:T(8,128)(2,1)} %q_ref.5, bf16[1024,512]{1,0:T(8,128)(2,1)} %k_ref.5, ...), custom_call_target="tpu_custom_call" | custom-call | flops 1073741824 | bytes 3145728 | tf_op jit(solution)/shard_map/prepare/pallas_call | solution.py:382
  2.1 5.0 %collective-permute-start = (bf16[656,128]{1,0:T(8,128)(2,1)S(1)}, bf16[656,128]{1,0:T(8,128)(2,1)S(1)}, u32[]{:S(2)}, u32[]{:S(2)}) collective-permute-start(bf16[656,128]{1,0:T(8,128)(2,1)S(1)} %get-tuple-element.29.own_ref), channel_id=1, source_target_pairs={{0,4},{1,5},{2,6},{3,7},{16,20},{17,21},{18,22},{19,23}} | collective-permute-start | bytes 503816 | tf_op jit(solution)/shard_map/ppermute | solution.py:444
  7.1 1.3 %collective-permute-start.2 = (bf16[512,256]{1,0:T(8,128)(2,1)S(1)}, bf16[512,256]{1,0:T(8,128)(2,1)S(1)}, u32[]{:S(2)}, u32[]{:S(2)}) collective-permute-start(bf16[512,256]{1,0:T(8,128)(2,1)S(1)} %get-tuple-element.32), channel_id=1, source_target_pairs={{0,4},{4,8},{8,12},{1,5},{5,9},{9,13},{2,6},{6,10},{10,14},{3,7},{... | collective-permute-start | bytes 786440 | tf_op jit(solution)/shard_map/ppermute | solution.py:365
  8.4 1.3 %collective-permute-start.3 = (bf16[512,256]{1,0:T(8,128)(2,1)S(1)}, bf16[512,256]{1,0:T(8,128)(2,1)S(1)}, u32[]{:S(2)}, u32[]{:S(2)}) collective-permute-start(bf16[512,256]{1,0:T(8,128)(2,1)S(1)} %get-tuple-element.33), channel_id=1, source_target_pairs={{4,0},{8,4},{12,8},{5,1},{9,5},{13,9},{6,2},{10,6},{14,10},{7,3},{... | collective-permute-start | bytes 786440 | tf_op jit(solution)/shard_map/ppermute | solution.py:365
  9.7 2.1 %collective-permute-done.got_ref.refs_10_ = bf16[656,128]{1,0:T(8,128)(2,1)S(1)} collective-permute-done((bf16[656,128]{1,0:T(8,128)(2,1)S(1)}, bf16[656,128]{1,0:T(8,128)(2,1)S(1)}, u32[]{:S(2)}, u32[]{:S(2)}) %collective-permute-start) | collective-permute-done | bytes 167968 | tf_op jit(solution)/shard_map/ppermute | solution.py:444
  11.8 0.7 %collective-permute-start.1 = (bf16[656,128]{1,0:T(8,128)(2,1)S(1)}, bf16[656,128]{1,0:T(8,128)(2,1)S(1)}, u32[]{:S(2)}, u32[]{:S(2)}) collective-permute-start(bf16[656,128]{1,0:T(8,128)(2,1)S(1)} %get-tuple-element.31), channel_id=1, source_target_pairs={{4,8},{5,9},{6,10},{7,11},{20,24},{21,25},{22,26},{23,27}} | collective-permute-start | bytes 503816 | tf_op jit(solution)/shard_map/ppermute | solution.py:444
  12.4 5.0 %collective-permute-start.5 = (bf16[512,256]{1,0:T(8,128)(2,1)S(1)}, bf16[512,256]{1,0:T(8,128)(2,1)S(1)}, u32[]{:S(2)}, u32[]{:S(2)}) collective-permute-start(bf16[512,256]{1,0:T(8,128)(2,1)S(1)} %get-tuple-element.36), channel_id=1, source_target_pairs={{0,4},{4,8},{8,12},{1,5},{5,9},{9,13},{2,6},{6,10},{10,14},{3,7},{... | collective-permute-start | bytes 786440 | tf_op jit(solution)/shard_map/ppermute | solution.py:365
  17.5 0.0 copy-done
  17.5 0.0 copy-done.1
  17.5 0.0 copy-done.2
  17.5 2.4 %local.2 = (f32[1024,256]{1,0:T(8,128)S(1)}, f32[1024,256]{1,0:T(8,128)S(1)}, f32[1024,256]{1,0:T(8,128)S(1)}, f32[1024,256]{1,0:T(8,128)S(1)}, f32[512,256]{1,0...) custom-call(bf16[1024,512]{1,0:T(8,128)(2,1)S(1)} %copy-done, bf16[1024,512]{1,0:T(8,128)(2,1)S(1)} %copy-done.1, ...), custom_call_target="tpu_custom_call" | custom-call | flops 4194304000 | bytes 1048576 | tf_op jit(solution)/shard_map/local/pallas_call | solution.py:406
  19.9 0.0 collective-permute-done.2._.kp_ref
  19.9 0.0 collective-permute-done.3.qb_ref
  20.0 0.7 %serve.1._ = bf16[528,256]{1,0:T(8,128)(2,1)S(1)} custom-call(bf16[512,256]{1,0:T(8,128)(2,1)S(1)} %collective-permute-done.2._.kp_ref, bf16[512,256]{1,0:T(8,128)(2,1)S(1)} %collective-permute-done.3.qb_ref, bf16[1024,512]{1,0:T(8,128)(2,1)S(1)} %copy-done.1, bf16[1024,512]{1,0:T(8,128)(2,1)S(1)} %copy-done.2, f32[512,256]{1,0:T(8,128)S(1)} %get-tuple-element.34.__.top_ref), custom_call_target="tpu_custom_call" | custom-call | flops 314572800 | bytes 1048576 | tf_op jit(solution)/shard_map/serve/pallas_call | solution.py:419
  20.7 0.0 collective-permute-done.1.got_ref.refs_11_
  20.7 0.1 relay.3
  20.8 0.7 %collective-permute-start.6 = (bf16[656,128]{1,0:T(8,128)(2,1)S(1)}, bf16[656,128]{1,0:T(8,128)(2,1)S(1)}, u32[]{:S(2)}, u32[]{:S(2)}) collective-permute-start(bf16[656,128]{1,0:T(8,128)(2,1)S(1)} %get-tuple-element.47), channel_id=1, source_target_pairs={{8,12},{9,13},{10,14},{11,15},{24,28},{25,29},{26,30},{27,31}} | collective-permute-start | bytes 503816 | tf_op jit(solution)/shard_map/ppermute | solution.py:444
  21.5 1.9 %collective-permute-start.4 = (bf16[528,256]{1,0:T(8,128)(2,1)S(1)}, bf16[528,256]{1,0:T(8,128)(2,1)S(1)}, u32[]{:S(2)}, u32[]{:S(2)}) collective-permute-start(bf16[528,256]{1,0:T(8,128)(2,1)S(1)} %get-tuple-element.35), channel_id=1, source_target_pairs={{0,4},{4,8},{8,12},{1,5},{5,9},{9,13},{2,6},{6,10},{10,14},{3,7},{... | collective-permute-start | bytes 811016 | tf_op jit(solution)/shard_map/ppermute | solution.py:365
  23.4 2.4 %local.3 = (f32[1024,256]{1,0:T(8,128)S(1)}, f32[1024,256]{1,0:T(8,128)S(1)}, f32[1024,256]{1,0:T(8,128)S(1)}, f32[1024,256]{1,0:T(8,128)S(1)}, f32[512,256]{1,0...) custom-call(bf16[1024,512]{1,0:T(8,128)(2,1)S(1)} %copy-done, bf16[1024,512]{1,0:T(8,128)(2,1)S(1)} %copy-done.1, ...), custom_call_target="tpu_custom_call" | custom-call | flops 1048576000 | bytes 1048576 | tf_op jit(solution)/shard_map/local/pallas_call | solution.py:406
  25.8 0.0 collective-permute-done.5.vp_ref
  25.8 0.0 collective-permute-done.6.refs_12_
  25.8 3.4 %final.1 = (bf16[1024,512]{1,0:T(8,128)(2,1)}, f32[512,256]{1,0:T(8,128)S(1)}, f32[1,256]{1,0:T(1,128)S(1)}) custom-call(bf16[1024,512]{1,0:T(8,128)(2,1)S(1)} %copy-done, bf16[512,256]{1,0:T(8,128)(2,1)S(1)} %collective-permute-done.2._.kp_ref, bf16[512,256]{1,0:T(8,128)(2,1)S(1)} %collective-permute-done.5.vp_ref, ...), custom_call_target="tpu_custom_call" | custom-call | flops 2097152000 | bytes 12582912 | tf_op jit(solution)/shard_map/final/pallas_call | solution.py:474
  29.2 0.0 collective-permute-done.4.ob_ref
  29.2 1.5 %last.1 = bf16[1024,512]{1,0:T(8,128)(2,1)} custom-call(bf16[528,256]{1,0:T(8,128)(2,1)S(1)} %collective-permute-done.4.ob_ref, f32[512,256]{1,0:T(8,128)S(1)} %get-tuple-element.49.lin_ref, f32[1024,256]{1,0:T(8,128)S(1)} %get-tuple-element.44.refs_7_.win_ref, f32[1024,256]{1,0:T(8,128)S(1)} %get-tuple-element.45.refs_8_.sum_ref, ...), custom_call_target="tpu_custom_call", output_to_operand_aliasing={{}: (6, {})} | custom-call | flops 1048576 | bytes 3145728 | tf_op jit(solution)/shard_map/last/pallas_call | solution.py:494
  (8 shorter events, 0.1 us)
Async XLA Ops:
  0.0 17.5 %copy-start = (bf16[1024,512]{1,0:T(8,128)(2,1)S(1)}, bf16[1024,512]{1,0:T(8,128)(2,1)}, u32[]{:S(2)}) copy-start(bf16[1024,512]{1,0:T(8,128)(2,1)} %q_ref.5) | copy-start | bytes 3145732
  0.0 17.5 %copy-start.1 = (bf16[1024,512]{1,0:T(8,128)(2,1)S(1)}, bf16[1024,512]{1,0:T(8,128)(2,1)}, u32[]{:S(2)}) copy-start(bf16[1024,512]{1,0:T(8,128)(2,1)} %k_ref.5) | copy-start | bytes 3145732
  0.0 17.5 %copy-start.2 = (bf16[1024,512]{1,0:T(8,128)(2,1)S(1)}, bf16[1024,512]{1,0:T(8,128)(2,1)}, u32[]{:S(2)}) copy-start(bf16[1024,512]{1,0:T(8,128)(2,1)} %v_ref.5) | copy-start | bytes 3145732
  0.0 17.5 %copy-start.3 = (bf16[1024,64]{0,1:T(8,128)(2,1)S(1)}, bf16[1024,64]{0,1:T(8,128)(2,1)}, u32[]{:S(2)}) copy-start(bf16[1024,64]{0,1:T(8,128)(2,1)} %param.7) | copy-start | bytes 393220
  0.0 17.5 %copy-start.4 = (bf16[1024,64]{0,1:T(8,128)(2,1)S(1)}, bf16[1024,64]{0,1:T(8,128)(2,1)}, u32[]{:S(2)}) copy-start(bf16[1024,64]{0,1:T(8,128)(2,1)} %param.6) | copy-start | bytes 393220
  2.1 9.6 %collective-permute-start = (bf16[656,128]{1,0:T(8,128)(2,1)S(1)}, bf16[656,128]{1,0:T(8,128)(2,1)S(1)}, u32[]{:S(2)}, u32[]{:S(2)}) collective-permute-start(bf16[656,128]{1,0:T(8,128)(2,1)S(1)} %get-tuple-element.29.own_ref), channel_id=1, source_target_pairs={{0,4},{1,5},{2,6},{3,7},{16,20},{17,21},{18,22},{19,23}} | collective-permute-start | bytes 503816 | tf_op jit(solution)/shard_map/ppermute | solution.py:444
  7.1 12.9 %collective-permute-start.2 = (bf16[512,256]{1,0:T(8,128)(2,1)S(1)}, bf16[512,256]{1,0:T(8,128)(2,1)S(1)}, u32[]{:S(2)}, u32[]{:S(2)}) collective-permute-start(bf16[512,256]{1,0:T(8,128)(2,1)S(1)} %get-tuple-element.32), channel_id=1, source_target_pairs={{0,4},{4,8},{8,12},{1,5},{5,9},{9,13},{2,6},{6,10},{10,14},{3,7},{... | collective-permute-start | bytes 786440 | tf_op jit(solution)/shard_map/ppermute | solution.py:365
  8.4 11.6 %collective-permute-start.3 = (bf16[512,256]{1,0:T(8,128)(2,1)S(1)}, bf16[512,256]{1,0:T(8,128)(2,1)S(1)}, u32[]{:S(2)}, u32[]{:S(2)}) collective-permute-start(bf16[512,256]{1,0:T(8,128)(2,1)S(1)} %get-tuple-element.33), channel_id=1, source_target_pairs={{4,0},{8,4},{12,8},{5,1},{9,5},{13,9},{6,2},{10,6},{14,10},{7,3},{... | collective-permute-start | bytes 786440 | tf_op jit(solution)/shard_map/ppermute | solution.py:365
  11.8 8.9 %collective-permute-start.1 = (bf16[656,128]{1,0:T(8,128)(2,1)S(1)}, bf16[656,128]{1,0:T(8,128)(2,1)S(1)}, u32[]{:S(2)}, u32[]{:S(2)}) collective-permute-start(bf16[656,128]{1,0:T(8,128)(2,1)S(1)} %get-tuple-element.31), channel_id=1, source_target_pairs={{4,8},{5,9},{6,10},{7,11},{20,24},{21,25},{22,26},{23,27}} | collective-permute-start | bytes 503816 | tf_op jit(solution)/shard_map/ppermute | solution.py:444
  12.4 13.4 %collective-permute-start.5 = (bf16[512,256]{1,0:T(8,128)(2,1)S(1)}, bf16[512,256]{1,0:T(8,128)(2,1)S(1)}, u32[]{:S(2)}, u32[]{:S(2)}) collective-permute-start(bf16[512,256]{1,0:T(8,128)(2,1)S(1)} %get-tuple-element.36), channel_id=1, source_target_pairs={{0,4},{4,8},{8,12},{1,5},{5,9},{9,13},{2,6},{6,10},{10,14},{3,7},{... | collective-permute-start | bytes 786440 | tf_op jit(solution)/shard_map/ppermute | solution.py:365
  20.8 5.0 %collective-permute-start.6 = (bf16[656,128]{1,0:T(8,128)(2,1)S(1)}, bf16[656,128]{1,0:T(8,128)(2,1)S(1)}, u32[]{:S(2)}, u32[]{:S(2)}) collective-permute-start(bf16[656,128]{1,0:T(8,128)(2,1)S(1)} %get-tuple-element.47), channel_id=1, source_target_pairs={{8,12},{9,13},{10,14},{11,15},{24,28},{25,29},{26,30},{27,31}} | collective-permute-start | bytes 503816 | tf_op jit(solution)/shard_map/ppermute | solution.py:444
  21.5 7.7 %collective-permute-start.4 = (bf16[528,256]{1,0:T(8,128)(2,1)S(1)}, bf16[528,256]{1,0:T(8,128)(2,1)S(1)}, u32[]{:S(2)}, u32[]{:S(2)}) collective-permute-start(bf16[528,256]{1,0:T(8,128)(2,1)S(1)} %get-tuple-element.35), channel_id=1, source_target_pairs={{0,4},{4,8},{8,12},{1,5},{5,9},{9,13},{2,6},{6,10},{10,14},{3,7},{... | collective-permute-start | bytes 811016 | tf_op jit(solution)/shard_map/ppermute | solution.py:365

commit v8 on v7

--- a/solution.py
+++ b/solution.py
@@ -28,7 +28,7 @@
 
 
 def state_rows(heads, width):
-    return heads * feature_rows(width) + 16
+    return heads * feature_rows(width)
 
 
 def answer_rows(heads):
@@ -81,7 +81,6 @@
 
 def prepare_kernel(kf_hbm, q_hbm, k_hbm, v_hbm, kp_ref, vp_ref, qb_ref, own_ref, before_ref, kf_ref, v_ref, sems, *, heads, width):
     feats = feature_rows(width)
-    base = heads * feats
     tokens = v_ref.shape[0]
     ahead = heads // 2 * HEAD_DIM
     tail = pl.ds(tokens - WINDOW, WINDOW)
@@ -112,7 +111,10 @@
         own_ref[h * feats : (h + 1) * feats, :] = total[:, :HEAD_DIM].astype(BF)
         norms = jnp.where(lane == h, total[:, HEAD_DIM:], norms)
     norms = jnp.concatenate([norms, jnp.zeros((2 * HEAD_DIM - feats, HEAD_DIM), F32)], 0).T[:8]
-    own_ref[base:, :] = jnp.concatenate([norms[:, :HEAD_DIM], norms[:, HEAD_DIM:]], 0).astype(BF)
+    for h in range(heads):
+        spare = (h + 1) * feats - 2
+        own_ref[spare : spare + 1, :] = norms[h : h + 1, :HEAD_DIM].astype(BF)
+        own_ref[spare + 1 : spare + 2, :] = norms[h : h + 1, HEAD_DIM:].astype(BF)
     for copy in copies:
         copy.wait()
     top = kp_ref[:16, :]
@@ -263,19 +265,19 @@
     count = heads // 2
     tokens = halves[0][0].shape[0]
     feats = feature_rows(width)
-    base = heads * feats
     fetch = pltpu.make_async_copy(gain_hbm, gain_ref, sems.at[heads])
     fetch.start()
 
     def prior(rows):
         return functools.reduce(jnp.add, [ref[rows, :].astype(F32) for ref in prior_refs])
 
-    tail = jnp.concatenate([prior(slice(base, base + 16)), jnp.zeros((HEAD_DIM - 16, HEAD_DIM), F32)], 0).T
+    tail = [prior(slice((h + 1) * feats - 16, (h + 1) * feats)) for h in range(heads)]
+    tail = jnp.concatenate(tail + [jnp.zeros((HEAD_DIM - 16 * heads, HEAD_DIM), F32)], 0).T
 
     def state(h):
         norm = [
-            jnp.broadcast_to(tail[:, h : h + 1], (HEAD_DIM, HEAD_DIM)),
-            jnp.broadcast_to(tail[: feats - HEAD_DIM, 8 + h : 9 + h], (feats - HEAD_DIM, HEAD_DIM)),
+            jnp.broadcast_to(tail[:, 16 * h + 14 : 16 * h + 15], (HEAD_DIM, HEAD_DIM)),
+            jnp.broadcast_to(tail[: feats - HEAD_DIM, 16 * h + 15 : 16 * h + 16], (feats - HEAD_DIM, HEAD_DIM)),
         ]
         return jnp.concatenate([prior(slice(h * feats, (h + 1) * feats)), jnp.concatenate(norm, 0)], 1)
 

time: 31 us -> 30.9 us (level)
  transfers between devices with their start and end apart: 7 -> 7, of which waited for: 1 -> 1; matrix products, arithmetic and copies ran while one was open for 0% -> 0% of each run, Pallas kernels for 29% -> 30%
where the time goes in v8:
time: 30.9 us; the launch traced here: 30.7 us
  starting transfers between devices  15.8 us (51%)
  Pallas kernels  12.6 us (41%)
  waiting for transfers between devices  1.98 us (6%)
    ppermute x4, starting transfers between devices, shifted(): return lax.ppermute(value, axis, pairs)  9.55 us
    ppermute x3, starting transfers between devices, body(): got = lax.ppermute(running, 'seq', [(i, i + 1)])  6.29 us
    pallas_call x2, Pallas kernels, local(): pl.pallas_call(functools.partial(local_kernel, start_head=start_head, wid...  4.83 us
    pallas_call x1, Pallas kernels, body(): pl.pallas_call(functools.partial(first_final_kernel, heads=heads, width=w...  3.45 us
    pallas_call x1, Pallas kernels, body(): pl.pallas_call(functools.partial(prepare_kernel, heads=heads, width=width...  2.08 us
    ppermute x3, waiting for transfers between devices, body(): got = lax.ppermute(running, 'seq', [(i, i + 1)])  1.97 us
    pallas_call x1, Pallas kernels, body(): pl.pallas_call(last_final_kernel, out_shape=jax.ShapeDtypeStruct((tokens,...  1.46 us
    pallas_call x1, Pallas kernels, serve(): pl.pallas_call(functools.partial(serve_kernel, behind=half), out_shape=ja...  0.75 us
  transfers between devices with their start and end apart: 7, of which 1 were waited for; matrix products, arithmetic and copies ran while one was open for 0% of the time, Pallas kernels for 30%

profile of v8, /device:TPU:0, one launch (start us, length us, event | category | flops | bytes accessed | tf_op | source)
XLA Modules:
  0.0 30.7 jit_solution(16608593709674025143)
XLA Ops:
  0.0 2.1 %prepare.1 = (bf16[512,256]{1,0:T(8,128)(2,1)S(1)}, bf16[512,256]{1,0:T(8,128)(2,1)S(1)}, bf16[512,256]{1,0:T(8,128)(2,1)S(1)}, bf16[640,128]{1,0:T(8,128)(2,1)S(1)}, f32[3,640,256]{2,1,0:T(8,128)S(1)}) custom-call(bf16[64,1024]{1,0:T(8,128)(2,1)} %bitcast.3, bf16[1024,512]{1,0:T(8,128)(2,1)} %q_ref.5, bf16[1024,512]{1,0:T(8,128)(2,1)} %k_ref.5, ...), custom_call_target="tpu_custom_call" | custom-call | flops 1073741824 | bytes 3145728 | tf_op jit(solution)/shard_map/prepare/pallas_call | solution.py:384
  2.1 5.0 %collective-permute-start = (bf16[640,128]{1,0:T(8,128)(2,1)S(1)}, bf16[640,128]{1,0:T(8,128)(2,1)S(1)}, u32[]{:S(2)}, u32[]{:S(2)}) collective-permute-start(bf16[640,128]{1,0:T(8,128)(2,1)S(1)} %get-tuple-element.29.own_ref), channel_id=1, source_target_pairs={{0,4},{1,5},{2,6},{3,7},{16,20},{17,21},{18,22},{19,23}} | collective-permute-start | bytes 491528 | tf_op jit(solution)/shard_map/ppermute | solution.py:446
  7.1 1.3 %collective-permute-start.2 = (bf16[512,256]{1,0:T(8,128)(2,1)S(1)}, bf16[512,256]{1,0:T(8,128)(2,1)S(1)}, u32[]{:S(2)}, u32[]{:S(2)}) collective-permute-start(bf16[512,256]{1,0:T(8,128)(2,1)S(1)} %get-tuple-element.32), channel_id=1, source_target_pairs={{0,4},{4,8},{8,12},{1,5},{5,9},{9,13},{2,6},{6,10},{10,14},{3,7},{... | collective-permute-start | bytes 786440 | tf_op jit(solution)/shard_map/ppermute | solution.py:367
  8.4 1.3 %collective-permute-start.3 = (bf16[512,256]{1,0:T(8,128)(2,1)S(1)}, bf16[512,256]{1,0:T(8,128)(2,1)S(1)}, u32[]{:S(2)}, u32[]{:S(2)}) collective-permute-start(bf16[512,256]{1,0:T(8,128)(2,1)S(1)} %get-tuple-element.33), channel_id=1, source_target_pairs={{4,0},{8,4},{12,8},{5,1},{9,5},{13,9},{6,2},{10,6},{14,10},{7,3},{... | collective-permute-start | bytes 786440 | tf_op jit(solution)/shard_map/ppermute | solution.py:367
  9.7 2.0 %collective-permute-done.got_ref.refs_10_ = bf16[640,128]{1,0:T(8,128)(2,1)S(1)} collective-permute-done((bf16[640,128]{1,0:T(8,128)(2,1)S(1)}, bf16[640,128]{1,0:T(8,128)(2,1)S(1)}, u32[]{:S(2)}, u32[]{:S(2)}) %collective-permute-start) | collective-permute-done | bytes 163872 | tf_op jit(solution)/shard_map/ppermute | solution.py:446
  11.7 0.7 %collective-permute-start.1 = (bf16[640,128]{1,0:T(8,128)(2,1)S(1)}, bf16[640,128]{1,0:T(8,128)(2,1)S(1)}, u32[]{:S(2)}, u32[]{:S(2)}) collective-permute-start(bf16[640,128]{1,0:T(8,128)(2,1)S(1)} %get-tuple-element.31), channel_id=1, source_target_pairs={{4,8},{5,9},{6,10},{7,11},{20,24},{21,25},{22,26},{23,27}} | collective-permute-start | bytes 491528 | tf_op jit(solution)/shard_map/ppermute | solution.py:446
  12.4 5.0 %collective-permute-start.5 = (bf16[512,256]{1,0:T(8,128)(2,1)S(1)}, bf16[512,256]{1,0:T(8,128)(2,1)S(1)}, u32[]{:S(2)}, u32[]{:S(2)}) collective-permute-start(bf16[512,256]{1,0:T(8,128)(2,1)S(1)} %get-tuple-element.36), channel_id=1, source_target_pairs={{0,4},{4,8},{8,12},{1,5},{5,9},{9,13},{2,6},{6,10},{10,14},{3,7},{... | collective-permute-start | bytes 786440 | tf_op jit(solution)/shard_map/ppermute | solution.py:367
  17.4 0.0 copy-done
  17.4 0.0 copy-done.1
  17.4 0.0 copy-done.2
  17.4 2.4 %local.2 = (f32[1024,256]{1,0:T(8,128)S(1)}, f32[1024,256]{1,0:T(8,128)S(1)}, f32[1024,256]{1,0:T(8,128)S(1)}, f32[1024,256]{1,0:T(8,128)S(1)}, f32[512,256]{1,0...) custom-call(bf16[1024,512]{1,0:T(8,128)(2,1)S(1)} %copy-done, bf16[1024,512]{1,0:T(8,128)(2,1)S(1)} %copy-done.1, ...), custom_call_target="tpu_custom_call" | custom-call | flops 4194304000 | bytes 1048576 | tf_op jit(solution)/shard_map/local/pallas_call | solution.py:408
  19.9 0.0 collective-permute-done.2._.kp_ref
  19.9 0.0 collective-permute-done.3.qb_ref
  19.9 0.7 %serve.1._ = bf16[528,256]{1,0:T(8,128)(2,1)S(1)} custom-call(bf16[512,256]{1,0:T(8,128)(2,1)S(1)} %collective-permute-done.2._.kp_ref, bf16[512,256]{1,0:T(8,128)(2,1)S(1)} %collective-permute-done.3.qb_ref, bf16[1024,512]{1,0:T(8,128)(2,1)S(1)} %copy-done.1, bf16[1024,512]{1,0:T(8,128)(2,1)S(1)} %copy-done.2, f32[512,256]{1,0:T(8,128)S(1)} %get-tuple-element.34.__.top_ref), custom_call_target="tpu_custom_call" | custom-call | flops 314572800 | bytes 1048576 | tf_op jit(solution)/shard_map/serve/pallas_call | solution.py:421
  20.6 0.0 collective-permute-done.1.got_ref.refs_11_
  20.6 0.1 relay.3
  20.7 0.7 %collective-permute-start.6 = (bf16[640,128]{1,0:T(8,128)(2,1)S(1)}, bf16[640,128]{1,0:T(8,128)(2,1)S(1)}, u32[]{:S(2)}, u32[]{:S(2)}) collective-permute-start(bf16[640,128]{1,0:T(8,128)(2,1)S(1)} %get-tuple-element.47), channel_id=1, source_target_pairs={{8,12},{9,13},{10,14},{11,15},{24,28},{25,29},{26,30},{27,31}} | collective-permute-start | bytes 491528 | tf_op jit(solution)/shard_map/ppermute | solution.py:446
  21.4 1.9 %collective-permute-start.4 = (bf16[528,256]{1,0:T(8,128)(2,1)S(1)}, bf16[528,256]{1,0:T(8,128)(2,1)S(1)}, u32[]{:S(2)}, u32[]{:S(2)}) collective-permute-start(bf16[528,256]{1,0:T(8,128)(2,1)S(1)} %get-tuple-element.35), channel_id=1, source_target_pairs={{0,4},{4,8},{8,12},{1,5},{5,9},{9,13},{2,6},{6,10},{10,14},{3,7},{... | collective-permute-start | bytes 811016 | tf_op jit(solution)/shard_map/ppermute | solution.py:367
  23.3 2.4 %local.3 = (f32[1024,256]{1,0:T(8,128)S(1)}, f32[1024,256]{1,0:T(8,128)S(1)}, f32[1024,256]{1,0:T(8,128)S(1)}, f32[1024,256]{1,0:T(8,128)S(1)}, f32[512,256]{1,0...) custom-call(bf16[1024,512]{1,0:T(8,128)(2,1)S(1)} %copy-done, bf16[1024,512]{1,0:T(8,128)(2,1)S(1)} %copy-done.1, ...), custom_call_target="tpu_custom_call" | custom-call | flops 1048576000 | bytes 1048576 | tf_op jit(solution)/shard_map/local/pallas_call | solution.py:408
  25.7 0.0 collective-permute-done.5.vp_ref
  25.7 0.0 collective-permute-done.6.refs_12_
  25.7 3.5 %final.1 = (bf16[1024,512]{1,0:T(8,128)(2,1)}, f32[512,256]{1,0:T(8,128)S(1)}, f32[1,256]{1,0:T(1,128)S(1)}) custom-call(bf16[1024,512]{1,0:T(8,128)(2,1)S(1)} %copy-done, bf16[512,256]{1,0:T(8,128)(2,1)S(1)} %collective-permute-done.2._.kp_ref, bf16[512,256]{1,0:T(8,128)(2,1)S(1)} %collective-permute-done.5.vp_ref, ...), custom_call_target="tpu_custom_call" | custom-call | flops 2097152000 | bytes 12582912 | tf_op jit(solution)/shard_map/final/pallas_call | solution.py:476
  29.2 0.0 collective-permute-done.4.ob_ref
  29.2 1.5 %last.1 = bf16[1024,512]{1,0:T(8,128)(2,1)} custom-call(bf16[528,256]{1,0:T(8,128)(2,1)S(1)} %collective-permute-done.4.ob_ref, f32[512,256]{1,0:T(8,128)S(1)} %get-tuple-element.49.lin_ref, f32[1024,256]{1,0:T(8,128)S(1)} %get-tuple-element.44.refs_7_.win_ref, f32[1024,256]{1,0:T(8,128)S(1)} %get-tuple-element.45.refs_8_.sum_ref, ...), custom_call_target="tpu_custom_call", output_to_operand_aliasing={{}: (6, {})} | custom-call | flops 1048576 | bytes 3145728 | tf_op jit(solution)/shard_map/last/pallas_call | solution.py:496
  (8 shorter events, 0.1 us)
Async XLA Ops:
  0.0 17.4 %copy-start = (bf16[1024,512]{1,0:T(8,128)(2,1)S(1)}, bf16[1024,512]{1,0:T(8,128)(2,1)}, u32[]{:S(2)}) copy-start(bf16[1024,512]{1,0:T(8,128)(2,1)} %q_ref.5) | copy-start | bytes 3145732
  0.0 17.4 %copy-start.1 = (bf16[1024,512]{1,0:T(8,128)(2,1)S(1)}, bf16[1024,512]{1,0:T(8,128)(2,1)}, u32[]{:S(2)}) copy-start(bf16[1024,512]{1,0:T(8,128)(2,1)} %k_ref.5) | copy-start | bytes 3145732
  0.0 17.4 %copy-start.2 = (bf16[1024,512]{1,0:T(8,128)(2,1)S(1)}, bf16[1024,512]{1,0:T(8,128)(2,1)}, u32[]{:S(2)}) copy-start(bf16[1024,512]{1,0:T(8,128)(2,1)} %v_ref.5) | copy-start | bytes 3145732
  0.0 17.4 %copy-start.3 = (bf16[1024,64]{0,1:T(8,128)(2,1)S(1)}, bf16[1024,64]{0,1:T(8,128)(2,1)}, u32[]{:S(2)}) copy-start(bf16[1024,64]{0,1:T(8,128)(2,1)} %param.7) | copy-start | bytes 393220
  0.0 17.4 %copy-start.4 = (bf16[1024,64]{0,1:T(8,128)(2,1)S(1)}, bf16[1024,64]{0,1:T(8,128)(2,1)}, u32[]{:S(2)}) copy-start(bf16[1024,64]{0,1:T(8,128)(2,1)} %param.6) | copy-start | bytes 393220
  2.1 9.5 %collective-permute-start = (bf16[640,128]{1,0:T(8,128)(2,1)S(1)}, bf16[640,128]{1,0:T(8,128)(2,1)S(1)}, u32[]{:S(2)}, u32[]{:S(2)}) collective-permute-start(bf16[640,128]{1,0:T(8,128)(2,1)S(1)} %get-tuple-element.29.own_ref), channel_id=1, source_target_pairs={{0,4},{1,5},{2,6},{3,7},{16,20},{17,21},{18,22},{19,23}} | collective-permute-start | bytes 491528 | tf_op jit(solution)/shard_map/ppermute | solution.py:446
  7.1 12.8 %collective-permute-start.2 = (bf16[512,256]{1,0:T(8,128)(2,1)S(1)}, bf16[512,256]{1,0:T(8,128)(2,1)S(1)}, u32[]{:S(2)}, u32[]{:S(2)}) collective-permute-start(bf16[512,256]{1,0:T(8,128)(2,1)S(1)} %get-tuple-element.32), channel_id=1, source_target_pairs={{0,4},{4,8},{8,12},{1,5},{5,9},{9,13},{2,6},{6,10},{10,14},{3,7},{... | collective-permute-start | bytes 786440 | tf_op jit(solution)/shard_map/ppermute | solution.py:367
  8.4 11.5 %collective-permute-start.3 = (bf16[512,256]{1,0:T(8,128)(2,1)S(1)}, bf16[512,256]{1,0:T(8,128)(2,1)S(1)}, u32[]{:S(2)}, u32[]{:S(2)}) collective-permute-start(bf16[512,256]{1,0:T(8,128)(2,1)S(1)} %get-tuple-element.33), channel_id=1, source_target_pairs={{4,0},{8,4},{12,8},{5,1},{9,5},{13,9},{6,2},{10,6},{14,10},{7,3},{... | collective-permute-start | bytes 786440 | tf_op jit(solution)/shard_map/ppermute | solution.py:367
  11.7 9.0 %collective-permute-start.1 = (bf16[640,128]{1,0:T(8,128)(2,1)S(1)}, bf16[640,128]{1,0:T(8,128)(2,1)S(1)}, u32[]{:S(2)}, u32[]{:S(2)}) collective-permute-start(bf16[640,128]{1,0:T(8,128)(2,1)S(1)} %get-tuple-element.31), channel_id=1, source_target_pairs={{4,8},{5,9},{6,10},{7,11},{20,24},{21,25},{22,26},{23,27}} | collective-permute-start | bytes 491528 | tf_op jit(solution)/shard_map/ppermute | solution.py:446
  12.4 13.4 %collective-permute-start.5 = (bf16[512,256]{1,0:T(8,128)(2,1)S(1)}, bf16[512,256]{1,0:T(8,128)(2,1)S(1)}, u32[]{:S(2)}, u32[]{:S(2)}) collective-permute-start(bf16[512,256]{1,0:T(8,128)(2,1)S(1)} %get-tuple-element.36), channel_id=1, source_target_pairs={{0,4},{4,8},{8,12},{1,5},{5,9},{9,13},{2,6},{6,10},{10,14},{3,7},{... | collective-permute-start | bytes 786440 | tf_op jit(solution)/shard_map/ppermute | solution.py:367
  20.7 5.0 %collective-permute-start.6 = (bf16[640,128]{1,0:T(8,128)(2,1)S(1)}, bf16[640,128]{1,0:T(8,128)(2,1)S(1)}, u32[]{:S(2)}, u32[]{:S(2)}) collective-permute-start(bf16[640,128]{1,0:T(8,128)(2,1)S(1)} %get-tuple-element.47), channel_id=1, source_target_pairs={{8,12},{9,13},{10,14},{11,15},{24,28},{25,29},{26,30},{27,31}} | collective-permute-start | bytes 491528 | tf_op jit(solution)/shard_map/ppermute | solution.py:446
  21.4 7.8 %collective-permute-start.4 = (bf16[528,256]{1,0:T(8,128)(2,1)S(1)}, bf16[528,256]{1,0:T(8,128)(2,1)S(1)}, u32[]{:S(2)}, u32[]{:S(2)}) collective-permute-start(bf16[528,256]{1,0:T(8,128)(2,1)S(1)} %get-tuple-element.35), channel_id=1, source_target_pairs={{0,4},{4,8},{8,12},{1,5},{5,9},{9,13},{2,6},{6,10},{10,14},{3,7},{... | collective-permute-start | bytes 811016 | tf_op jit(solution)/shard_map/ppermute | solution.py:367
